TPU v7x, 32 devices: a whole 2x2x4 slice. The times are simulated.
32 devices in a mesh: row: 4 (over y, x), col: 8 (over z, core).
Axes of the slice: x: 2, y: 2, z: 4, core: 2. Of those that a mesh axis runs over, the one named last changes fastest.
Arguments:
- cov: float32 [18432, 18432], P('row', 'col'), may hold values from -1 to 70, as said below
- weights: float32 [18432], P(('row', 'col')), may hold values from -0.6 to 0.6
- act: bfloat16 [8, 512, 144], P('row', 'col'), may hold values from -6 to 6
- upstream: bfloat16 [8, 512, 128], P('row', 'col'), may hold values from -6 to 6
- neighbors: int32 [8, 512, 138], P('row', 'col'), may hold values from 0 to 511
- types: int32 [8, 512], P('row', 'col'), may hold values from 0 to 1
- type_gain: float32 [2, 128], replicated, may hold values from 0.25 to 1.75
- sens: float32 [64, 512], P('row', 'col'), may hold values from -0.0009765625 to 0.0009765625
- frame_for_measure: int32 [64], P('row'), may hold values from 0 to 1
- noise_variance: float32 [64], replicated, may hold values from 0.5 to 2
- innovation: float32 [64], replicated, may hold values from -6 to 6
Outputs:
- weights_new: float32 [18432], P(('row', 'col'))
- cov_new: float32 [18432, 18432], P('row', 'col')
Inputs may be any that keep to these rules, and one draw needn't show every extreme that they name: cov is symmetric and positive definite.
All inputs are finite; a program needn't handle non-finite values. Where the computation divides by a largest or mean magnitude, that divisor is 1e-20 or more.
Results may differ from a plain program's by a relative error of at most 0.0023.
Values may be sent and summed in bfloat16 or wider, within the bound.
No kernel may reach another device: no remote copies, remote signals or barrier semaphores. Data moves between devices by JAX's collectives and lax.ppermute only.
A program may use at most 128 MiB of HBM per device.

v0:
```python
import functools
import math

import jax
import jax.numpy as jnp
from jax import lax
from jax.experimental import pallas as pl
from jax.experimental.pallas import tpu as pltpu
from jax.sharding import PartitionSpec as P


NS_ITERS = 5
FULL = lax.Precision.HIGHEST
F32 = jnp.float32
BF16 = jnp.bfloat16
EACH = (3, 2, 1)
EARLY, LATER = 2, 2

VMEM = pl.BlockSpec(memory_space=pltpu.VMEM)
SMEM = pl.BlockSpec(memory_space=pltpu.SMEM)


ANY = pl.BlockSpec(memory_space=pl.ANY)


def swap(block, axis, step):
    n = lax.axis_size(axis)
    return lax.ppermute(block, axis, [(i, i ^ step) for i in range(n)])


def gather_apart(block):
    return [block] + [swap(block, "col", k) for k in range(2, lax.axis_size("col"), 2)]


def exchange(blocks):
    return [blocks[0]] + [swap(block, "row", k) for k, block in enumerate(blocks) if k]


def gather(block):
    pieces = []
    for piece in gather_apart(block):
        pieces += [piece, swap(piece, "col", 1)]
    return pieces


def params(mib):
    return pltpu.CompilerParams(vmem_limit_bytes=mib * 2**20)


def shape(dims, kind=F32):
    return jax.ShapeDtypeStruct(dims, kind)


def resident(dims, kind=F32):
    return pltpu.VMEM(dims, kind)


def outside(block):
    return pltpu.with_memory_space_constraint(block, pltpu.HBM)


def keep(block):
    return pltpu.with_memory_space_constraint(block, pltpu.VMEM)


def estimate(flops, moved):
    return pl.CostEstimate(flops=flops, bytes_accessed=moved, transcendentals=0)


def loads(source, first, targets, sems):
    copies = []
    for i, target in enumerate(targets):
        rows = target.shape[0]
        copies.append(
            pltpu.make_async_copy(source.at[pl.ds(first, rows), :], target, sems.at[i])
        )
        first += rows
    return copies


def pack_kernel(
    up_ref, act_ref, neighbors_ref, types_ref, gain_ref, sens_ref, frame_ref,
    packed_ref, near_ref, kinds_ref, scale_ref, masked_ref,
    up, act, sens, frame_of, sems,
):
    copies = [
        pltpu.make_async_copy(source, target, sems.at[i])
        for i, (source, target) in enumerate(
            (
                (up_ref, up),
                (act_ref, act),
                (neighbors_ref, near_ref),
                (types_ref, kinds_ref),
                (gain_ref, scale_ref),
                (sens_ref, sens),
                (frame_ref, frame_of),
            )
        )
    ]
    for copy in copies:
        copy.start()
    for copy in copies:
        copy.wait()
    width_out, width_in = up.shape[2], act.shape[2]
    packed_ref[:, :, pl.ds(0, width_out)] = up[...]
    packed_ref[:, :, pl.ds(width_out, width_in)] = act[...]
    measures, _ = sens.shape
    frames = up.shape[0]
    index = lax.broadcasted_iota(jnp.int32, sens.shape, 0)
    frame = jnp.zeros(sens.shape, jnp.int32)
    for m in range(measures):
        frame = jnp.where(index == m, frame_of[m], frame)
    masked_ref[...] = jnp.concatenate(
        [jnp.where(frame == f, sens[...], 0.0) for f in range(frames)], axis=1
    )


def counts_kernel(first, near_ref, cov_ref, counts_ref, *refs):
    kept, (flipped, sems) = refs[:-2], refs[-2:]
    copies = loads(cov_ref, first, kept, sems)
    for copy in copies:
        copy.start()
    frames, atoms, slots = near_ref.shape
    lanes = frames * atoms
    whole, _ = counts_ref.shape
    flipped[...] = near_ref[...].reshape(lanes, slots).T
    chunk = min(256, whole)
    unroll = next(u for u in (6, 4, 3, 2, 1) if slots % u == 0)
    for base in range(0, whole, chunk):
        atom = lax.broadcasted_iota(jnp.int32, (chunk, lanes), 0) + base

        def step(s, total):
            for u in range(unroll):
                row = flipped[pl.ds(s * unroll + u, 1), :]
                total = jnp.where(atom == row, total + 1.0, total)
            return total

        total = lax.fori_loop(0, slots // unroll, step, jnp.zeros((chunk, lanes), F32))
        counts_ref[pl.ds(base, chunk), :] = total.astype(BF16)
    for copy in copies:
        copy.wait()


def adjoint_kernel(slots, width, *refs):
    counts_ref, kinds_ref, scale_ref, masked_ref = refs[:4]
    pieces, (out_ref, lookup) = refs[4:-2], refs[-2:]
    frames, atoms, _ = pieces[0].shape
    lanes = frames * atoms
    me = lax.axis_index("col")
    for k, piece in enumerate(pieces):
        start = pl.multiple_of((me ^ k) * atoms, atoms)
        for f in range(frames):
            lookup[f, pl.ds(start, atoms), :] = piece[f, :, pl.ds(0, width)]
    lane = lax.broadcasted_iota(jnp.int32, (1, lanes), 1)
    total = jnp.zeros((width, lanes), F32)
    for f in range(frames):
        part = lax.dot_general(
            lookup[f], counts_ref[...], (((0,), (0,)), ((), ())), preferred_element_type=F32
        )
        total = jnp.where((lane // atoms) == f, part, total)
    own = pieces[0][:, :, pl.ds(0, width)].reshape(lanes, width).astype(F32).T
    total = own + total * (1.0 / math.sqrt(slots))
    kinds = jnp.concatenate([kinds_ref[f : f + 1, :] for f in range(frames)], axis=1)
    gain = scale_ref[...].T
    scale = jnp.zeros((width, lanes), F32)
    for t in range(scale_ref.shape[0]):
        scale = jnp.where(kinds == t, gain[:, t : t + 1], scale)
    out_ref[pl.ds(0, width), :] = scale * total
    out_ref[pl.ds(width, masked_ref.shape[0]), :] = masked_ref[...]


def jacobian_kernel(count, peers, width_in, skip, span, first_row, *refs):
    sides, packs, cov_ref = refs[:count], refs[count : 2 * count], refs[2 * count]
    outs, kept = refs[2 * count + 1 : 2 * count + 1 + peers], refs[2 * count + 1 + peers : -4]
    inputs, mixed, flat, sems = refs[-4:]
    copies = loads(cov_ref, first_row, kept, sems)
    for copy in copies:
        copy.start()
    row, col = lax.axis_index("row"), lax.axis_index("col")
    frames, atoms, _ = packs[0].shape
    lanes = frames * atoms
    measures = outs[0].shape[0]
    width_out = sides[0].shape[0] - measures
    for k, pack in enumerate(packs):
        inputs[pl.ds(k * lanes, lanes), :] = pack[:, :, pl.ds(width_out, width_in)].reshape(
            lanes, width_in
        )

    def block(targets, base, held, first):
        size = min(8, held)

        def group(g, carry):
            start = first + g * size
            for k, side in enumerate(sides):
                sens = side[pl.ds(width_out, measures), :]
                for b in range(size):
                    line = side[pl.ds(start + b, 1), :]
                    mixed[pl.ds(b * measures, measures), pl.ds(k * lanes, lanes)] = (
                        sens * line
                    ).astype(BF16)
            found = jnp.dot(
                mixed[pl.ds(0, size * measures), :], inputs[...], preferred_element_type=F32
            )
            for b in range(size):
                flat[:, pl.ds(b * width_in, width_in)] = found[
                    b * measures : (b + 1) * measures, :
                ]
            reach = size * width_in
            at = base + g * reach
            if reach % 128 == 0:
                at = pl.multiple_of(at, 128)
            for target in targets:
                target[:, pl.ds(at, reach)] = flat[:, pl.ds(0, reach)].astype(BF16)
            return carry

        if held == size:
            group(0, 0)
        else:
            lax.fori_loop(0, held // size, group, 0)

    per_row = width_out // peers
    for k in range(peers):
        block([outs[k]], 0, span // width_in, (row ^ k) * per_row + skip // width_in)
    side_span = (outs[0].shape[1] - span) // width_in
    if side_span:
        block(outs, span, side_span, col * side_span)
    for copy in copies:
        copy.wait()


def multiply(whole_ref, jac, base, depth, part, tiles):
    def tile(i, carry):
        at = i * depth
        if not isinstance(i, int):
            at = pl.multiple_of(at, depth)
        left = jac[:, pl.ds(base + at, depth)]
        block = part[pl.ds(at, depth), :]
        high = block.astype(BF16)
        low = (block - high.astype(F32)).astype(BF16)
        whole_ref[...] += jnp.dot(left, high, preferred_element_type=F32) + jnp.dot(
            left, low, preferred_element_type=F32
        )
        return carry

    if tiles == 1:
        tile(0, 0)
    else:
        lax.fori_loop(0, tiles, tile, 0)


def arrange(target, sources, start, span):
    me = lax.axis_index("row")
    for k, source in enumerate(sources):
        measures = source.shape[0]
        at = pl.multiple_of((me ^ k) * measures, measures)
        target[pl.ds(at, measures), :] = source[:, pl.ds(start, span)].astype(target.dtype)


def product_first_kernel(peers, depth, *refs):
    jac_refs, kept, (whole_ref, jac) = refs[:peers], refs[peers:-2], refs[-2:]
    arrange(jac, jac_refs, 0, jac.shape[1])
    whole_ref[...] = jnp.zeros_like(whole_ref)
    base = 0
    for part in kept:
        multiply(whole_ref, jac, base, depth, part, part.shape[0] // depth)
        base += part.shape[0]


def product_last_kernel(peers, depth, count, *refs):
    jac_refs, begun_ref, kept = refs[:peers], refs[peers], refs[peers + 1 : peers + 1 + count]
    cov_ref = refs[peers + 1 + count]
    outs, (jac, side, whole, tiles, sems) = refs[peers + 2 + count : -5], refs[-5:]
    slots = tiles.shape[0]
    span = jac.shape[1]
    held = sum(part.shape[0] for part in kept)
    start = cov_ref.shape[0] - span + held
    copies = [
        pltpu.make_async_copy(
            cov_ref.at[pl.ds(start + i * depth, depth), :], tiles.at[i % slots], sems.at[i % slots]
        )
        for i in range((span - held) // depth)
    ]
    for copy in copies[:slots]:
        copy.start()
    arrange(jac, jac_refs, 0, span)
    arrange(side, jac_refs, span, side.shape[1])
    whole[...] = begun_ref[...]
    base = 0
    for part in kept:
        multiply(whole, jac, base, depth, part, part.shape[0] // depth)
        base += part.shape[0]
    for i, copy in enumerate(copies):
        copy.wait()
        multiply(whole, jac, base + i * depth, depth, tiles.at[i % slots], 1)
        if i + slots < len(copies):
            copies[i + slots].start()
    inner = lax.dot_general(
        whole[...], side[...], (((1,), (1,)), ((), ())), precision=FULL, preferred_element_type=F32
    )
    me = lax.axis_index("row")
    overall, width = whole.shape
    measures = overall // peers
    for k in range(peers):
        at = pl.multiple_of((me ^ k) * measures, measures)
        outs[k][:, pl.ds(0, width)] = whole[pl.ds(at, measures), :]
        outs[k][:, pl.ds(width, overall * peers)] = jnp.concatenate(
            [inner[q * measures : (q + 1) * measures, :] for q in range(peers)], axis=1
        )


def sum_kernel(*refs):
    parts, (exact_ref, sent_ref) = refs[:-2], refs[-2:]
    width = exact_ref.shape[1]
    total = parts[0][...]
    for part in parts[1:]:
        total = total + part[...]
    exact_ref[...] = total[:, :width]
    sent_ref[:, pl.ds(0, width)] = total[:, :width].astype(BF16)
    inner = total[:, width:]
    high = inner.astype(BF16)
    sent_ref[:, pl.ds(width, inner.shape[1])] = high
    sent_ref[:, pl.ds(width + inner.shape[1], inner.shape[1])] = (
        inner - high.astype(F32)
    ).astype(BF16)


def route_kernel(peers, width, *refs):
    pieces, outs, inner_ref, held = refs[: -peers - 2], refs[-peers - 2 : -2], refs[-2], refs[-1]
    row, col = lax.axis_index("row"), lax.axis_index("col")
    count = len(pieces)
    per_block = count // peers
    measures = pieces[0].shape[0]
    overall = inner_ref.shape[0]
    total = jnp.zeros((measures, overall * peers), F32)
    for k, piece in enumerate(pieces):
        held[(col // 2) ^ k] = piece[:, pl.ds(0, width)]
        total = total + piece[:, pl.ds(width, overall * peers)].astype(F32)
        total = total + piece[:, pl.ds(width + overall * peers, overall * peers)].astype(F32)
    for q in range(peers):
        inner_ref[pl.ds(q * measures, measures), :] = total[:, q * overall : (q + 1) * overall]
    for k in range(peers):
        for p in range(per_block):
            outs[k][:, pl.ds(p * width, width)] = held[(row ^ k) * per_block + p]
        outs[k][:, pl.ds(per_block * width, width)] = pieces[0][:, pl.ds(0, width)]


def inverse_kernel(peers, *refs):
    inner_refs = refs[:2]
    exact_ref, noise_ref, innovation_ref, inverse_ref, change_ref, weight = refs[2:]
    row = lax.axis_index("row")
    overall = inverse_ref.shape[0]
    measures, width = exact_ref.shape
    inner = inner_refs[0][...] + inner_refs[1][...]
    down = lax.broadcasted_iota(jnp.int32, (overall, overall), 0)
    across = lax.broadcasted_iota(jnp.int32, (overall, overall), 1)
    diagonal = down == across
    inner = inner + jnp.where(diagonal, noise_ref[...], 0.0)
    scale = 1.0 / jnp.max(jnp.sum(jnp.abs(inner), axis=1, keepdims=True), axis=0, keepdims=True)
    inverse = jnp.where(diagonal, scale, 0.0)
    for _ in range(NS_ITERS):
        left = jnp.dot(inverse, inner, precision=FULL, preferred_element_type=F32)
        inverse = 2.0 * inverse - jnp.dot(left, inverse, precision=FULL, preferred_element_type=F32)
    inverse_ref[...] = inverse
    weight[...] = jnp.sum(inverse * innovation_ref[...], axis=1, keepdims=True)
    mine = weight[pl.ds(pl.multiple_of(row * measures, measures), measures), :]
    change = jnp.sum(exact_ref[...] * mine, axis=0, keepdims=True)
    part = width // peers
    for q in range(peers):
        change_ref[row ^ q] = change[:, q * part : (q + 1) * part]


def merge_kernel(*refs):
    pieces, half_ref, right_ref = refs[:-2], refs[-2], refs[-1]
    me = lax.axis_index("row")
    measures = pieces[0].shape[0]
    span, width = half_ref.shape[1], right_ref.shape[1]
    for k, piece in enumerate(pieces):
        at = pl.multiple_of((me ^ k) * measures, measures)
        half_ref[pl.ds(at, measures), :] = piece[:, pl.ds(0, span)]
        right_ref[pl.ds(at, measures), :] = piece[:, pl.ds(span, width)]


def update_kernel(mine_ref, other_ref, right_ref, inverse_ref, *refs):
    kept, (cov_ref, out_ref, left, staged) = refs[:-4], refs[-4:]
    step = pl.program_id(0)
    depth, width = out_ref.shape
    height = left.shape[1]

    @pl.when(step == 0)
    def _():
        core = lax.axis_index("col") % 2
        for p in range(height // (2 * width)):
            part = pl.ds(p * width, width)
            here = mine_ref[:, part].astype(F32)
            there = other_ref[:, part].astype(F32)
            staged[:, pl.ds(2 * p * width, width)] = jnp.where(core == 0, here, there)
            staged[:, pl.ds((2 * p + 1) * width, width)] = jnp.where(core == 0, there, here)
        left[...] = lax.dot_general(
            inverse_ref[...],
            staged[...],
            (((0,), (0,)), ((), ())),
            precision=FULL,
            preferred_element_type=F32,
        ).astype(BF16)

    gain = left[:, pl.ds(pl.multiple_of(step * depth, depth), depth)]
    change = lax.dot_general(
        gain, right_ref[...], (((0,), (0,)), ((), ())), preferred_element_type=F32
    )
    first = 0
    for part in kept:
        held = part.shape[0] // depth

        @pl.when((step >= first) & (step < first + held))
        def _(part=part, first=first):
            at = pl.multiple_of((step - first) * depth, depth)
            out_ref[...] = part[pl.ds(at, depth), :] - change

        first += held

    @pl.when(step >= first)
    def _():
        out_ref[...] = cov_ref[...] - change


def on_device(
    cov,
    weights,
    act,
    upstream,
    neighbors,
    types,
    type_gain,
    sens,
    frame_for_measure,
    noise_variance,
    innovation,
):
    rows, cols = lax.axis_size("row"), lax.axis_size("col")
    frames, atoms, width_in = act.shape
    width_out = upstream.shape[2]
    slots = neighbors.shape[2]
    lanes = frames * atoms
    measures = sens.shape[0]
    overall = measures * rows
    height, width = cov.shape
    part = weights.shape[0]
    dma = pltpu.SemaphoreType.DMA
    depth = next(d for d in (256, 128) if height % d == 0)
    tiles = height // depth
    each = next(n for n in EACH if tiles % n == 0)
    segments = tiles // each
    held = resident((each * depth, width))
    early, later = segments * EARLY // 6, segments * LATER // 6
    packed_width = width_out + -(-width_in // 128) * 128

    packed, near, kinds, scale, masked = pl.pallas_call(
        pack_kernel,
        out_shape=[
            shape((frames, atoms, packed_width), BF16),
            shape(neighbors.shape, jnp.int32),
            shape(types.shape, jnp.int32),
            shape(type_gain.shape),
            shape((measures, lanes)),
        ],
        in_specs=[ANY] * 7,
        out_specs=[VMEM] * 5,
        scratch_shapes=[
            pltpu.VMEM(upstream.shape, BF16),
            pltpu.VMEM(act.shape, BF16),
            pltpu.VMEM(sens.shape, F32),
            pltpu.SMEM(frame_for_measure.shape, jnp.int32),
            dma((7,)),
        ],
        compiler_params=params(3),
        name="pack",
    )(*map(outside, (upstream, act, neighbors, types, type_gain, sens, frame_for_measure)))
    packs = gather(packed)
    counts, *kept = pl.pallas_call(
        functools.partial(counts_kernel, 0),
        out_shape=[shape((atoms * cols, lanes), BF16)] + [held] * early,
        in_specs=[VMEM, ANY],
        out_specs=[VMEM] * (1 + early),
        scratch_shapes=[pltpu.VMEM((slots, lanes), jnp.int32), dma((early,))],
        compiler_params=params(3),
        cost_estimate=estimate(3 * 10**9, 4 * early * each * depth * width),
        name="counts",
    )(near, outside(cov))
    side = pl.pallas_call(
        functools.partial(adjoint_kernel, slots, width_out),
        out_shape=shape((width_out + measures, lanes)),
        in_specs=[VMEM] * (4 + cols),
        out_specs=VMEM,
        scratch_shapes=[pltpu.VMEM((frames, atoms * cols, width_out), BF16)],
        compiler_params=params(3),
        name="adjoint",
    )(counts, kinds, scale, masked, *packs)
    sides = gather(side)
    part_a = tiles // 2 // each * each * depth
    part_b = height - part_a
    kept = list(kept)
    jacs = []
    for skip, size, extra, loaded in (
        (0, part_a, 0, later // 2),
        (part_a, part_b, width, later - later // 2),
    ):
        found = pl.pallas_call(
            functools.partial(
                jacobian_kernel, cols, rows, width_in, skip, size, len(kept) * each * depth
            ),
            out_shape=[shape((measures, size + extra), BF16)] * rows + [held] * loaded,
            in_specs=[VMEM] * (2 * cols) + [ANY],
            out_specs=[VMEM] * (rows + loaded),
            scratch_shapes=[
                pltpu.VMEM((cols * lanes, width_in), BF16),
                pltpu.VMEM((8 * measures, cols * lanes), BF16),
                pltpu.VMEM((measures, 8 * width_in), F32),
                dma((max(1, loaded),)),
            ],
            compiler_params=params(5),
            cost_estimate=estimate(3 * 10**9, 4 * loaded * each * depth * width),
            name="jacobian_last" if skip else "jacobian_first",
        )(*sides, *packs, outside(cov))
        kept += found[rows:]
        jacs.append(exchange(found[:rows]))
    first = part_a // (each * depth)
    begun = pl.pallas_call(
        functools.partial(product_first_kernel, rows, depth),
        out_shape=shape((overall, width)),
        in_specs=[VMEM] * (rows + first),
        out_specs=VMEM,
        scratch_shapes=[pltpu.VMEM((overall, part_a), BF16)],
        compiler_params=params(9),
        cost_estimate=estimate(8 * overall * part_a * width, 4 * part_a * width),
        name="product_first",
    )(*jacs[0], *map(keep, kept[:first]))
    rest = len(kept) - first
    parts = pl.pallas_call(
        functools.partial(product_last_kernel, rows, depth, rest),
        out_shape=[shape((measures, width + overall * rows))] * rows,
        in_specs=[VMEM] * (rows + 1 + rest) + [ANY],
        out_specs=[VMEM] * rows,
        scratch_shapes=[
            pltpu.VMEM((overall, part_b), BF16),
            pltpu.VMEM((overall, width), F32),
            pltpu.VMEM((overall, width), F32),
            pltpu.VMEM((2, depth, width), F32),
            dma((2,)),
        ],
        compiler_params=params(14),
        cost_estimate=estimate(8 * overall * part_b * width, 4 * part_b * width),
        name="product_last",
    )(*jacs[1], begun, *map(keep, kept[first:]), outside(cov))
    parts = exchange(parts)
    exact, sent = pl.pallas_call(
        sum_kernel,
        out_shape=[
            shape((measures, width)),
            shape((measures, width + 2 * overall * rows), BF16),
        ],
        in_specs=[VMEM] * rows,
        out_specs=[VMEM] * 2,
        compiler_params=params(3),
        name="sum",
    )(*parts)
    sents = gather_apart(sent)
    span = height // 2
    *routed, inner = pl.pallas_call(
        functools.partial(route_kernel, rows, width),
        out_shape=[shape((measures, span + width), BF16)] * rows + [shape((overall, overall))],
        in_specs=[VMEM] * (cols // 2),
        out_specs=[VMEM] * (rows + 1),
        scratch_shapes=[pltpu.VMEM((cols // 2, measures, width), BF16)],
        compiler_params=params(3),
        name="route",
    )(*sents)
    routed = exchange(routed)
    shared = swap(inner, "col", 1)
    inverse, change = pl.pallas_call(
        functools.partial(inverse_kernel, rows),
        out_shape=[shape((overall, overall)), shape((rows, 1, part))],
        in_specs=[VMEM] * 5,
        out_specs=[VMEM] * 2,
        scratch_shapes=[pltpu.VMEM((overall, 1), F32)],
        compiler_params=params(3),
        name="inverse",
    )(inner, shared, exact, noise_variance[None, :], innovation[None, :])
    half, right = pl.pallas_call(
        merge_kernel,
        out_shape=[shape((overall, span), BF16), shape((overall, width), BF16)],
        in_specs=[VMEM] * rows,
        out_specs=[VMEM] * 2,
        compiler_params=params(3),
        name="merge",
    )(*routed)
    other = swap(half, "col", 1)
    weights_new = weights
    for k in range(rows):
        pairs = [
            (r * cols + c, c * rows + (r ^ k)) for r in range(rows) for c in range(cols)
        ]
        moved = lax.ppermute(change, ("row", "col"), pairs)
        weights_new = weights_new + moved[k, 0]
    skipped = (early + later) * each
    cov_new = pl.pallas_call(
        update_kernel,
        out_shape=shape((height, width)),
        grid=(tiles,),
        in_specs=[VMEM] * (4 + early + later)
        + [pl.BlockSpec((depth, width), lambda i: (jnp.maximum(i, skipped), 0))],
        out_specs=pl.BlockSpec((depth, width), lambda i: (i, 0)),
        scratch_shapes=[
            pltpu.VMEM((overall, height), BF16),
            pltpu.VMEM((overall, height), F32),
        ],
        compiler_params=params(14),
        cost_estimate=estimate(2 * overall * height * width, 4 * height * width),
        name="update",
    )(half, other, right, inverse, *map(keep, kept), outside(cov))
    return (weights_new, cov_new)


def solution(mesh):
    return jax.shard_map(
        on_device,
        mesh=mesh,
        in_specs=(
            P("row", "col"),
            P(("row", "col")),
            P("row", "col", None),
            P("row", "col", None),
            P("row", "col", None),
            P("row", "col"),
            P(),
            P("row", "col"),
            P("row"),
            P(),
            P(),
        ),
        out_specs=(P(("row", "col")), P("row", "col")),
        check_vma=False,
    )
```

profile of v0, /device:TPU:6, one launch (start us, length us, event | category | flops | bytes accessed | tf_op | source)
XLA Modules:
  0.0 131.4 jit_solution(13973987592836538856)
XLA Ops:
  0.6 1.1 pack.1
  1.8 3.7 %collective-permute-start.5 = (bf16[2,64,384]{2,1,0:T(8,128)(2,1)S(1)}, bf16[2,64,384]{2,1,0:T(8,128)(2,1)S(1)}, u32[]{:S(2)}, u32[]{:S(2)}) collective-permute-start(bf16[2,64,384]{2,1,0:T(8,128)(2,1)S(1)} %get-tuple-element.40.refs_4_.refs_8_), channel_id=1, source_target_pairs={{0,6},{1,7},{2,4},{3,5},{4,2},{5,3},{6,0},{7,1},{8,14},{9,15},{10,... | collective-permute-start | bytes 294920 | tf_op jit(solution)/shard_map/ppermute | solution.py:28
  5.4 0.0 collective-permute-start.3
  5.4 0.8 collective-permute-start.1
  6.2 0.0 collective-permute-start
  6.2 2.9 %collective-permute-done.5.refs_10_.refs_14_ = bf16[2,64,384]{2,1,0:T(8,128)(2,1)S(1)} collective-permute-done((bf16[2,64,384]{2,1,0:T(8,128)(2,1)S(1)}, bf16[2,64,384]{2,1,0:T(8,128)(2,1)S(1)}, u32[]{:S(2)}, u32[]{:S(2)}) %collective-permute-start.5) | collective-permute-done | bytes 98336 | tf_op jit(solution)/shard_map/ppermute | solution.py:28
  9.1 0.0 collective-permute-start.6
  9.1 4.6 %collective-permute-done.3.refs_8_.refs_12_ = bf16[2,64,384]{2,1,0:T(8,128)(2,1)S(1)} collective-permute-done((bf16[2,64,384]{2,1,0:T(8,128)(2,1)S(1)}, bf16[2,64,384]{2,1,0:T(8,128)(2,1)S(1)}, u32[]{:S(2)}, u32[]{:S(2)}) %collective-permute-start.3) | collective-permute-done | bytes 98336 | tf_op jit(solution)/shard_map/ppermute | solution.py:28
  13.7 0.0 collective-permute-start.4
  13.7 0.0 collective-permute-done.1.refs_6_.refs_10_
  13.7 0.5 collective-permute-start.2
  14.2 6.7 %counts.1 = (bf16[512,128]{1,0:T(8,128)(2,1)S(1)}, f32[768,2304]{1,0:T(8,128)S(1)}, f32[768,2304]{1,0:T(8,128)S(1)}) custom-call(s32[2,64,138]{2,1,0:T(8,128)S(1)} %get-tuple-element.35.near_ref, f32[4608,2304]{1,0:T(8,128)} %refs_4_.1), custom_call_target="tpu_custom_call" | custom-call | flops 3000000000 | bytes 14155776 | tf_op jit(solution)/shard_map/counts/pallas_call | solution.py:479
  20.9 0.0 collective-permute-done.refs_5_.refs_9_
  20.9 0.0 collective-permute-done.4.refs_9_.refs_13_
  20.9 0.0 collective-permute-done.2.refs_7_.refs_11_
  20.9 0.4 adjoint.1.refs_0_
  21.3 2.6 %collective-permute-start.12 = (f32[144,128]{1,0:T(8,128)S(1)}, f32[144,128]{1,0:T(8,128)S(1)}, u32[]{:S(2)}, u32[]{:S(2)}) collective-permute-start(f32[144,128]{1,0:T(8,128)S(1)} %adjoint.1.refs_0_), channel_id=1, source_target_pairs={{0,6},{1,7},{2,4},{3,5},{4,2},{5,3},{6,0},{7,1},{8,14},{9,15},{10,... | collective-permute-start | bytes 221192 | tf_op jit(solution)/shard_map/ppermute | solution.py:28
  23.9 0.0 collective-permute-start.10
  23.9 1.9 %collective-permute-start.8 = (f32[144,128]{1,0:T(8,128)S(1)}, f32[144,128]{1,0:T(8,128)S(1)}, u32[]{:S(2)}, u32[]{:S(2)}) collective-permute-start(f32[144,128]{1,0:T(8,128)S(1)} %adjoint.1.refs_0_), channel_id=1, source_target_pairs={{0,2},{1,3},{2,0},{3,1},{4,6},{5,7},{6,4},{7,5},{8,10},{9,11},{10,... | collective-permute-start | bytes 221192 | tf_op jit(solution)/shard_map/ppermute | solution.py:28
  25.8 2.5 %collective-permute-done.12.refs_6_ = f32[144,128]{1,0:T(8,128)S(1)} collective-permute-done((f32[144,128]{1,0:T(8,128)S(1)}, f32[144,128]{1,0:T(8,128)S(1)}, u32[]{:S(2)}, u32[]{:S(2)}) %collective-permute-start.12) | collective-permute-done | bytes 73760 | tf_op jit(solution)/shard_map/ppermute | solution.py:28
  28.3 2.3 %collective-permute-done.10.refs_4_ = f32[144,128]{1,0:T(8,128)S(1)} collective-permute-done((f32[144,128]{1,0:T(8,128)S(1)}, f32[144,128]{1,0:T(8,128)S(1)}, u32[]{:S(2)}, u32[]{:S(2)}) %collective-permute-start.10) | collective-permute-done | bytes 73760 | tf_op jit(solution)/shard_map/ppermute | solution.py:28
  30.5 0.0 collective-permute-start.11
  30.5 0.5 collective-permute-start.9
  31.0 0.7 collective-permute-done.11.refs_5_
  31.8 0.2 collective-permute-done.9.refs_3_
  31.9 3.0 %jacobian_first.1 = (bf16[16,2304]{1,0:T(8,128)(2,1)S(1)}, bf16[16,2304]{1,0:T(8,128)(2,1)S(1)}, bf16[16,2304]{1,0:T(8,128)(2,1)S(1)}, bf16[16,2304]{1,0:T(8,128)(2,1)S(1)}, f32[768,2304]{1,0:T(8,128)S(1)}) custom-call(f32[144,128]{1,0:T(8,128)S(1)} %adjoint.1.refs_0_, f32[144,128]{1,0:T(8,128)S(1)} %collective-permute-done.7.refs_1_, ...), custom_call_target="tpu_custom_call" | custom-call | flops 3000000000 | bytes 7077888 | tf_op jit(solution)/shard_map/jacobian_first/pallas_call | solution.py:507
  35.0 0.6 collective-permute-start.17
  35.6 0.5 collective-permute-start.18
  36.1 2.4 %collective-permute-start.19 = (bf16[16,2304]{1,0:T(8,128)(2,1)S(1)}, bf16[16,2304]{1,0:T(8,128)(2,1)S(1)}, u32[]{:S(2)}, u32[]{:S(2)}) collective-permute-start(bf16[16,2304]{1,0:T(8,128)(2,1)S(1)} %get-tuple-element.48), channel_id=1, source_target_pairs={{0,24},{8,16},{16,8},{24,0},{1,25},{9,17},{17,9},{25,1},{2,26},{10... | collective-permute-start | bytes 221192 | tf_op jit(solution)/shard_map/ppermute | solution.py:28
  38.5 3.4 %jacobian_last.1 = (bf16[16,4608]{1,0:T(8,128)(2,1)S(1)}, bf16[16,4608]{1,0:T(8,128)(2,1)S(1)}, bf16[16,4608]{1,0:T(8,128)(2,1)S(1)}, bf16[16,4608]{1,0:T(8,128)(2,1)S(1)}, f32[768,2304]{1,0:T(8,128)S(1)}) custom-call(f32[144,128]{1,0:T(8,128)S(1)} %adjoint.1.refs_0_, f32[144,128]{1,0:T(8,128)S(1)} %collective-permute-done.7.refs_1_, ...), custom_call_target="tpu_custom_call" | custom-call | flops 3000000000 | bytes 7077888 | tf_op jit(solution)/shard_map/jacobian_last/pallas_call | solution.py:507
  42.0 0.6 collective-permute-start.14
  42.6 0.5 collective-permute-start.15
  43.1 2.5 %collective-permute-start.16 = (bf16[16,4608]{1,0:T(8,128)(2,1)S(1)}, bf16[16,4608]{1,0:T(8,128)(2,1)S(1)}, u32[]{:S(2)}, u32[]{:S(2)}) collective-permute-start(bf16[16,4608]{1,0:T(8,128)(2,1)S(1)} %get-tuple-element.44), channel_id=1, source_target_pairs={{0,24},{8,16},{16,8},{24,0},{1,25},{9,17},{17,9},{25,1},{2,26},{10... | collective-permute-start | bytes 442376 | tf_op jit(solution)/shard_map/ppermute | solution.py:28
  45.5 5.4 %product_first.1.refs_4_ = f32[64,2304]{1,0:T(8,128)S(1)} custom-call(bf16[16,2304]{1,0:T(8,128)(2,1)S(1)} %get-tuple-element.45.refs_0_, bf16[16,2304]{1,0:T(8,128)(2,1)S(1)} %collective-permute-done.17.refs_1_, bf16[16,2304]{1,0:T(8,128)(2,1)S(1)} %collective-permute-done.18.refs_2_, bf16[16,2304]{1,0:T(8,128)(2,1)S(1)} %collective-permute-done.19.refs_3_, ...), custom_call_target="tpu_custom_call" | custom-call | flops 2717908992 | bytes 21233664 | tf_op jit(solution)/shard_map/product_first/pallas_call | solution.py:527
  51.0 0.0 copy-start
  51.0 0.0 copy-start.1
  51.0 0.0 copy-start.2
  51.0 8.5 %product_last.1 = (f32[16,2560]{1,0:T(8,128)S(1)}, f32[16,2560]{1,0:T(8,128)S(1)}, f32[16,2560]{1,0:T(8,128)S(1)}, f32[16,2560]{1,0:T(8,128)S(1)}) custom-call(bf16[16,4608]{1,0:T(8,128)(2,1)S(1)} %get-tuple-element.41.refs_0_, bf16[16,4608]{1,0:T(8,128)(2,1)S(1)} %collective-permute-done.14.refs_1_, bf16[16,4608]{1,0:T(8,128)(2,1)S(1)} %collective-permute-done.15.refs_2_, ...), custom_call_target="tpu_custom_call" | custom-call | flops 2717908992 | bytes 21233664 | tf_op jit(solution)/shard_map/product_last/pallas_call | solution.py:538
  59.5 1.3 collective-permute-start.20
  60.7 0.7 collective-permute-start.21
  61.4 1.6 %collective-permute-start.22 = (f32[16,2560]{1,0:T(8,128)S(1)}, f32[16,2560]{1,0:T(8,128)S(1)}, u32[]{:S(2)}, u32[]{:S(2)}) collective-permute-start(f32[16,2560]{1,0:T(8,128)S(1)} %get-tuple-element.56), channel_id=1, source_target_pairs={{0,24},{8,16},{16,8},{24,0},{1,25},{9,17},{17,9},{25,1},{2,26},{10... | collective-permute-start | bytes 491528 | tf_op jit(solution)/shard_map/ppermute | solution.py:28
  63.0 3.1 %collective-permute-done.20.refs_1_ = f32[16,2560]{1,0:T(8,128)S(1)} collective-permute-done((f32[16,2560]{1,0:T(8,128)S(1)}, f32[16,2560]{1,0:T(8,128)S(1)}, u32[]{:S(2)}, u32[]{:S(2)}) %collective-permute-start.20) | collective-permute-done | bytes 163872 | tf_op jit(solution)/shard_map/ppermute | solution.py:28
  66.1 2.5 %collective-permute-done.21.refs_2_ = f32[16,2560]{1,0:T(8,128)S(1)} collective-permute-done((f32[16,2560]{1,0:T(8,128)S(1)}, f32[16,2560]{1,0:T(8,128)S(1)}, u32[]{:S(2)}, u32[]{:S(2)}) %collective-permute-start.21) | collective-permute-done | bytes 163872 | tf_op jit(solution)/shard_map/ppermute | solution.py:28
  68.6 2.6 %collective-permute-start.25 = (bf16[16,2816]{1,0:T(8,128)(2,1)S(1)}, bf16[16,2816]{1,0:T(8,128)(2,1)S(1)}, u32[]{:S(2)}, u32[]{:S(2)}) collective-permute-start(bf16[16,2816]{1,0:T(8,128)(2,1)S(1)} %get-tuple-element.57.refs_0_), channel_id=1, source_target_pairs={{0,6},{1,7},{2,4},{3,5},{4,2},{5,3},{6,0},{7,1},{8,14},{9,15},{10,... | collective-permute-start | bytes 270344 | tf_op jit(solution)/shard_map/ppermute | solution.py:28
  71.2 1.9 %collective-permute-start.23 = (bf16[16,2816]{1,0:T(8,128)(2,1)S(1)}, bf16[16,2816]{1,0:T(8,128)(2,1)S(1)}, u32[]{:S(2)}, u32[]{:S(2)}) collective-permute-start(bf16[16,2816]{1,0:T(8,128)(2,1)S(1)} %get-tuple-element.57.refs_0_), channel_id=1, source_target_pairs={{0,2},{1,3},{2,0},{3,1},{4,6},{5,7},{6,4},{7,5},{8,10},{9,11},{10,... | collective-permute-start | bytes 270344 | tf_op jit(solution)/shard_map/ppermute | solution.py:28
  73.1 1.9 %collective-permute-done.25.refs_3_ = bf16[16,2816]{1,0:T(8,128)(2,1)S(1)} collective-permute-done((bf16[16,2816]{1,0:T(8,128)(2,1)S(1)}, bf16[16,2816]{1,0:T(8,128)(2,1)S(1)}, u32[]{:S(2)}, u32[]{:S(2)}) %collective-permute-start.25) | collective-permute-done | bytes 90144 | tf_op jit(solution)/shard_map/ppermute | solution.py:28
  75.0 1.9 %collective-permute-done.24.refs_2_ = bf16[16,2816]{1,0:T(8,128)(2,1)S(1)} collective-permute-done((bf16[16,2816]{1,0:T(8,128)(2,1)S(1)}, bf16[16,2816]{1,0:T(8,128)(2,1)S(1)}, u32[]{:S(2)}, u32[]{:S(2)}) %collective-permute-start.24) | collective-permute-done | bytes 90144 | tf_op jit(solution)/shard_map/ppermute | solution.py:28
  77.0 0.1 route.1
  77.0 0.1 collective-permute-start.26
  77.1 1.2 collective-permute-done.26.refs_1_
  78.3 2.0 %inverse.1 = (f32[64,64]{1,0:T(8,128)S(1)}, f32[4,1,576]{2,1,0:T(1,128)S(1)}) custom-call(f32[64,64]{1,0:T(8,128)S(1)} %get-tuple-element.58.refs_0_, f32[64,64]{1,0:T(8,128)S(1)} %collective-permute-done.26.refs_1_, f32[16,2304]{1,0:T(8,128)S(1)} %get-tuple-element.59.refs_2_, f32[1,64]{1,0:T(1,128)S(1)} %bitcast.2, f32[1,64]{1,0:T(1,128)S(1)} %bitcast.3), custom_call_target="tpu_custom_call" | custom-call | tf_op jit(solution)/shard_map/inverse/pallas_call | solution.py:579
  80.3 3.6 %collective-permute-start.30 = (f32[4,1,576]{2,1,0:T(1,128)S(1)}, f32[4,1,576]{2,1,0:T(1,128)S(1)}, u32[]{:S(2)}, u32[]{:S(2)}) collective-permute-start(f32[4,1,576]{2,1,0:T(1,128)S(1)} %get-tuple-element.60), channel_id=1, source_target_pairs={{0,3},{1,7},{2,11},{3,15},{4,19},{5,23},{6,27},{7,31},{8,2},{9,6},... | collective-permute-start | bytes 27656 | tf_op jit(solution)/shard_map/ppermute | solution.py:602
  83.9 0.4 collective-permute-start.31
  84.3 0.5 collective-permute-start.32
  84.8 2.7 %collective-permute-start.33 = (bf16[16,4608]{1,0:T(8,128)(2,1)S(1)}, bf16[16,4608]{1,0:T(8,128)(2,1)S(1)}, u32[]{:S(2)}, u32[]{:S(2)}) collective-permute-start(bf16[16,4608]{1,0:T(8,128)(2,1)S(1)} %get-tuple-element.64), channel_id=1, source_target_pairs={{0,24},{8,16},{16,8},{24,0},{1,25},{9,17},{17,9},{25,1},{2,26},{10... | collective-permute-start | bytes 442376 | tf_op jit(solution)/shard_map/ppermute | solution.py:28
  87.5 1.2 collective-permute-start.29
  88.7 0.6 collective-permute-start.28
  89.3 4.7 %collective-permute-done.29 = f32[4,1,576]{2,1,0:T(1,128)S(1)} collective-permute-done((f32[4,1,576]{2,1,0:T(1,128)S(1)}, f32[4,1,576]{2,1,0:T(1,128)S(1)}, u32[]{:S(2)}, u32[]{:S(2)}) %collective-permute-start.29) | collective-permute-done | bytes 9248 | tf_op jit(solution)/shard_map/ppermute | solution.py:602
  94.0 2.1 %collective-permute-start.27 = (f32[4,1,576]{2,1,0:T(1,128)S(1)}, f32[4,1,576]{2,1,0:T(1,128)S(1)}, u32[]{:S(2)}, u32[]{:S(2)}) collective-permute-start(f32[4,1,576]{2,1,0:T(1,128)S(1)} %get-tuple-element.60), channel_id=1, source_target_pairs={{0,0},{1,4},{2,8},{3,12},{4,16},{5,20},{6,24},{7,28},{8,1},{9,5},{... | collective-permute-start | bytes 27656 | tf_op jit(solution)/shard_map/ppermute | solution.py:602
  96.2 0.1 merge.1
  96.2 0.8 collective-permute-start.34
  97.0 6.1 %collective-permute-done.27 = f32[4,1,576]{2,1,0:T(1,128)S(1)} collective-permute-done((f32[4,1,576]{2,1,0:T(1,128)S(1)}, f32[4,1,576]{2,1,0:T(1,128)S(1)}, u32[]{:S(2)}, u32[]{:S(2)}) %collective-permute-start.27) | collective-permute-done | bytes 9248 | tf_op jit(solution)/shard_map/ppermute | solution.py:602
  103.1 0.6 add_add_fusion
  103.8 27.7 %update.1 = f32[4608,2304]{1,0:T(8,128)} custom-call(bf16[64,2304]{1,0:T(8,128)(2,1)S(1)} %get-tuple-element.65.mine_ref, bf16[64,2304]{1,0:T(8,128)(2,1)S(1)} %collective-permute-done.34.other_ref, bf16[64,2304]{1,0:T(8,128)(2,1)S(1)} %get-tuple-element.66.right_ref, f32[64,64]{1,0:T(8,128)S(1)} %get-tuple-element.67.inverse_ref, ...), custom_call_target="tpu_custom_call" | custom-call | flops 1358954496 | bytes 42467328 | tf_op jit(solution)/shard_map/update/pallas_call | solution.py:605
  (29 shorter events, 0.2 us)
Async XLA Ops:
  1.8 7.4 %collective-permute-start.5 = (bf16[2,64,384]{2,1,0:T(8,128)(2,1)S(1)}, bf16[2,64,384]{2,1,0:T(8,128)(2,1)S(1)}, u32[]{:S(2)}, u32[]{:S(2)}) collective-permute-start(bf16[2,64,384]{2,1,0:T(8,128)(2,1)S(1)} %get-tuple-element.40.refs_4_.refs_8_), channel_id=1, source_target_pairs={{0,6},{1,7},{2,4},{3,5},{4,2},{5,3},{6,0},{7,1},{8,14},{9,15},{10,... | collective-permute-start | bytes 294920 | tf_op jit(solution)/shard_map/ppermute | solution.py:28
  5.4 8.3 %collective-permute-start.3 = (bf16[2,64,384]{2,1,0:T(8,128)(2,1)S(1)}, bf16[2,64,384]{2,1,0:T(8,128)(2,1)S(1)}, u32[]{:S(2)}, u32[]{:S(2)}) collective-permute-start(bf16[2,64,384]{2,1,0:T(8,128)(2,1)S(1)} %get-tuple-element.40.refs_4_.refs_8_), channel_id=1, source_target_pairs={{0,4},{1,5},{2,6},{3,7},{4,0},{5,1},{6,2},{7,3},{8,12},{9,13},{10,... | collective-permute-start | bytes 294920 | tf_op jit(solution)/shard_map/ppermute | solution.py:28
  5.4 8.3 %collective-permute-start.1 = (bf16[2,64,384]{2,1,0:T(8,128)(2,1)S(1)}, bf16[2,64,384]{2,1,0:T(8,128)(2,1)S(1)}, u32[]{:S(2)}, u32[]{:S(2)}) collective-permute-start(bf16[2,64,384]{2,1,0:T(8,128)(2,1)S(1)} %get-tuple-element.40.refs_4_.refs_8_), channel_id=1, source_target_pairs={{0,2},{1,3},{2,0},{3,1},{4,6},{5,7},{6,4},{7,5},{8,10},{9,11},{10,... | collective-permute-start | bytes 294920 | tf_op jit(solution)/shard_map/ppermute | solution.py:28
  6.2 14.7 %collective-permute-start = (bf16[2,64,384]{2,1,0:T(8,128)(2,1)S(1)}, bf16[2,64,384]{2,1,0:T(8,128)(2,1)S(1)}, u32[]{:S(2)}, u32[]{:S(2)}) collective-permute-start(bf16[2,64,384]{2,1,0:T(8,128)(2,1)S(1)} %get-tuple-element.40.refs_4_.refs_8_), channel_id=1, source_target_pairs={{0,1},{1,0},{2,3},{3,2},{4,5},{5,4},{6,7},{7,6},{8,9},{9,8},{10,11... | collective-permute-start | bytes 294920 | tf_op jit(solution)/shard_map/ppermute | solution.py:28
  9.1 11.8 %collective-permute-start.6 = (bf16[2,64,384]{2,1,0:T(8,128)(2,1)S(1)}, bf16[2,64,384]{2,1,0:T(8,128)(2,1)S(1)}, u32[]{:S(2)}, u32[]{:S(2)}) collective-permute-start(bf16[2,64,384]{2,1,0:T(8,128)(2,1)S(1)} %collective-permute-done.5.refs_10_.refs_14_), channel_id=1, source_target_pairs={{0,1},{1,0},{2,3},{3,2},{4,5},{5,4},{6,7},{7,6},{8,9},{9,8},{10,11... | collective-permute-start | bytes 294920 | tf_op jit(solution)/shard_map/ppermute | solution.py:28
  13.7 7.2 %collective-permute-start.4 = (bf16[2,64,384]{2,1,0:T(8,128)(2,1)S(1)}, bf16[2,64,384]{2,1,0:T(8,128)(2,1)S(1)}, u32[]{:S(2)}, u32[]{:S(2)}) collective-permute-start(bf16[2,64,384]{2,1,0:T(8,128)(2,1)S(1)} %collective-permute-done.3.refs_8_.refs_12_), channel_id=1, source_target_pairs={{0,1},{1,0},{2,3},{3,2},{4,5},{5,4},{6,7},{7,6},{8,9},{9,8},{10,11... | collective-permute-start | bytes 294920 | tf_op jit(solution)/shard_map/ppermute | solution.py:28
  13.7 7.2 %collective-permute-start.2 = (bf16[2,64,384]{2,1,0:T(8,128)(2,1)S(1)}, bf16[2,64,384]{2,1,0:T(8,128)(2,1)S(1)}, u32[]{:S(2)}, u32[]{:S(2)}) collective-permute-start(bf16[2,64,384]{2,1,0:T(8,128)(2,1)S(1)} %collective-permute-done.1.refs_6_.refs_10_), channel_id=1, source_target_pairs={{0,1},{1,0},{2,3},{3,2},{4,5},{5,4},{6,7},{7,6},{8,9},{9,8},{10,11... | collective-permute-start | bytes 294920 | tf_op jit(solution)/shard_map/ppermute | solution.py:28
  21.3 6.9 %collective-permute-start.12 = (f32[144,128]{1,0:T(8,128)S(1)}, f32[144,128]{1,0:T(8,128)S(1)}, u32[]{:S(2)}, u32[]{:S(2)}) collective-permute-start(f32[144,128]{1,0:T(8,128)S(1)} %adjoint.1.refs_0_), channel_id=1, source_target_pairs={{0,6},{1,7},{2,4},{3,5},{4,2},{5,3},{6,0},{7,1},{8,14},{9,15},{10,... | collective-permute-start | bytes 221192 | tf_op jit(solution)/shard_map/ppermute | solution.py:28
  23.9 6.6 %collective-permute-start.10 = (f32[144,128]{1,0:T(8,128)S(1)}, f32[144,128]{1,0:T(8,128)S(1)}, u32[]{:S(2)}, u32[]{:S(2)}) collective-permute-start(f32[144,128]{1,0:T(8,128)S(1)} %adjoint.1.refs_0_), channel_id=1, source_target_pairs={{0,4},{1,5},{2,6},{3,7},{4,0},{5,1},{6,2},{7,3},{8,12},{9,13},{10,... | collective-permute-start | bytes 221192 | tf_op jit(solution)/shard_map/ppermute | solution.py:28
  23.9 6.6 %collective-permute-start.8 = (f32[144,128]{1,0:T(8,128)S(1)}, f32[144,128]{1,0:T(8,128)S(1)}, u32[]{:S(2)}, u32[]{:S(2)}) collective-permute-start(f32[144,128]{1,0:T(8,128)S(1)} %adjoint.1.refs_0_), channel_id=1, source_target_pairs={{0,2},{1,3},{2,0},{3,1},{4,6},{5,7},{6,4},{7,5},{8,10},{9,11},{10,... | collective-permute-start | bytes 221192 | tf_op jit(solution)/shard_map/ppermute | solution.py:28
  25.8 5.3 %collective-permute-start.7 = (f32[144,128]{1,0:T(8,128)S(1)}, f32[144,128]{1,0:T(8,128)S(1)}, u32[]{:S(2)}, u32[]{:S(2)}) collective-permute-start(f32[144,128]{1,0:T(8,128)S(1)} %adjoint.1.refs_0_), channel_id=1, source_target_pairs={{0,1},{1,0},{2,3},{3,2},{4,5},{5,4},{6,7},{7,6},{8,9},{9,8},{10,11... | collective-permute-start | bytes 221192 | tf_op jit(solution)/shard_map/ppermute | solution.py:28
  28.2 2.8 %collective-permute-start.13 = (f32[144,128]{1,0:T(8,128)S(1)}, f32[144,128]{1,0:T(8,128)S(1)}, u32[]{:S(2)}, u32[]{:S(2)}) collective-permute-start(f32[144,128]{1,0:T(8,128)S(1)} %collective-permute-done.12.refs_6_), channel_id=1, source_target_pairs={{0,1},{1,0},{2,3},{3,2},{4,5},{5,4},{6,7},{7,6},{8,9},{9,8},{10,11... | collective-permute-start | bytes 221192 | tf_op jit(solution)/shard_map/ppermute | solution.py:28
  30.5 1.3 collective-permute-start.11
  30.5 1.4 %collective-permute-start.9 = (f32[144,128]{1,0:T(8,128)S(1)}, f32[144,128]{1,0:T(8,128)S(1)}, u32[]{:S(2)}, u32[]{:S(2)}) collective-permute-start(f32[144,128]{1,0:T(8,128)S(1)} %collective-permute-done.8.refs_2_), channel_id=1, source_target_pairs={{0,1},{1,0},{2,3},{3,2},{4,5},{5,4},{6,7},{7,6},{8,9},{9,8},{10,11... | collective-permute-start | bytes 221192 | tf_op jit(solution)/shard_map/ppermute | solution.py:28
  35.0 8.1 %collective-permute-start.17 = (bf16[16,2304]{1,0:T(8,128)(2,1)S(1)}, bf16[16,2304]{1,0:T(8,128)(2,1)S(1)}, u32[]{:S(2)}, u32[]{:S(2)}) collective-permute-start(bf16[16,2304]{1,0:T(8,128)(2,1)S(1)} %get-tuple-element.46), channel_id=1, source_target_pairs={{0,8},{8,0},{16,24},{24,16},{1,9},{9,1},{17,25},{25,17},{2,10},{10... | collective-permute-start | bytes 221192 | tf_op jit(solution)/shard_map/ppermute | solution.py:28
  35.6 9.9 %collective-permute-start.18 = (bf16[16,2304]{1,0:T(8,128)(2,1)S(1)}, bf16[16,2304]{1,0:T(8,128)(2,1)S(1)}, u32[]{:S(2)}, u32[]{:S(2)}) collective-permute-start(bf16[16,2304]{1,0:T(8,128)(2,1)S(1)} %get-tuple-element.47), channel_id=1, source_target_pairs={{0,16},{8,24},{16,0},{24,8},{1,17},{9,25},{17,1},{25,9},{2,18},{10... | collective-permute-start | bytes 221192 | tf_op jit(solution)/shard_map/ppermute | solution.py:28
  36.1 9.4 %collective-permute-start.19 = (bf16[16,2304]{1,0:T(8,128)(2,1)S(1)}, bf16[16,2304]{1,0:T(8,128)(2,1)S(1)}, u32[]{:S(2)}, u32[]{:S(2)}) collective-permute-start(bf16[16,2304]{1,0:T(8,128)(2,1)S(1)} %get-tuple-element.48), channel_id=1, source_target_pairs={{0,24},{8,16},{16,8},{24,0},{1,25},{9,17},{17,9},{25,1},{2,26},{10... | collective-permute-start | bytes 221192 | tf_op jit(solution)/shard_map/ppermute | solution.py:28
  42.0 9.0 %collective-permute-start.14 = (bf16[16,4608]{1,0:T(8,128)(2,1)S(1)}, bf16[16,4608]{1,0:T(8,128)(2,1)S(1)}, u32[]{:S(2)}, u32[]{:S(2)}) collective-permute-start(bf16[16,4608]{1,0:T(8,128)(2,1)S(1)} %get-tuple-element.42), channel_id=1, source_target_pairs={{0,8},{8,0},{16,24},{24,16},{1,9},{9,1},{17,25},{25,17},{2,10},{10... | collective-permute-start | bytes 442376 | tf_op jit(solution)/shard_map/ppermute | solution.py:28
  42.6 8.4 %collective-permute-start.15 = (bf16[16,4608]{1,0:T(8,128)(2,1)S(1)}, bf16[16,4608]{1,0:T(8,128)(2,1)S(1)}, u32[]{:S(2)}, u32[]{:S(2)}) collective-permute-start(bf16[16,4608]{1,0:T(8,128)(2,1)S(1)} %get-tuple-element.43), channel_id=1, source_target_pairs={{0,16},{8,24},{16,0},{24,8},{1,17},{9,25},{17,1},{25,9},{2,18},{10... | collective-permute-start | bytes 442376 | tf_op jit(solution)/shard_map/ppermute | solution.py:28
  43.1 7.9 %collective-permute-start.16 = (bf16[16,4608]{1,0:T(8,128)(2,1)S(1)}, bf16[16,4608]{1,0:T(8,128)(2,1)S(1)}, u32[]{:S(2)}, u32[]{:S(2)}) collective-permute-start(bf16[16,4608]{1,0:T(8,128)(2,1)S(1)} %get-tuple-element.44), channel_id=1, source_target_pairs={{0,24},{8,16},{16,8},{24,0},{1,25},{9,17},{17,9},{25,1},{2,26},{10... | collective-permute-start | bytes 442376 | tf_op jit(solution)/shard_map/ppermute | solution.py:28
  51.0 27.3 %copy-start = (f32[64]{0:T(128)S(1)}, f32[64]{0:T(128)}, u32[]{:S(2)}) copy-start(f32[64]{0:T(128)} %param.20) | copy-start | bytes 772
  51.0 27.3 %copy-start.1 = (f32[64]{0:T(128)S(1)}, f32[64]{0:T(128)}, u32[]{:S(2)}) copy-start(f32[64]{0:T(128)} %param.21) | copy-start | bytes 772
  51.0 52.1 %copy-start.2 = (f32[576]{0:T(1024)S(1)}, f32[576]{0:T(1024)}, u32[]{:S(2)}) copy-start(f32[576]{0:T(1024)} %param.12) | copy-start | bytes 6916
  59.5 6.6 %collective-permute-start.20 = (f32[16,2560]{1,0:T(8,128)S(1)}, f32[16,2560]{1,0:T(8,128)S(1)}, u32[]{:S(2)}, u32[]{:S(2)}) collective-permute-start(f32[16,2560]{1,0:T(8,128)S(1)} %get-tuple-element.54), channel_id=1, source_target_pairs={{0,8},{8,0},{16,24},{24,16},{1,9},{9,1},{17,25},{25,17},{2,10},{10... | collective-permute-start | bytes 491528 | tf_op jit(solution)/shard_map/ppermute | solution.py:28
  60.7 7.8 %collective-permute-start.21 = (f32[16,2560]{1,0:T(8,128)S(1)}, f32[16,2560]{1,0:T(8,128)S(1)}, u32[]{:S(2)}, u32[]{:S(2)}) collective-permute-start(f32[16,2560]{1,0:T(8,128)S(1)} %get-tuple-element.55), channel_id=1, source_target_pairs={{0,16},{8,24},{16,0},{24,8},{1,17},{9,25},{17,1},{25,9},{2,18},{10... | collective-permute-start | bytes 491528 | tf_op jit(solution)/shard_map/ppermute | solution.py:28
  61.4 7.2 %collective-permute-start.22 = (f32[16,2560]{1,0:T(8,128)S(1)}, f32[16,2560]{1,0:T(8,128)S(1)}, u32[]{:S(2)}, u32[]{:S(2)}) collective-permute-start(f32[16,2560]{1,0:T(8,128)S(1)} %get-tuple-element.56), channel_id=1, source_target_pairs={{0,24},{8,16},{16,8},{24,0},{1,25},{9,17},{17,9},{25,1},{2,26},{10... | collective-permute-start | bytes 491528 | tf_op jit(solution)/shard_map/ppermute | solution.py:28
  68.6 6.4 %collective-permute-start.25 = (bf16[16,2816]{1,0:T(8,128)(2,1)S(1)}, bf16[16,2816]{1,0:T(8,128)(2,1)S(1)}, u32[]{:S(2)}, u32[]{:S(2)}) collective-permute-start(bf16[16,2816]{1,0:T(8,128)(2,1)S(1)} %get-tuple-element.57.refs_0_), channel_id=1, source_target_pairs={{0,6},{1,7},{2,4},{3,5},{4,2},{5,3},{6,0},{7,1},{8,14},{9,15},{10,... | collective-permute-start | bytes 270344 | tf_op jit(solution)/shard_map/ppermute | solution.py:28
  71.2 5.7 %collective-permute-start.24 = (bf16[16,2816]{1,0:T(8,128)(2,1)S(1)}, bf16[16,2816]{1,0:T(8,128)(2,1)S(1)}, u32[]{:S(2)}, u32[]{:S(2)}) collective-permute-start(bf16[16,2816]{1,0:T(8,128)(2,1)S(1)} %get-tuple-element.57.refs_0_), channel_id=1, source_target_pairs={{0,4},{1,5},{2,6},{3,7},{4,0},{5,1},{6,2},{7,3},{8,12},{9,13},{10,... | collective-permute-start | bytes 270344 | tf_op jit(solution)/shard_map/ppermute | solution.py:28
  71.2 5.7 %collective-permute-start.23 = (bf16[16,2816]{1,0:T(8,128)(2,1)S(1)}, bf16[16,2816]{1,0:T(8,128)(2,1)S(1)}, u32[]{:S(2)}, u32[]{:S(2)}) collective-permute-start(bf16[16,2816]{1,0:T(8,128)(2,1)S(1)} %get-tuple-element.57.refs_0_), channel_id=1, source_target_pairs={{0,2},{1,3},{2,0},{3,1},{4,6},{5,7},{6,4},{7,5},{8,10},{9,11},{10,... | collective-permute-start | bytes 270344 | tf_op jit(solution)/shard_map/ppermute | solution.py:28
  77.0 1.3 collective-permute-start.26
  80.3 8.4 %collective-permute-start.30 = (f32[4,1,576]{2,1,0:T(1,128)S(1)}, f32[4,1,576]{2,1,0:T(1,128)S(1)}, u32[]{:S(2)}, u32[]{:S(2)}) collective-permute-start(f32[4,1,576]{2,1,0:T(1,128)S(1)} %get-tuple-element.60), channel_id=1, source_target_pairs={{0,3},{1,7},{2,11},{3,15},{4,19},{5,23},{6,27},{7,31},{8,2},{9,6},... | collective-permute-start | bytes 27656 | tf_op jit(solution)/shard_map/ppermute | solution.py:602
  83.9 12.2 %collective-permute-start.31 = (bf16[16,4608]{1,0:T(8,128)(2,1)S(1)}, bf16[16,4608]{1,0:T(8,128)(2,1)S(1)}, u32[]{:S(2)}, u32[]{:S(2)}) collective-permute-start(bf16[16,4608]{1,0:T(8,128)(2,1)S(1)} %get-tuple-element.62), channel_id=1, source_target_pairs={{0,8},{8,0},{16,24},{24,16},{1,9},{9,1},{17,25},{25,17},{2,10},{10... | collective-permute-start | bytes 442376 | tf_op jit(solution)/shard_map/ppermute | solution.py:28
  84.3 11.8 %collective-permute-start.32 = (bf16[16,4608]{1,0:T(8,128)(2,1)S(1)}, bf16[16,4608]{1,0:T(8,128)(2,1)S(1)}, u32[]{:S(2)}, u32[]{:S(2)}) collective-permute-start(bf16[16,4608]{1,0:T(8,128)(2,1)S(1)} %get-tuple-element.63), channel_id=1, source_target_pairs={{0,16},{8,24},{16,0},{24,8},{1,17},{9,25},{17,1},{25,9},{2,18},{10... | collective-permute-start | bytes 442376 | tf_op jit(solution)/shard_map/ppermute | solution.py:28
  84.8 11.3 %collective-permute-start.33 = (bf16[16,4608]{1,0:T(8,128)(2,1)S(1)}, bf16[16,4608]{1,0:T(8,128)(2,1)S(1)}, u32[]{:S(2)}, u32[]{:S(2)}) collective-permute-start(bf16[16,4608]{1,0:T(8,128)(2,1)S(1)} %get-tuple-element.64), channel_id=1, source_target_pairs={{0,24},{8,16},{16,8},{24,0},{1,25},{9,17},{17,9},{25,1},{2,26},{10... | collective-permute-start | bytes 442376 | tf_op jit(solution)/shard_map/ppermute | solution.py:28
  87.5 6.5 %collective-permute-start.29 = (f32[4,1,576]{2,1,0:T(1,128)S(1)}, f32[4,1,576]{2,1,0:T(1,128)S(1)}, u32[]{:S(2)}, u32[]{:S(2)}) collective-permute-start(f32[4,1,576]{2,1,0:T(1,128)S(1)} %get-tuple-element.60), channel_id=1, source_target_pairs={{0,2},{1,6},{2,10},{3,14},{4,18},{5,22},{6,26},{7,30},{8,3},{9,7},... | collective-permute-start | bytes 27656 | tf_op jit(solution)/shard_map/ppermute | solution.py:602
  88.7 7.4 %collective-permute-start.28 = (f32[4,1,576]{2,1,0:T(1,128)S(1)}, f32[4,1,576]{2,1,0:T(1,128)S(1)}, u32[]{:S(2)}, u32[]{:S(2)}) collective-permute-start(f32[4,1,576]{2,1,0:T(1,128)S(1)} %get-tuple-element.60), channel_id=1, source_target_pairs={{0,1},{1,5},{2,9},{3,13},{4,17},{5,21},{6,25},{7,29},{8,0},{9,4},{... | collective-permute-start | bytes 27656 | tf_op jit(solution)/shard_map/ppermute | solution.py:602
  94.0 9.2 %collective-permute-start.27 = (f32[4,1,576]{2,1,0:T(1,128)S(1)}, f32[4,1,576]{2,1,0:T(1,128)S(1)}, u32[]{:S(2)}, u32[]{:S(2)}) collective-permute-start(f32[4,1,576]{2,1,0:T(1,128)S(1)} %get-tuple-element.60), channel_id=1, source_target_pairs={{0,0},{1,4},{2,8},{3,12},{4,16},{5,20},{6,24},{7,28},{8,1},{9,5},{... | collective-permute-start | bytes 27656 | tf_op jit(solution)/shard_map/ppermute | solution.py:602
  96.2 7.5 %collective-permute-start.34 = (bf16[64,2304]{1,0:T(8,128)(2,1)S(1)}, bf16[64,2304]{1,0:T(8,128)(2,1)S(1)}, u32[]{:S(2)}, u32[]{:S(2)}) collective-permute-start(bf16[64,2304]{1,0:T(8,128)(2,1)S(1)} %get-tuple-element.65.mine_ref), channel_id=1, source_target_pairs={{0,1},{1,0},{2,3},{3,2},{4,5},{5,4},{6,7},{7,6},{8,9},{9,8},{10,11... | collective-permute-start | bytes 884744 | tf_op jit(solution)/shard_map/ppermute | solution.py:28
where the time goes:
time: 132 us; the launch traced here: 131 us
  Pallas kernels  58.3 us (44%)
  starting transfers between devices  37 us (28%)
  waiting for transfers between devices  34.6 us (26%)
    ppermute x31, starting transfers between devices, swap(): return lax.ppermute(block, axis, [(i, i ^ step) for i in range(n)])  29.5 us
    pallas_call x1, Pallas kernels, on_device(): pl.pallas_call(update_kernel, out_shape=shape((height, width)), grid=(til...  27.7 us
    ppermute x31, waiting for transfers between devices, swap(): return lax.ppermute(block, axis, [(i, i ^ step) for i in range(n)])  23.8 us
    ppermute x4, waiting for transfers between devices, on_device(): moved = lax.ppermute(change, ('row', 'col'), pairs)  10.8 us
    pallas_call x1, Pallas kernels, on_device(): pl.pallas_call(functools.partial(product_last_kernel, rows, depth, rest),...  8.45 us
    ppermute x4, starting transfers between devices, on_device(): moved = lax.ppermute(change, ('row', 'col'), pairs)  7.49 us
    pallas_call x1, Pallas kernels, on_device(): pl.pallas_call(functools.partial(counts_kernel, 0), out_shape=[shape((ato...  6.7 us
    pallas_call x2, Pallas kernels, on_device(): pl.pallas_call(functools.partial(jacobian_kernel, cols, rows, width_in, s...  6.44 us
  transfers between devices with their start and end apart: 35, of which 13 were waited for; matrix products, arithmetic and copies ran while one was open for 1% of the time, Pallas kernels for 12%

commit v1 on v0

--- a/solution.py
+++ b/solution.py
@@ -14,7 +14,9 @@
 F32 = jnp.float32
 BF16 = jnp.bfloat16
 EACH = (3, 2, 1)
-EARLY, LATER = 2, 2
+EARLY, LATER = 3, 2
+CUT = 768
+THIN, SLOTS = 128, 4
 
 VMEM = pl.BlockSpec(memory_space=pltpu.VMEM)
 SMEM = pl.BlockSpec(memory_space=pltpu.SMEM)
@@ -324,13 +326,18 @@
     ).astype(BF16)
 
 
-def route_kernel(peers, width, *refs):
-    pieces, outs, inner_ref, held = refs[: -peers - 2], refs[-peers - 2 : -2], refs[-2], refs[-1]
+def route_kernel(peers, width, exact_ref, *refs):
+    pieces, outs, (inner_ref, held, rest) = refs[: -peers - 3], refs[-peers - 3 : -3], refs[-3:]
     row, col = lax.axis_index("row"), lax.axis_index("col")
     count = len(pieces)
     per_block = count // peers
-    measures = pieces[0].shape[0]
+    measures, _ = exact_ref.shape
     overall = inner_ref.shape[0]
+    share = width // peers
+    exact = exact_ref[...]
+    low = exact - exact.astype(BF16).astype(F32)
+    for q in range(peers):
+        rest[q] = low[:, q * share : (q + 1) * share]
     total = jnp.zeros((measures, overall * peers), F32)
     for k, piece in enumerate(pieces):
         held[(col // 2) ^ k] = piece[:, pl.ds(0, width)]
@@ -342,14 +349,12 @@
         for p in range(per_block):
             outs[k][:, pl.ds(p * width, width)] = held[(row ^ k) * per_block + p]
         outs[k][:, pl.ds(per_block * width, width)] = pieces[0][:, pl.ds(0, width)]
-
-
-def inverse_kernel(peers, *refs):
-    inner_refs = refs[:2]
-    exact_ref, noise_ref, innovation_ref, inverse_ref, change_ref, weight = refs[2:]
-    row = lax.axis_index("row")
+        outs[k][:, pl.ds((per_block + 1) * width, share)] = rest[row ^ k].astype(BF16)
+
+
+def inverse_kernel(*refs):
+    inner_refs, (noise_ref, innovation_ref, inverse_ref, weight_ref) = refs[:2], refs[2:]
     overall = inverse_ref.shape[0]
-    measures, width = exact_ref.shape
     inner = inner_refs[0][...] + inner_refs[1][...]
     down = lax.broadcasted_iota(jnp.int32, (overall, overall), 0)
     across = lax.broadcasted_iota(jnp.int32, (overall, overall), 1)
@@ -361,66 +366,96 @@
         left = jnp.dot(inverse, inner, precision=FULL, preferred_element_type=F32)
         inverse = 2.0 * inverse - jnp.dot(left, inverse, precision=FULL, preferred_element_type=F32)
     inverse_ref[...] = inverse
-    weight[...] = jnp.sum(inverse * innovation_ref[...], axis=1, keepdims=True)
-    mine = weight[pl.ds(pl.multiple_of(row * measures, measures), measures), :]
-    change = jnp.sum(exact_ref[...] * mine, axis=0, keepdims=True)
-    part = width // peers
-    for q in range(peers):
-        change_ref[row ^ q] = change[:, q * part : (q + 1) * part]
-
-
-def merge_kernel(*refs):
-    pieces, half_ref, right_ref = refs[:-2], refs[-2], refs[-1]
+    weight_ref[...] = jnp.sum(inverse * innovation_ref[...], axis=1, keepdims=True)
+
+
+def merge_kernel(weight_ref, *refs):
+    pieces, (half_ref, right_ref, change_ref) = refs[:-3], refs[-3:]
     me = lax.axis_index("row")
+    peers = len(pieces)
     measures = pieces[0].shape[0]
     span, width = half_ref.shape[1], right_ref.shape[1]
+    share = width // peers
+    total = jnp.zeros((measures, share), F32)
     for k, piece in enumerate(pieces):
         at = pl.multiple_of((me ^ k) * measures, measures)
         half_ref[pl.ds(at, measures), :] = piece[:, pl.ds(0, span)]
-        right_ref[pl.ds(at, measures), :] = piece[:, pl.ds(span, width)]
-
-
-def update_kernel(mine_ref, other_ref, right_ref, inverse_ref, *refs):
-    kept, (cov_ref, out_ref, left, staged) = refs[:-4], refs[-4:]
-    step = pl.program_id(0)
-    depth, width = out_ref.shape
-    height = left.shape[1]
-
-    @pl.when(step == 0)
-    def _():
-        core = lax.axis_index("col") % 2
-        for p in range(height // (2 * width)):
-            part = pl.ds(p * width, width)
-            here = mine_ref[:, part].astype(F32)
-            there = other_ref[:, part].astype(F32)
-            staged[:, pl.ds(2 * p * width, width)] = jnp.where(core == 0, here, there)
-            staged[:, pl.ds((2 * p + 1) * width, width)] = jnp.where(core == 0, there, here)
+        right = piece[:, pl.ds(span, width)]
+        right_ref[pl.ds(at, measures), :] = right
+        right = right.astype(F32)
+        exact = piece[:, pl.ds(span + width, share)].astype(F32)
+        for q in range(peers):
+            exact = exact + jnp.where(me == q, right[:, q * share : (q + 1) * share], 0.0)
+        total = total + weight_ref[pl.ds(at, measures), :] * exact
+    change_ref[...] = jnp.sum(total, axis=0, keepdims=True)
+
+
+def update_kernel(depth, weights_ref, moved_ref, *refs):
+    mine_ref, other_ref, right_ref, inverse_ref = refs[:4]
+    kept, (cov_ref, weights_new_ref, out_ref) = refs[4:-11], refs[-11:-8]
+    numerator, left, fresh, done, loaded, sems, fixed, fixed_sem = refs[-8:]
+    height, width = cov_ref.shape
+    skipped = height - fresh.shape[0]
+    size = kept[0].shape[0]
+    copies = loads(
+        cov_ref,
+        skipped,
+        [fresh.at[pl.ds(at, size), :] for at in range(0, height - skipped, size)],
+        loaded,
+    )
+    for copy in copies:
+        copy.start()
+    fixed[...] = weights_ref[...] + moved_ref[0, :]
+    fix = pltpu.make_async_copy(fixed, weights_new_ref, fixed_sem)
+    fix.start()
+    core = lax.axis_index("col") % 2
+    for p in range(height // (2 * width)):
+        part = pl.ds(p * width, width)
+        here, there = mine_ref[:, part], other_ref[:, part]
+        numerator[:, pl.ds(2 * p * width, width)] = jnp.where(core == 0, here, there)
+        numerator[:, pl.ds((2 * p + 1) * width, width)] = jnp.where(core == 0, there, here)
+    slots = done.shape[0]
+
+    def leave(slot, at):
+        return pltpu.make_async_copy(
+            done.at[slot], out_ref.at[pl.ds(at, depth), :], sems.at[slot]
+        )
+
+    parts = [(part, 0, None) for part in kept]
+    parts += [(fresh, k * size, copy) for k, copy in enumerate(copies)]
+    for k, (part, base, copy) in enumerate(parts):
         left[...] = lax.dot_general(
             inverse_ref[...],
-            staged[...],
+            numerator[:, pl.ds(k * size, size)].astype(F32),
             (((0,), (0,)), ((), ())),
             precision=FULL,
             preferred_element_type=F32,
         ).astype(BF16)
-
-    gain = left[:, pl.ds(pl.multiple_of(step * depth, depth), depth)]
-    change = lax.dot_general(
-        gain, right_ref[...], (((0,), (0,)), ((), ())), preferred_element_type=F32
-    )
-    first = 0
-    for part in kept:
-        held = part.shape[0] // depth
-
-        @pl.when((step >= first) & (step < first + held))
-        def _(part=part, first=first):
-            at = pl.multiple_of((step - first) * depth, depth)
-            out_ref[...] = part[pl.ds(at, depth), :] - change
-
-        first += held
-
-    @pl.when(step >= first)
-    def _():
-        out_ref[...] = cov_ref[...] - change
+        if copy is not None:
+            copy.wait()
+
+        def tile(i, carry, k=k, part=part, base=base):
+            at = pl.multiple_of(i * depth, depth)
+            gain = left[:, pl.ds(at, depth)]
+            count = i + k * (size // depth)
+            slot = lax.rem(count, slots)
+
+            @pl.when(count >= slots)
+            def _():
+                leave(slot, 0).wait()
+
+            for start in range(0, width, CUT):
+                cut = pl.ds(start, min(CUT, width - start))
+                done[slot, :, cut] = part[pl.ds(base + at, depth), cut] - lax.dot_general(
+                    gain, right_ref[:, cut], (((0,), (0,)), ((), ())), preferred_element_type=F32
+                )
+            leave(slot, pl.multiple_of(k * size + at, depth)).start()
+            return carry
+
+        lax.fori_loop(0, size // depth, tile, 0)
+    for slot in range(slots):
+        leave(slot, 0).wait()
+    fix.wait()
 
 
 def on_device(
@@ -567,56 +602,63 @@
     span = height // 2
     *routed, inner = pl.pallas_call(
         functools.partial(route_kernel, rows, width),
-        out_shape=[shape((measures, span + width), BF16)] * rows + [shape((overall, overall))],
-        in_specs=[VMEM] * (cols // 2),
+        out_shape=[shape((measures, span + width + part), BF16)] * rows
+        + [shape((overall, overall))],
+        in_specs=[VMEM] * (1 + cols // 2),
         out_specs=[VMEM] * (rows + 1),
-        scratch_shapes=[pltpu.VMEM((cols // 2, measures, width), BF16)],
+        scratch_shapes=[
+            pltpu.VMEM((cols // 2, measures, width), BF16),
+            pltpu.VMEM((rows, measures, part), F32),
+        ],
         compiler_params=params(3),
         name="route",
-    )(*sents)
+    )(exact, *sents)
     routed = exchange(routed)
     shared = swap(inner, "col", 1)
-    inverse, change = pl.pallas_call(
-        functools.partial(inverse_kernel, rows),
-        out_shape=[shape((overall, overall)), shape((rows, 1, part))],
-        in_specs=[VMEM] * 5,
+    inverse, weight = pl.pallas_call(
+        inverse_kernel,
+        out_shape=[shape((overall, overall)), shape((overall, 1))],
+        in_specs=[VMEM] * 4,
         out_specs=[VMEM] * 2,
-        scratch_shapes=[pltpu.VMEM((overall, 1), F32)],
         compiler_params=params(3),
         name="inverse",
-    )(inner, shared, exact, noise_variance[None, :], innovation[None, :])
-    half, right = pl.pallas_call(
+    )(inner, shared, noise_variance[None, :], innovation[None, :])
+    half, right, change = pl.pallas_call(
         merge_kernel,
-        out_shape=[shape((overall, span), BF16), shape((overall, width), BF16)],
-        in_specs=[VMEM] * rows,
-        out_specs=[VMEM] * 2,
+        out_shape=[
+            shape((overall, span), BF16),
+            shape((overall, width), BF16),
+            shape((1, part)),
+        ],
+        in_specs=[VMEM] * (1 + rows),
+        out_specs=[VMEM] * 3,
         compiler_params=params(3),
         name="merge",
-    )(*routed)
+    )(weight, *routed)
     other = swap(half, "col", 1)
-    weights_new = weights
-    for k in range(rows):
-        pairs = [
-            (r * cols + c, c * rows + (r ^ k)) for r in range(rows) for c in range(cols)
-        ]
-        moved = lax.ppermute(change, ("row", "col"), pairs)
-        weights_new = weights_new + moved[k, 0]
-    skipped = (early + later) * each
-    cov_new = pl.pallas_call(
-        update_kernel,
-        out_shape=shape((height, width)),
-        grid=(tiles,),
-        in_specs=[VMEM] * (4 + early + later)
-        + [pl.BlockSpec((depth, width), lambda i: (jnp.maximum(i, skipped), 0))],
-        out_specs=pl.BlockSpec((depth, width), lambda i: (i, 0)),
+    pairs = [(r * cols + c, c * rows + r) for r in range(rows) for c in range(cols)]
+    moved = lax.ppermute(change, ("row", "col"), pairs)
+    size = each * depth
+    fresh = height - len(kept) * size
+    weights_new, cov_new = pl.pallas_call(
+        functools.partial(update_kernel, THIN),
+        out_shape=[shape((part,)), shape((height, width))],
+        in_specs=[VMEM] * (6 + len(kept)) + [ANY],
+        out_specs=[ANY, ANY],
         scratch_shapes=[
             pltpu.VMEM((overall, height), BF16),
-            pltpu.VMEM((overall, height), F32),
+            pltpu.VMEM((overall, size), BF16),
+            pltpu.VMEM((fresh, width), F32),
+            pltpu.VMEM((SLOTS, THIN, width), F32),
+            dma((fresh // size,)),
+            dma((SLOTS,)),
+            pltpu.VMEM((part,), F32),
+            dma,
         ],
-        compiler_params=params(14),
+        compiler_params=params(15),
         cost_estimate=estimate(2 * overall * height * width, 4 * height * width),
         name="update",
-    )(half, other, right, inverse, *map(keep, kept), outside(cov))
+    )(weights, moved, half, other, right, inverse, *map(keep, kept), outside(cov))
     return (weights_new, cov_new)
 
 

time: 132 us -> 112 us (0.85)
  Pallas kernels: 58.3 us -> 46.3 us
  starting transfers between devices: 37 us -> 30.9 us
    pallas_call x2, Pallas kernels: 29.7 us -> 18.3 us  [the longest x1 16.4 us: on_device(): pl.pallas_call(functools.partial(update_kernel, THIN), out_shape=[shape((...]
    ppermute x4 -> x1, starting transfers between devices: 7.49 us -> 2.23 us  [on_device(): moved = lax.ppermute(change, ('row', 'col'), pairs)]
    ppermute x4 -> x1, waiting for transfers between devices: 10.8 us -> 6.84 us  [on_device(): moved = lax.ppermute(change, ('row', 'col'), pairs)]
    ppermute x31, waiting for transfers between devices: 23.8 us -> 27.1 us  [swap(): return lax.ppermute(block, axis, [(i, i ^ step) for i in range(n)])]
  transfers between devices with their start and end apart: 35 -> 32, of which waited for: 13 -> 14; matrix products, arithmetic and copies ran while one was open for 1% -> 0% of each run, Pallas kernels for 12% -> 16%
where the time goes in v1:
time: 112 us
  Pallas kernels  46.3 us (41%)
  waiting for transfers between devices  33.9 us (30%)
  starting transfers between devices  30.9 us (28%)
    ppermute x31, starting transfers between devices, swap(): return lax.ppermute(block, axis, [(i, i ^ step) for i in range(n)])  28.7 us
    ppermute x31, waiting for transfers between devices, swap(): return lax.ppermute(block, axis, [(i, i ^ step) for i in range(n)])  27.1 us
    pallas_call x1, Pallas kernels, on_device(): pl.pallas_call(functools.partial(update_kernel, THIN), out_shape=[shape((...  16.4 us
    pallas_call x1, Pallas kernels, on_device(): pl.pallas_call(functools.partial(product_last_kernel, rows, depth, rest),...  7.28 us
    pallas_call x1, Pallas kernels, on_device(): pl.pallas_call(functools.partial(counts_kernel, 0), out_shape=[shape((ato...  7.06 us
    ppermute x1, waiting for transfers between devices, on_device(): moved = lax.ppermute(change, ('row', 'col'), pairs)  6.84 us
    pallas_call x2, Pallas kernels, on_device(): pl.pallas_call(functools.partial(jacobian_kernel, cols, rows, width_in, s...  6.44 us
    pallas_call x1, Pallas kernels, on_device(): pl.pallas_call(functools.partial(product_first_kernel, rows, depth), out_...  5.43 us
  transfers between devices with their start and end apart: 32, of which 14 were waited for; matrix products, arithmetic and copies ran while one was open for 0% of the time, Pallas kernels for 16%

profile of v1, /device:TPU:6, one launch (start us, length us, event | category | flops | bytes accessed | tf_op | source)
XLA Modules:
  0.0 112.1 jit_solution(13733752034369379985)
XLA Ops:
  0.6 1.1 pack.1
  1.8 3.7 %collective-permute-start.5 = (bf16[2,64,384]{2,1,0:T(8,128)(2,1)S(1)}, bf16[2,64,384]{2,1,0:T(8,128)(2,1)S(1)}, u32[]{:S(2)}, u32[]{:S(2)}) collective-permute-start(bf16[2,64,384]{2,1,0:T(8,128)(2,1)S(1)} %get-tuple-element.42.refs_4_.refs_8_), channel_id=1, source_target_pairs={{0,6},{1,7},{2,4},{3,5},{4,2},{5,3},{6,0},{7,1},{8,14},{9,15},{10,... | collective-permute-start | bytes 294920 | tf_op jit(solution)/shard_map/ppermute | solution.py:30
  5.4 0.0 collective-permute-start.3
  5.4 0.8 collective-permute-start.1
  6.2 0.0 collective-permute-start
  6.2 2.9 %collective-permute-done.5.refs_10_.refs_14_ = bf16[2,64,384]{2,1,0:T(8,128)(2,1)S(1)} collective-permute-done((bf16[2,64,384]{2,1,0:T(8,128)(2,1)S(1)}, bf16[2,64,384]{2,1,0:T(8,128)(2,1)S(1)}, u32[]{:S(2)}, u32[]{:S(2)}) %collective-permute-start.5) | collective-permute-done | bytes 98336 | tf_op jit(solution)/shard_map/ppermute | solution.py:30
  9.1 0.0 collective-permute-start.6
  9.1 4.6 %collective-permute-done.3.refs_8_.refs_12_ = bf16[2,64,384]{2,1,0:T(8,128)(2,1)S(1)} collective-permute-done((bf16[2,64,384]{2,1,0:T(8,128)(2,1)S(1)}, bf16[2,64,384]{2,1,0:T(8,128)(2,1)S(1)}, u32[]{:S(2)}, u32[]{:S(2)}) %collective-permute-start.3) | collective-permute-done | bytes 98336 | tf_op jit(solution)/shard_map/ppermute | solution.py:30
  13.7 0.0 collective-permute-start.4
  13.7 0.0 collective-permute-done.1.refs_6_.refs_10_
  13.7 0.5 collective-permute-start.2
  14.2 7.1 %counts.1 = (bf16[512,128]{1,0:T(8,128)(2,1)S(1)}, f32[768,2304]{1,0:T(8,128)S(1)}, f32[768,2304]{1,0:T(8,128)S(1)}, f32[768,2304]{1,0:T(8,128)S(1)}) custom-call(s32[2,64,138]{2,1,0:T(8,128)S(1)} %get-tuple-element.37.near_ref, f32[4608,2304]{1,0:T(8,128)} %refs_9_.1), custom_call_target="tpu_custom_call" | custom-call | flops 3000000000 | bytes 21233664 | tf_op jit(solution)/shard_map/counts/pallas_call | solution.py:514
  21.3 0.0 collective-permute-done.refs_5_.refs_9_
  21.3 0.0 collective-permute-done.6.refs_11_.refs_15_
  21.3 0.4 adjoint.1.refs_0_
  21.7 2.6 %collective-permute-start.12 = (f32[144,128]{1,0:T(8,128)S(1)}, f32[144,128]{1,0:T(8,128)S(1)}, u32[]{:S(2)}, u32[]{:S(2)}) collective-permute-start(f32[144,128]{1,0:T(8,128)S(1)} %adjoint.1.refs_0_), channel_id=1, source_target_pairs={{0,6},{1,7},{2,4},{3,5},{4,2},{5,3},{6,0},{7,1},{8,14},{9,15},{10,... | collective-permute-start | bytes 221192 | tf_op jit(solution)/shard_map/ppermute | solution.py:30
  24.3 0.0 collective-permute-start.10
  24.3 1.9 %collective-permute-start.8 = (f32[144,128]{1,0:T(8,128)S(1)}, f32[144,128]{1,0:T(8,128)S(1)}, u32[]{:S(2)}, u32[]{:S(2)}) collective-permute-start(f32[144,128]{1,0:T(8,128)S(1)} %adjoint.1.refs_0_), channel_id=1, source_target_pairs={{0,2},{1,3},{2,0},{3,1},{4,6},{5,7},{6,4},{7,5},{8,10},{9,11},{10,... | collective-permute-start | bytes 221192 | tf_op jit(solution)/shard_map/ppermute | solution.py:30
  26.1 2.5 %collective-permute-done.12.refs_6_ = f32[144,128]{1,0:T(8,128)S(1)} collective-permute-done((f32[144,128]{1,0:T(8,128)S(1)}, f32[144,128]{1,0:T(8,128)S(1)}, u32[]{:S(2)}, u32[]{:S(2)}) %collective-permute-start.12) | collective-permute-done | bytes 73760 | tf_op jit(solution)/shard_map/ppermute | solution.py:30
  28.6 0.0 collective-permute-start.13
  28.6 2.3 %collective-permute-done.10.refs_4_ = f32[144,128]{1,0:T(8,128)S(1)} collective-permute-done((f32[144,128]{1,0:T(8,128)S(1)}, f32[144,128]{1,0:T(8,128)S(1)}, u32[]{:S(2)}, u32[]{:S(2)}) %collective-permute-start.10) | collective-permute-done | bytes 73760 | tf_op jit(solution)/shard_map/ppermute | solution.py:30
  30.9 0.0 collective-permute-start.11
  30.9 0.0 collective-permute-done.8.refs_2_
  30.9 0.5 collective-permute-start.9
  31.4 0.7 collective-permute-done.11.refs_5_
  32.2 0.2 collective-permute-done.9.refs_3_
  32.3 3.0 %jacobian_first.1 = (bf16[16,2304]{1,0:T(8,128)(2,1)S(1)}, bf16[16,2304]{1,0:T(8,128)(2,1)S(1)}, bf16[16,2304]{1,0:T(8,128)(2,1)S(1)}, bf16[16,2304]{1,0:T(8,128)(2,1)S(1)}, f32[768,2304]{1,0:T(8,128)S(1)}) custom-call(f32[144,128]{1,0:T(8,128)S(1)} %adjoint.1.refs_0_, f32[144,128]{1,0:T(8,128)S(1)} %collective-permute-done.7.refs_1_, ...), custom_call_target="tpu_custom_call" | custom-call | flops 3000000000 | bytes 7077888 | tf_op jit(solution)/shard_map/jacobian_first/pallas_call | solution.py:542
  35.3 0.6 collective-permute-start.17
  35.9 0.5 collective-permute-start.18
  36.4 2.4 %collective-permute-start.19 = (bf16[16,2304]{1,0:T(8,128)(2,1)S(1)}, bf16[16,2304]{1,0:T(8,128)(2,1)S(1)}, u32[]{:S(2)}, u32[]{:S(2)}) collective-permute-start(bf16[16,2304]{1,0:T(8,128)(2,1)S(1)} %get-tuple-element.50), channel_id=1, source_target_pairs={{0,24},{8,16},{16,8},{24,0},{1,25},{9,17},{17,9},{25,1},{2,26},{10... | collective-permute-start | bytes 221192 | tf_op jit(solution)/shard_map/ppermute | solution.py:30
  38.9 3.4 %jacobian_last.1 = (bf16[16,4608]{1,0:T(8,128)(2,1)S(1)}, bf16[16,4608]{1,0:T(8,128)(2,1)S(1)}, bf16[16,4608]{1,0:T(8,128)(2,1)S(1)}, bf16[16,4608]{1,0:T(8,128)(2,1)S(1)}, f32[768,2304]{1,0:T(8,128)S(1)}) custom-call(f32[144,128]{1,0:T(8,128)S(1)} %adjoint.1.refs_0_, f32[144,128]{1,0:T(8,128)S(1)} %collective-permute-done.7.refs_1_, ...), custom_call_target="tpu_custom_call" | custom-call | flops 3000000000 | bytes 7077888 | tf_op jit(solution)/shard_map/jacobian_last/pallas_call | solution.py:542
  42.3 0.6 collective-permute-start.14
  42.9 0.5 collective-permute-start.15
  43.4 0.0 collective-permute-done.17.refs_1_
  43.4 2.4 %collective-permute-start.16 = (bf16[16,4608]{1,0:T(8,128)(2,1)S(1)}, bf16[16,4608]{1,0:T(8,128)(2,1)S(1)}, u32[]{:S(2)}, u32[]{:S(2)}) collective-permute-start(bf16[16,4608]{1,0:T(8,128)(2,1)S(1)} %get-tuple-element.46), channel_id=1, source_target_pairs={{0,24},{8,16},{16,8},{24,0},{1,25},{9,17},{17,9},{25,1},{2,26},{10... | collective-permute-start | bytes 442376 | tf_op jit(solution)/shard_map/ppermute | solution.py:30
  45.9 0.0 collective-permute-done.19.refs_3_
  45.9 5.4 %product_first.1.refs_4_ = f32[64,2304]{1,0:T(8,128)S(1)} custom-call(bf16[16,2304]{1,0:T(8,128)(2,1)S(1)} %get-tuple-element.47.refs_0_, bf16[16,2304]{1,0:T(8,128)(2,1)S(1)} %collective-permute-done.17.refs_1_, bf16[16,2304]{1,0:T(8,128)(2,1)S(1)} %collective-permute-done.18.refs_2_, bf16[16,2304]{1,0:T(8,128)(2,1)S(1)} %collective-permute-done.19.refs_3_, ...), custom_call_target="tpu_custom_call" | custom-call | flops 2717908992 | bytes 21233664 | tf_op jit(solution)/shard_map/product_first/pallas_call | solution.py:562
  51.3 0.0 collective-permute-done.15.refs_2_
  51.4 0.0 copy-start.1
  51.4 0.0 copy-start.2
  51.4 0.0 copy-start
  51.4 7.3 %product_last.1 = (f32[16,2560]{1,0:T(8,128)S(1)}, f32[16,2560]{1,0:T(8,128)S(1)}, f32[16,2560]{1,0:T(8,128)S(1)}, f32[16,2560]{1,0:T(8,128)S(1)}) custom-call(bf16[16,4608]{1,0:T(8,128)(2,1)S(1)} %get-tuple-element.43.refs_0_, bf16[16,4608]{1,0:T(8,128)(2,1)S(1)} %collective-permute-done.14.refs_1_, bf16[16,4608]{1,0:T(8,128)(2,1)S(1)} %collective-permute-done.15.refs_2_, ...), custom_call_target="tpu_custom_call" | custom-call | flops 2717908992 | bytes 21233664 | tf_op jit(solution)/shard_map/product_last/pallas_call | solution.py:573
  58.7 1.2 %collective-permute-start.20 = (f32[16,2560]{1,0:T(8,128)S(1)}, f32[16,2560]{1,0:T(8,128)S(1)}, u32[]{:S(2)}, u32[]{:S(2)}) collective-permute-start(f32[16,2560]{1,0:T(8,128)S(1)} %get-tuple-element.57), channel_id=1, source_target_pairs={{0,8},{8,0},{16,24},{24,16},{1,9},{9,1},{17,25},{25,17},{2,10},{10... | collective-permute-start | bytes 491528 | tf_op jit(solution)/shard_map/ppermute | solution.py:30
  59.9 0.7 collective-permute-start.21
  60.6 1.7 %collective-permute-start.22 = (f32[16,2560]{1,0:T(8,128)S(1)}, f32[16,2560]{1,0:T(8,128)S(1)}, u32[]{:S(2)}, u32[]{:S(2)}) collective-permute-start(f32[16,2560]{1,0:T(8,128)S(1)} %get-tuple-element.59), channel_id=1, source_target_pairs={{0,24},{8,16},{16,8},{24,0},{1,25},{9,17},{17,9},{25,1},{2,26},{10... | collective-permute-start | bytes 491528 | tf_op jit(solution)/shard_map/ppermute | solution.py:30
  62.2 3.0 %collective-permute-done.20.refs_1_ = f32[16,2560]{1,0:T(8,128)S(1)} collective-permute-done((f32[16,2560]{1,0:T(8,128)S(1)}, f32[16,2560]{1,0:T(8,128)S(1)}, u32[]{:S(2)}, u32[]{:S(2)}) %collective-permute-start.20) | collective-permute-done | bytes 163872 | tf_op jit(solution)/shard_map/ppermute | solution.py:30
  65.3 2.5 %collective-permute-done.21.refs_2_ = f32[16,2560]{1,0:T(8,128)S(1)} collective-permute-done((f32[16,2560]{1,0:T(8,128)S(1)}, f32[16,2560]{1,0:T(8,128)S(1)}, u32[]{:S(2)}, u32[]{:S(2)}) %collective-permute-start.21) | collective-permute-done | bytes 163872 | tf_op jit(solution)/shard_map/ppermute | solution.py:30
  67.8 2.6 %collective-permute-start.25 = (bf16[16,2816]{1,0:T(8,128)(2,1)S(1)}, bf16[16,2816]{1,0:T(8,128)(2,1)S(1)}, u32[]{:S(2)}, u32[]{:S(2)}) collective-permute-start(bf16[16,2816]{1,0:T(8,128)(2,1)S(1)} %get-tuple-element.61.refs_0_), channel_id=1, source_target_pairs={{0,6},{1,7},{2,4},{3,5},{4,2},{5,3},{6,0},{7,1},{8,14},{9,15},{10,... | collective-permute-start | bytes 270344 | tf_op jit(solution)/shard_map/ppermute | solution.py:30
  70.4 1.9 %collective-permute-start.23 = (bf16[16,2816]{1,0:T(8,128)(2,1)S(1)}, bf16[16,2816]{1,0:T(8,128)(2,1)S(1)}, u32[]{:S(2)}, u32[]{:S(2)}) collective-permute-start(bf16[16,2816]{1,0:T(8,128)(2,1)S(1)} %get-tuple-element.61.refs_0_), channel_id=1, source_target_pairs={{0,2},{1,3},{2,0},{3,1},{4,6},{5,7},{6,4},{7,5},{8,10},{9,11},{10,... | collective-permute-start | bytes 270344 | tf_op jit(solution)/shard_map/ppermute | solution.py:30
  72.3 1.9 %collective-permute-done.25.refs_3_ = bf16[16,2816]{1,0:T(8,128)(2,1)S(1)} collective-permute-done((bf16[16,2816]{1,0:T(8,128)(2,1)S(1)}, bf16[16,2816]{1,0:T(8,128)(2,1)S(1)}, u32[]{:S(2)}, u32[]{:S(2)}) %collective-permute-start.25) | collective-permute-done | bytes 90144 | tf_op jit(solution)/shard_map/ppermute | solution.py:30
  74.2 1.9 %collective-permute-done.24.refs_2_ = bf16[16,2816]{1,0:T(8,128)(2,1)S(1)} collective-permute-done((bf16[16,2816]{1,0:T(8,128)(2,1)S(1)}, bf16[16,2816]{1,0:T(8,128)(2,1)S(1)}, u32[]{:S(2)}, u32[]{:S(2)}) %collective-permute-start.24) | collective-permute-done | bytes 90144 | tf_op jit(solution)/shard_map/ppermute | solution.py:30
  76.1 0.1 route.1
  76.3 1.4 %collective-permute-start.27 = (bf16[16,5184]{1,0:T(8,128)(2,1)S(1)}, bf16[16,5184]{1,0:T(8,128)(2,1)S(1)}, u32[]{:S(2)}, u32[]{:S(2)}) collective-permute-start(bf16[16,5184]{1,0:T(8,128)(2,1)S(1)} %get-tuple-element.65), channel_id=1, source_target_pairs={{0,8},{8,0},{16,24},{24,16},{1,9},{9,1},{17,25},{25,17},{2,10},{10... | collective-permute-start | bytes 497672 | tf_op jit(solution)/shard_map/ppermute | solution.py:30
  77.7 1.0 collective-permute-start.28
  78.6 1.2 %collective-permute-start.29 = (bf16[16,5184]{1,0:T(8,128)(2,1)S(1)}, bf16[16,5184]{1,0:T(8,128)(2,1)S(1)}, u32[]{:S(2)}, u32[]{:S(2)}) collective-permute-start(bf16[16,5184]{1,0:T(8,128)(2,1)S(1)} %get-tuple-element.67), channel_id=1, source_target_pairs={{0,24},{8,16},{16,8},{24,0},{1,25},{9,17},{17,9},{25,1},{2,26},{10... | collective-permute-start | bytes 497672 | tf_op jit(solution)/shard_map/ppermute | solution.py:30
  79.8 1.2 %collective-permute-done.26.refs_1_ = f32[64,64]{1,0:T(8,128)S(1)} collective-permute-done((f32[64,64]{1,0:T(8,128)S(1)}, f32[64,64]{1,0:T(8,128)S(1)}, u32[]{:S(2)}, u32[]{:S(2)}) %collective-permute-start.26) | collective-permute-done | bytes 16416 | tf_op jit(solution)/shard_map/ppermute | solution.py:30
  81.0 1.8 %inverse.1 = (f32[64,64]{1,0:T(8,128)S(1)}, f32[64,1]{1,0:T(8,128)S(1)}) custom-call(f32[64,64]{1,0:T(8,128)S(1)} %get-tuple-element.62.refs_0_, f32[64,64]{1,0:T(8,128)S(1)} %collective-permute-done.26.refs_1_, f32[1,64]{1,0:T(1,128)S(1)} %bitcast.2, f32[1,64]{1,0:T(1,128)S(1)} %bitcast.3), custom_call_target="tpu_custom_call" | custom-call | tf_op jit(solution)/shard_map/inverse/pallas_call | solution.py:618
  82.8 0.5 collective-permute-done.27.refs_1_
  83.4 2.8 %collective-permute-done.28.refs_2_ = bf16[16,5184]{1,0:T(8,128)(2,1)S(1)} collective-permute-done((bf16[16,5184]{1,0:T(8,128)(2,1)S(1)}, bf16[16,5184]{1,0:T(8,128)(2,1)S(1)}, u32[]{:S(2)}, u32[]{:S(2)}) %collective-permute-start.28) | collective-permute-done | bytes 165920 | tf_op jit(solution)/shard_map/ppermute | solution.py:30
  86.2 0.2 merge.1
  86.4 0.1 collective-permute-start.31
  86.4 2.2 %collective-permute-start.30 = (f32[1,576]{1,0:T(1,128)S(1)}, f32[1,576]{1,0:T(1,128)S(1)}, u32[]{:S(2)}, u32[]{:S(2)}) collective-permute-start(f32[1,576]{1,0:T(1,128)S(1)} %get-tuple-element.68), channel_id=1, source_target_pairs={{0,0},{1,4},{2,8},{3,12},{4,16},{5,20},{6,24},{7,28},{8,1},{9,5},{... | collective-permute-start | bytes 6920 | tf_op jit(solution)/shard_map/ppermute | solution.py:640
  88.7 6.8 %collective-permute-done.30.moved_ref = f32[1,576]{1,0:T(1,128)S(1)} collective-permute-done((f32[1,576]{1,0:T(1,128)S(1)}, f32[1,576]{1,0:T(1,128)S(1)}, u32[]{:S(2)}, u32[]{:S(2)}) %collective-permute-start.30) | collective-permute-done | bytes 2336 | tf_op jit(solution)/shard_map/ppermute | solution.py:640
  95.5 16.4 %update.1 = (f32[576]{0:T(1024)}, f32[4608,2304]{1,0:T(8,128)}) custom-call(f32[576]{0:T(1024)S(1)} %copy-done, f32[1,576]{1,0:T(1,128)S(1)} %collective-permute-done.30.moved_ref, bf16[64,2304]{1,0:T(8,128)(2,1)S(1)} %get-tuple-element.69.refs_0_, bf16[64,2304]{1,0:T(8,128)(2,1)S(1)} %collective-permute-done.31.refs_1_, ...), custom_call_target="tpu_custom_call" | custom-call | flops 1358954496 | bytes 42467328 | tf_op jit(solution)/shard_map/update/pallas_call | solution.py:643
  (18 shorter events, 0.1 us)
Async XLA Ops:
  1.8 7.4 %collective-permute-start.5 = (bf16[2,64,384]{2,1,0:T(8,128)(2,1)S(1)}, bf16[2,64,384]{2,1,0:T(8,128)(2,1)S(1)}, u32[]{:S(2)}, u32[]{:S(2)}) collective-permute-start(bf16[2,64,384]{2,1,0:T(8,128)(2,1)S(1)} %get-tuple-element.42.refs_4_.refs_8_), channel_id=1, source_target_pairs={{0,6},{1,7},{2,4},{3,5},{4,2},{5,3},{6,0},{7,1},{8,14},{9,15},{10,... | collective-permute-start | bytes 294920 | tf_op jit(solution)/shard_map/ppermute | solution.py:30
  5.4 8.3 %collective-permute-start.3 = (bf16[2,64,384]{2,1,0:T(8,128)(2,1)S(1)}, bf16[2,64,384]{2,1,0:T(8,128)(2,1)S(1)}, u32[]{:S(2)}, u32[]{:S(2)}) collective-permute-start(bf16[2,64,384]{2,1,0:T(8,128)(2,1)S(1)} %get-tuple-element.42.refs_4_.refs_8_), channel_id=1, source_target_pairs={{0,4},{1,5},{2,6},{3,7},{4,0},{5,1},{6,2},{7,3},{8,12},{9,13},{10,... | collective-permute-start | bytes 294920 | tf_op jit(solution)/shard_map/ppermute | solution.py:30
  5.4 8.3 %collective-permute-start.1 = (bf16[2,64,384]{2,1,0:T(8,128)(2,1)S(1)}, bf16[2,64,384]{2,1,0:T(8,128)(2,1)S(1)}, u32[]{:S(2)}, u32[]{:S(2)}) collective-permute-start(bf16[2,64,384]{2,1,0:T(8,128)(2,1)S(1)} %get-tuple-element.42.refs_4_.refs_8_), channel_id=1, source_target_pairs={{0,2},{1,3},{2,0},{3,1},{4,6},{5,7},{6,4},{7,5},{8,10},{9,11},{10,... | collective-permute-start | bytes 294920 | tf_op jit(solution)/shard_map/ppermute | solution.py:30
  6.2 15.1 %collective-permute-start = (bf16[2,64,384]{2,1,0:T(8,128)(2,1)S(1)}, bf16[2,64,384]{2,1,0:T(8,128)(2,1)S(1)}, u32[]{:S(2)}, u32[]{:S(2)}) collective-permute-start(bf16[2,64,384]{2,1,0:T(8,128)(2,1)S(1)} %get-tuple-element.42.refs_4_.refs_8_), channel_id=1, source_target_pairs={{0,1},{1,0},{2,3},{3,2},{4,5},{5,4},{6,7},{7,6},{8,9},{9,8},{10,11... | collective-permute-start | bytes 294920 | tf_op jit(solution)/shard_map/ppermute | solution.py:30
  9.1 12.2 %collective-permute-start.6 = (bf16[2,64,384]{2,1,0:T(8,128)(2,1)S(1)}, bf16[2,64,384]{2,1,0:T(8,128)(2,1)S(1)}, u32[]{:S(2)}, u32[]{:S(2)}) collective-permute-start(bf16[2,64,384]{2,1,0:T(8,128)(2,1)S(1)} %collective-permute-done.5.refs_10_.refs_14_), channel_id=1, source_target_pairs={{0,1},{1,0},{2,3},{3,2},{4,5},{5,4},{6,7},{7,6},{8,9},{9,8},{10,11... | collective-permute-start | bytes 294920 | tf_op jit(solution)/shard_map/ppermute | solution.py:30
  13.7 7.6 %collective-permute-start.4 = (bf16[2,64,384]{2,1,0:T(8,128)(2,1)S(1)}, bf16[2,64,384]{2,1,0:T(8,128)(2,1)S(1)}, u32[]{:S(2)}, u32[]{:S(2)}) collective-permute-start(bf16[2,64,384]{2,1,0:T(8,128)(2,1)S(1)} %collective-permute-done.3.refs_8_.refs_12_), channel_id=1, source_target_pairs={{0,1},{1,0},{2,3},{3,2},{4,5},{5,4},{6,7},{7,6},{8,9},{9,8},{10,11... | collective-permute-start | bytes 294920 | tf_op jit(solution)/shard_map/ppermute | solution.py:30
  13.7 7.6 %collective-permute-start.2 = (bf16[2,64,384]{2,1,0:T(8,128)(2,1)S(1)}, bf16[2,64,384]{2,1,0:T(8,128)(2,1)S(1)}, u32[]{:S(2)}, u32[]{:S(2)}) collective-permute-start(bf16[2,64,384]{2,1,0:T(8,128)(2,1)S(1)} %collective-permute-done.1.refs_6_.refs_10_), channel_id=1, source_target_pairs={{0,1},{1,0},{2,3},{3,2},{4,5},{5,4},{6,7},{7,6},{8,9},{9,8},{10,11... | collective-permute-start | bytes 294920 | tf_op jit(solution)/shard_map/ppermute | solution.py:30
  21.7 6.9 %collective-permute-start.12 = (f32[144,128]{1,0:T(8,128)S(1)}, f32[144,128]{1,0:T(8,128)S(1)}, u32[]{:S(2)}, u32[]{:S(2)}) collective-permute-start(f32[144,128]{1,0:T(8,128)S(1)} %adjoint.1.refs_0_), channel_id=1, source_target_pairs={{0,6},{1,7},{2,4},{3,5},{4,2},{5,3},{6,0},{7,1},{8,14},{9,15},{10,... | collective-permute-start | bytes 221192 | tf_op jit(solution)/shard_map/ppermute | solution.py:30
  24.3 6.6 %collective-permute-start.10 = (f32[144,128]{1,0:T(8,128)S(1)}, f32[144,128]{1,0:T(8,128)S(1)}, u32[]{:S(2)}, u32[]{:S(2)}) collective-permute-start(f32[144,128]{1,0:T(8,128)S(1)} %adjoint.1.refs_0_), channel_id=1, source_target_pairs={{0,4},{1,5},{2,6},{3,7},{4,0},{5,1},{6,2},{7,3},{8,12},{9,13},{10,... | collective-permute-start | bytes 221192 | tf_op jit(solution)/shard_map/ppermute | solution.py:30
  24.3 6.6 %collective-permute-start.8 = (f32[144,128]{1,0:T(8,128)S(1)}, f32[144,128]{1,0:T(8,128)S(1)}, u32[]{:S(2)}, u32[]{:S(2)}) collective-permute-start(f32[144,128]{1,0:T(8,128)S(1)} %adjoint.1.refs_0_), channel_id=1, source_target_pairs={{0,2},{1,3},{2,0},{3,1},{4,6},{5,7},{6,4},{7,5},{8,10},{9,11},{10,... | collective-permute-start | bytes 221192 | tf_op jit(solution)/shard_map/ppermute | solution.py:30
  26.1 5.3 %collective-permute-start.7 = (f32[144,128]{1,0:T(8,128)S(1)}, f32[144,128]{1,0:T(8,128)S(1)}, u32[]{:S(2)}, u32[]{:S(2)}) collective-permute-start(f32[144,128]{1,0:T(8,128)S(1)} %adjoint.1.refs_0_), channel_id=1, source_target_pairs={{0,1},{1,0},{2,3},{3,2},{4,5},{5,4},{6,7},{7,6},{8,9},{9,8},{10,11... | collective-permute-start | bytes 221192 | tf_op jit(solution)/shard_map/ppermute | solution.py:30
  28.6 2.8 %collective-permute-start.13 = (f32[144,128]{1,0:T(8,128)S(1)}, f32[144,128]{1,0:T(8,128)S(1)}, u32[]{:S(2)}, u32[]{:S(2)}) collective-permute-start(f32[144,128]{1,0:T(8,128)S(1)} %collective-permute-done.12.refs_6_), channel_id=1, source_target_pairs={{0,1},{1,0},{2,3},{3,2},{4,5},{5,4},{6,7},{7,6},{8,9},{9,8},{10,11... | collective-permute-start | bytes 221192 | tf_op jit(solution)/shard_map/ppermute | solution.py:30
  30.9 1.3 %collective-permute-start.11 = (f32[144,128]{1,0:T(8,128)S(1)}, f32[144,128]{1,0:T(8,128)S(1)}, u32[]{:S(2)}, u32[]{:S(2)}) collective-permute-start(f32[144,128]{1,0:T(8,128)S(1)} %collective-permute-done.10.refs_4_), channel_id=1, source_target_pairs={{0,1},{1,0},{2,3},{3,2},{4,5},{5,4},{6,7},{7,6},{8,9},{9,8},{10,11... | collective-permute-start | bytes 221192 | tf_op jit(solution)/shard_map/ppermute | solution.py:30
  30.9 1.4 %collective-permute-start.9 = (f32[144,128]{1,0:T(8,128)S(1)}, f32[144,128]{1,0:T(8,128)S(1)}, u32[]{:S(2)}, u32[]{:S(2)}) collective-permute-start(f32[144,128]{1,0:T(8,128)S(1)} %collective-permute-done.8.refs_2_), channel_id=1, source_target_pairs={{0,1},{1,0},{2,3},{3,2},{4,5},{5,4},{6,7},{7,6},{8,9},{9,8},{10,11... | collective-permute-start | bytes 221192 | tf_op jit(solution)/shard_map/ppermute | solution.py:30
  35.3 8.1 %collective-permute-start.17 = (bf16[16,2304]{1,0:T(8,128)(2,1)S(1)}, bf16[16,2304]{1,0:T(8,128)(2,1)S(1)}, u32[]{:S(2)}, u32[]{:S(2)}) collective-permute-start(bf16[16,2304]{1,0:T(8,128)(2,1)S(1)} %get-tuple-element.48), channel_id=1, source_target_pairs={{0,8},{8,0},{16,24},{24,16},{1,9},{9,1},{17,25},{25,17},{2,10},{10... | collective-permute-start | bytes 221192 | tf_op jit(solution)/shard_map/ppermute | solution.py:30
  35.9 9.9 %collective-permute-start.18 = (bf16[16,2304]{1,0:T(8,128)(2,1)S(1)}, bf16[16,2304]{1,0:T(8,128)(2,1)S(1)}, u32[]{:S(2)}, u32[]{:S(2)}) collective-permute-start(bf16[16,2304]{1,0:T(8,128)(2,1)S(1)} %get-tuple-element.49), channel_id=1, source_target_pairs={{0,16},{8,24},{16,0},{24,8},{1,17},{9,25},{17,1},{25,9},{2,18},{10... | collective-permute-start | bytes 221192 | tf_op jit(solution)/shard_map/ppermute | solution.py:30
  36.4 9.4 %collective-permute-start.19 = (bf16[16,2304]{1,0:T(8,128)(2,1)S(1)}, bf16[16,2304]{1,0:T(8,128)(2,1)S(1)}, u32[]{:S(2)}, u32[]{:S(2)}) collective-permute-start(bf16[16,2304]{1,0:T(8,128)(2,1)S(1)} %get-tuple-element.50), channel_id=1, source_target_pairs={{0,24},{8,16},{16,8},{24,0},{1,25},{9,17},{17,9},{25,1},{2,26},{10... | collective-permute-start | bytes 221192 | tf_op jit(solution)/shard_map/ppermute | solution.py:30
  42.3 9.0 %collective-permute-start.14 = (bf16[16,4608]{1,0:T(8,128)(2,1)S(1)}, bf16[16,4608]{1,0:T(8,128)(2,1)S(1)}, u32[]{:S(2)}, u32[]{:S(2)}) collective-permute-start(bf16[16,4608]{1,0:T(8,128)(2,1)S(1)} %get-tuple-element.44), channel_id=1, source_target_pairs={{0,8},{8,0},{16,24},{24,16},{1,9},{9,1},{17,25},{25,17},{2,10},{10... | collective-permute-start | bytes 442376 | tf_op jit(solution)/shard_map/ppermute | solution.py:30
  42.9 8.4 %collective-permute-start.15 = (bf16[16,4608]{1,0:T(8,128)(2,1)S(1)}, bf16[16,4608]{1,0:T(8,128)(2,1)S(1)}, u32[]{:S(2)}, u32[]{:S(2)}) collective-permute-start(bf16[16,4608]{1,0:T(8,128)(2,1)S(1)} %get-tuple-element.45), channel_id=1, source_target_pairs={{0,16},{8,24},{16,0},{24,8},{1,17},{9,25},{17,1},{25,9},{2,18},{10... | collective-permute-start | bytes 442376 | tf_op jit(solution)/shard_map/ppermute | solution.py:30
  43.4 7.9 %collective-permute-start.16 = (bf16[16,4608]{1,0:T(8,128)(2,1)S(1)}, bf16[16,4608]{1,0:T(8,128)(2,1)S(1)}, u32[]{:S(2)}, u32[]{:S(2)}) collective-permute-start(bf16[16,4608]{1,0:T(8,128)(2,1)S(1)} %get-tuple-element.46), channel_id=1, source_target_pairs={{0,24},{8,16},{16,8},{24,0},{1,25},{9,17},{17,9},{25,1},{2,26},{10... | collective-permute-start | bytes 442376 | tf_op jit(solution)/shard_map/ppermute | solution.py:30
  51.4 29.7 %copy-start.1 = (f32[64]{0:T(128)S(1)}, f32[64]{0:T(128)}, u32[]{:S(2)}) copy-start(f32[64]{0:T(128)} %param.20) | copy-start | bytes 772
  51.4 29.6 %copy-start.2 = (f32[64]{0:T(128)S(1)}, f32[64]{0:T(128)}, u32[]{:S(2)}) copy-start(f32[64]{0:T(128)} %param.21) | copy-start | bytes 772
  51.4 44.1 %copy-start = (f32[576]{0:T(1024)S(1)}, f32[576]{0:T(1024)}, u32[]{:S(2)}) copy-start(f32[576]{0:T(1024)} %weights_ref.1) | copy-start | bytes 6916
  58.7 6.6 %collective-permute-start.20 = (f32[16,2560]{1,0:T(8,128)S(1)}, f32[16,2560]{1,0:T(8,128)S(1)}, u32[]{:S(2)}, u32[]{:S(2)}) collective-permute-start(f32[16,2560]{1,0:T(8,128)S(1)} %get-tuple-element.57), channel_id=1, source_target_pairs={{0,8},{8,0},{16,24},{24,16},{1,9},{9,1},{17,25},{25,17},{2,10},{10... | collective-permute-start | bytes 491528 | tf_op jit(solution)/shard_map/ppermute | solution.py:30
  59.9 7.8 %collective-permute-start.21 = (f32[16,2560]{1,0:T(8,128)S(1)}, f32[16,2560]{1,0:T(8,128)S(1)}, u32[]{:S(2)}, u32[]{:S(2)}) collective-permute-start(f32[16,2560]{1,0:T(8,128)S(1)} %get-tuple-element.58), channel_id=1, source_target_pairs={{0,16},{8,24},{16,0},{24,8},{1,17},{9,25},{17,1},{25,9},{2,18},{10... | collective-permute-start | bytes 491528 | tf_op jit(solution)/shard_map/ppermute | solution.py:30
  60.6 7.2 %collective-permute-start.22 = (f32[16,2560]{1,0:T(8,128)S(1)}, f32[16,2560]{1,0:T(8,128)S(1)}, u32[]{:S(2)}, u32[]{:S(2)}) collective-permute-start(f32[16,2560]{1,0:T(8,128)S(1)} %get-tuple-element.59), channel_id=1, source_target_pairs={{0,24},{8,16},{16,8},{24,0},{1,25},{9,17},{17,9},{25,1},{2,26},{10... | collective-permute-start | bytes 491528 | tf_op jit(solution)/shard_map/ppermute | solution.py:30
  67.8 6.4 %collective-permute-start.25 = (bf16[16,2816]{1,0:T(8,128)(2,1)S(1)}, bf16[16,2816]{1,0:T(8,128)(2,1)S(1)}, u32[]{:S(2)}, u32[]{:S(2)}) collective-permute-start(bf16[16,2816]{1,0:T(8,128)(2,1)S(1)} %get-tuple-element.61.refs_0_), channel_id=1, source_target_pairs={{0,6},{1,7},{2,4},{3,5},{4,2},{5,3},{6,0},{7,1},{8,14},{9,15},{10,... | collective-permute-start | bytes 270344 | tf_op jit(solution)/shard_map/ppermute | solution.py:30
  70.4 5.7 %collective-permute-start.24 = (bf16[16,2816]{1,0:T(8,128)(2,1)S(1)}, bf16[16,2816]{1,0:T(8,128)(2,1)S(1)}, u32[]{:S(2)}, u32[]{:S(2)}) collective-permute-start(bf16[16,2816]{1,0:T(8,128)(2,1)S(1)} %get-tuple-element.61.refs_0_), channel_id=1, source_target_pairs={{0,4},{1,5},{2,6},{3,7},{4,0},{5,1},{6,2},{7,3},{8,12},{9,13},{10,... | collective-permute-start | bytes 270344 | tf_op jit(solution)/shard_map/ppermute | solution.py:30
  70.4 5.7 %collective-permute-start.23 = (bf16[16,2816]{1,0:T(8,128)(2,1)S(1)}, bf16[16,2816]{1,0:T(8,128)(2,1)S(1)}, u32[]{:S(2)}, u32[]{:S(2)}) collective-permute-start(bf16[16,2816]{1,0:T(8,128)(2,1)S(1)} %get-tuple-element.61.refs_0_), channel_id=1, source_target_pairs={{0,2},{1,3},{2,0},{3,1},{4,6},{5,7},{6,4},{7,5},{8,10},{9,11},{10,... | collective-permute-start | bytes 270344 | tf_op jit(solution)/shard_map/ppermute | solution.py:30
  76.3 7.1 %collective-permute-start.27 = (bf16[16,5184]{1,0:T(8,128)(2,1)S(1)}, bf16[16,5184]{1,0:T(8,128)(2,1)S(1)}, u32[]{:S(2)}, u32[]{:S(2)}) collective-permute-start(bf16[16,5184]{1,0:T(8,128)(2,1)S(1)} %get-tuple-element.65), channel_id=1, source_target_pairs={{0,8},{8,0},{16,24},{24,16},{1,9},{9,1},{17,25},{25,17},{2,10},{10... | collective-permute-start | bytes 497672 | tf_op jit(solution)/shard_map/ppermute | solution.py:30
  77.7 8.5 %collective-permute-start.28 = (bf16[16,5184]{1,0:T(8,128)(2,1)S(1)}, bf16[16,5184]{1,0:T(8,128)(2,1)S(1)}, u32[]{:S(2)}, u32[]{:S(2)}) collective-permute-start(bf16[16,5184]{1,0:T(8,128)(2,1)S(1)} %get-tuple-element.66), channel_id=1, source_target_pairs={{0,16},{8,24},{16,0},{24,8},{1,17},{9,25},{17,1},{25,9},{2,18},{10... | collective-permute-start | bytes 497672 | tf_op jit(solution)/shard_map/ppermute | solution.py:30
  78.6 7.5 %collective-permute-start.29 = (bf16[16,5184]{1,0:T(8,128)(2,1)S(1)}, bf16[16,5184]{1,0:T(8,128)(2,1)S(1)}, u32[]{:S(2)}, u32[]{:S(2)}) collective-permute-start(bf16[16,5184]{1,0:T(8,128)(2,1)S(1)} %get-tuple-element.67), channel_id=1, source_target_pairs={{0,24},{8,16},{16,8},{24,0},{1,25},{9,17},{17,9},{25,1},{2,26},{10... | collective-permute-start | bytes 497672 | tf_op jit(solution)/shard_map/ppermute | solution.py:30
  79.8 1.2 %collective-permute-start.26 = (f32[64,64]{1,0:T(8,128)S(1)}, f32[64,64]{1,0:T(8,128)S(1)}, u32[]{:S(2)}, u32[]{:S(2)}) collective-permute-start(f32[64,64]{1,0:T(8,128)S(1)} %get-tuple-element.62.refs_0_), channel_id=1, source_target_pairs={{0,1},{1,0},{2,3},{3,2},{4,5},{5,4},{6,7},{7,6},{8,9},{9,8},{10,11... | collective-permute-start | bytes 49160 | tf_op jit(solution)/shard_map/ppermute | solution.py:30
  86.4 9.2 %collective-permute-start.31 = (bf16[64,2304]{1,0:T(8,128)(2,1)S(1)}, bf16[64,2304]{1,0:T(8,128)(2,1)S(1)}, u32[]{:S(2)}, u32[]{:S(2)}) collective-permute-start(bf16[64,2304]{1,0:T(8,128)(2,1)S(1)} %get-tuple-element.69.refs_0_), channel_id=1, source_target_pairs={{0,1},{1,0},{2,3},{3,2},{4,5},{5,4},{6,7},{7,6},{8,9},{9,8},{10,11... | collective-permute-start | bytes 884744 | tf_op jit(solution)/shard_map/ppermute | solution.py:30
  86.4 9.1 %collective-permute-start.30 = (f32[1,576]{1,0:T(1,128)S(1)}, f32[1,576]{1,0:T(1,128)S(1)}, u32[]{:S(2)}, u32[]{:S(2)}) collective-permute-start(f32[1,576]{1,0:T(1,128)S(1)} %get-tuple-element.68), channel_id=1, source_target_pairs={{0,0},{1,4},{2,8},{3,12},{4,16},{5,20},{6,24},{7,28},{8,1},{9,5},{... | collective-permute-start | bytes 6920 | tf_op jit(solution)/shard_map/ppermute | solution.py:640

commit v2 on v1

--- a/solution.py
+++ b/solution.py
@@ -16,7 +16,7 @@
 EACH = (3, 2, 1)
 EARLY, LATER = 3, 2
 CUT = 768
-THIN, SLOTS = 128, 4
+THIN, SLOTS = 128, 6
 
 VMEM = pl.BlockSpec(memory_space=pltpu.VMEM)
 SMEM = pl.BlockSpec(memory_space=pltpu.SMEM)
@@ -310,34 +310,38 @@
         )
 
 
-def sum_kernel(*refs):
-    parts, (exact_ref, sent_ref) = refs[:-2], refs[-2:]
-    width = exact_ref.shape[1]
+def sum_kernel(peers, *refs):
+    parts, sent_ref, outs, rest = refs[:peers], refs[peers], refs[peers + 1 : -1], refs[-1]
+    row = lax.axis_index("row")
+    share = rest.shape[2]
+    width = share * peers
     total = parts[0][...]
     for part in parts[1:]:
         total = total + part[...]
-    exact_ref[...] = total[:, :width]
-    sent_ref[:, pl.ds(0, width)] = total[:, :width].astype(BF16)
+    exact = total[:, :width]
+    right = exact.astype(BF16)
+    low = exact - right.astype(F32)
+    for q in range(peers):
+        rest[q] = low[:, q * share : (q + 1) * share]
+    sent_ref[:, pl.ds(0, width)] = right
     inner = total[:, width:]
     high = inner.astype(BF16)
     sent_ref[:, pl.ds(width, inner.shape[1])] = high
     sent_ref[:, pl.ds(width + inner.shape[1], inner.shape[1])] = (
         inner - high.astype(F32)
     ).astype(BF16)
-
-
-def route_kernel(peers, width, exact_ref, *refs):
-    pieces, outs, (inner_ref, held, rest) = refs[: -peers - 3], refs[-peers - 3 : -3], refs[-3:]
+    for k, out in enumerate(outs):
+        out[:, pl.ds(0, width)] = right
+        out[:, pl.ds(width, share)] = rest[row ^ k].astype(BF16)
+
+
+def route_kernel(peers, width, *refs):
+    pieces, outs, inner_ref, held = refs[: -peers - 2], refs[-peers - 2 : -2], refs[-2], refs[-1]
     row, col = lax.axis_index("row"), lax.axis_index("col")
     count = len(pieces)
     per_block = count // peers
-    measures, _ = exact_ref.shape
+    measures = pieces[0].shape[0]
     overall = inner_ref.shape[0]
-    share = width // peers
-    exact = exact_ref[...]
-    low = exact - exact.astype(BF16).astype(F32)
-    for q in range(peers):
-        rest[q] = low[:, q * share : (q + 1) * share]
     total = jnp.zeros((measures, overall * peers), F32)
     for k, piece in enumerate(pieces):
         held[(col // 2) ^ k] = piece[:, pl.ds(0, width)]
@@ -348,8 +352,6 @@
     for k in range(peers):
         for p in range(per_block):
             outs[k][:, pl.ds(p * width, width)] = held[(row ^ k) * per_block + p]
-        outs[k][:, pl.ds(per_block * width, width)] = pieces[0][:, pl.ds(0, width)]
-        outs[k][:, pl.ds((per_block + 1) * width, share)] = rest[row ^ k].astype(BF16)
 
 
 def inverse_kernel(*refs):
@@ -369,21 +371,20 @@
     weight_ref[...] = jnp.sum(inverse * innovation_ref[...], axis=1, keepdims=True)
 
 
-def merge_kernel(weight_ref, *refs):
-    pieces, (half_ref, right_ref, change_ref) = refs[:-3], refs[-3:]
+def merge_kernel(peers, weight_ref, *refs):
+    pieces, blocks = refs[:peers], refs[peers : 2 * peers]
+    half_ref, right_ref, change_ref = refs[2 * peers :]
     me = lax.axis_index("row")
-    peers = len(pieces)
+    width = right_ref.shape[1]
+    share = width // peers
     measures = pieces[0].shape[0]
-    span, width = half_ref.shape[1], right_ref.shape[1]
-    share = width // peers
+    arrange(half_ref, pieces, 0, half_ref.shape[1])
+    arrange(right_ref, blocks, 0, width)
     total = jnp.zeros((measures, share), F32)
-    for k, piece in enumerate(pieces):
+    for k, block in enumerate(blocks):
         at = pl.multiple_of((me ^ k) * measures, measures)
-        half_ref[pl.ds(at, measures), :] = piece[:, pl.ds(0, span)]
-        right = piece[:, pl.ds(span, width)]
-        right_ref[pl.ds(at, measures), :] = right
-        right = right.astype(F32)
-        exact = piece[:, pl.ds(span + width, share)].astype(F32)
+        right = block[:, pl.ds(0, width)].astype(F32)
+        exact = block[:, pl.ds(width, share)].astype(F32)
         for q in range(peers):
             exact = exact + jnp.where(me == q, right[:, q * share : (q + 1) * share], 0.0)
         total = total + weight_ref[pl.ds(at, measures), :] * exact
@@ -587,32 +588,28 @@
         name="product_last",
     )(*jacs[1], begun, *map(keep, kept[first:]), outside(cov))
     parts = exchange(parts)
-    exact, sent = pl.pallas_call(
-        sum_kernel,
-        out_shape=[
-            shape((measures, width)),
-            shape((measures, width + 2 * overall * rows), BF16),
-        ],
+    sent, *blocks = pl.pallas_call(
+        functools.partial(sum_kernel, rows),
+        out_shape=[shape((measures, width + 2 * overall * rows), BF16)]
+        + [shape((measures, width + part), BF16)] * rows,
         in_specs=[VMEM] * rows,
-        out_specs=[VMEM] * 2,
+        out_specs=[VMEM] * (rows + 1),
+        scratch_shapes=[pltpu.VMEM((rows, measures, part), F32)],
         compiler_params=params(3),
         name="sum",
     )(*parts)
     sents = gather_apart(sent)
+    blocks = exchange(blocks)
     span = height // 2
     *routed, inner = pl.pallas_call(
         functools.partial(route_kernel, rows, width),
-        out_shape=[shape((measures, span + width + part), BF16)] * rows
-        + [shape((overall, overall))],
-        in_specs=[VMEM] * (1 + cols // 2),
+        out_shape=[shape((measures, span), BF16)] * rows + [shape((overall, overall))],
+        in_specs=[VMEM] * (cols // 2),
         out_specs=[VMEM] * (rows + 1),
-        scratch_shapes=[
-            pltpu.VMEM((cols // 2, measures, width), BF16),
-            pltpu.VMEM((rows, measures, part), F32),
-        ],
+        scratch_shapes=[pltpu.VMEM((cols // 2, measures, width), BF16)],
         compiler_params=params(3),
         name="route",
-    )(exact, *sents)
+    )(*sents)
     routed = exchange(routed)
     shared = swap(inner, "col", 1)
     inverse, weight = pl.pallas_call(
@@ -624,17 +621,17 @@
         name="inverse",
     )(inner, shared, noise_variance[None, :], innovation[None, :])
     half, right, change = pl.pallas_call(
-        merge_kernel,
+        functools.partial(merge_kernel, rows),
         out_shape=[
             shape((overall, span), BF16),
             shape((overall, width), BF16),
             shape((1, part)),
         ],
-        in_specs=[VMEM] * (1 + rows),
+        in_specs=[VMEM] * (1 + 2 * rows),
         out_specs=[VMEM] * 3,
         compiler_params=params(3),
         name="merge",
-    )(weight, *routed)
+    )(weight, *routed, *blocks)
     other = swap(half, "col", 1)
     pairs = [(r * cols + c, c * rows + r) for r in range(rows) for c in range(cols)]
     moved = lax.ppermute(change, ("row", "col"), pairs)

time: 112 us -> 109 us (0.973)
  waiting for transfers between devices: 33.9 us -> 26.2 us
  starting transfers between devices: 30.9 us -> 36.4 us
    ppermute x31 -> x34, waiting for transfers between devices: 27.1 us -> 21.3 us  [swap(): return lax.ppermute(block, axis, [(i, i ^ step) for i in range(n)])]
    ppermute x31 -> x34, starting transfers between devices: 28.7 us -> 32.2 us  [swap(): return lax.ppermute(block, axis, [(i, i ^ step) for i in range(n)])]
    ppermute x1, waiting for transfers between devices: 6.84 us -> 4.93 us  [on_device(): moved = lax.ppermute(change, ('row', 'col'), pairs)]
    ppermute x1, starting transfers between devices: 2.23 us -> 4.14 us  [on_device(): moved = lax.ppermute(change, ('row', 'col'), pairs)]
  transfers between devices with their start and end apart: 32 -> 35, of which waited for: 14 -> 12; matrix products, arithmetic and copies ran while one was open for 0% -> 0% of each run, Pallas kernels for 16% -> 16%
where the time goes in v2:
time: 109 us
  Pallas kernels  45.6 us (42%)
  starting transfers between devices  36.4 us (33%)
  waiting for transfers between devices  26.2 us (24%)
    ppermute x34, starting transfers between devices, swap(): return lax.ppermute(block, axis, [(i, i ^ step) for i in range(n)])  32.2 us
    ppermute x34, waiting for transfers between devices, swap(): return lax.ppermute(block, axis, [(i, i ^ step) for i in range(n)])  21.3 us
    pallas_call x1, Pallas kernels, on_device(): pl.pallas_call(functools.partial(update_kernel, THIN), out_shape=[shape((...  15.7 us
    pallas_call x1, Pallas kernels, on_device(): pl.pallas_call(functools.partial(product_last_kernel, rows, depth, rest),...  7.28 us
    pallas_call x1, Pallas kernels, on_device(): pl.pallas_call(functools.partial(counts_kernel, 0), out_shape=[shape((ato...  7.06 us
    pallas_call x2, Pallas kernels, on_device(): pl.pallas_call(functools.partial(jacobian_kernel, cols, rows, width_in, s...  6.44 us
    pallas_call x1, Pallas kernels, on_device(): pl.pallas_call(functools.partial(product_first_kernel, rows, depth), out_...  5.43 us
    ppermute x1, waiting for transfers between devices, on_device(): moved = lax.ppermute(change, ('row', 'col'), pairs)  4.93 us
  transfers between devices with their start and end apart: 35, of which 12 were waited for; matrix products, arithmetic and copies ran while one was open for 0% of the time, Pallas kernels for 16%

profile of v2, /device:TPU:6, one launch (start us, length us, event | category | flops | bytes accessed | tf_op | source)
XLA Modules:
  0.0 109.2 jit_solution(11807359151259419318)
XLA Ops:
  0.6 1.1 %pack.1 = (bf16[2,64,384]{2,1,0:T(8,128)(2,1)S(1)}, s32[2,64,138]{2,1,0:T(8,128)S(1)}, s32[2,64]{1,0:T(2,128)S(1)}, f32[2,128]{1,0:T(2,128)S(1)}, f32[16,128]{1,0:T(8,128)S(1)}) custom-call(bf16[2,64,128]{2,1,0:T(8,128)(2,1)} %up_ref.1, bf16[2,64,144]{2,1,0:T(8,128)(2,1)} %act_ref.1, s32[2,64,138]{2,1,0:T(8,128)} %neighbors_ref.1, s32[2,64]{1,0:T(2,128)} %types_ref.1, ...), custom_call_target="tpu_custom_call" | custom-call | tf_op jit(solution)/shard_map/pack/pallas_call | solution.py:493
  1.8 3.7 %collective-permute-start.5 = (bf16[2,64,384]{2,1,0:T(8,128)(2,1)S(1)}, bf16[2,64,384]{2,1,0:T(8,128)(2,1)S(1)}, u32[]{:S(2)}, u32[]{:S(2)}) collective-permute-start(bf16[2,64,384]{2,1,0:T(8,128)(2,1)S(1)} %get-tuple-element.45.refs_4_.refs_8_), channel_id=1, source_target_pairs={{0,6},{1,7},{2,4},{3,5},{4,2},{5,3},{6,0},{7,1},{8,14},{9,15},{10,... | collective-permute-start | bytes 294920 | tf_op jit(solution)/shard_map/ppermute | solution.py:30
  5.4 0.0 collective-permute-start.3
  5.4 0.8 collective-permute-start.1
  6.2 0.0 collective-permute-start
  6.2 2.9 %collective-permute-done.5.refs_10_.refs_14_ = bf16[2,64,384]{2,1,0:T(8,128)(2,1)S(1)} collective-permute-done((bf16[2,64,384]{2,1,0:T(8,128)(2,1)S(1)}, bf16[2,64,384]{2,1,0:T(8,128)(2,1)S(1)}, u32[]{:S(2)}, u32[]{:S(2)}) %collective-permute-start.5) | collective-permute-done | bytes 98336 | tf_op jit(solution)/shard_map/ppermute | solution.py:30
  9.1 0.0 collective-permute-start.6
  9.1 4.6 %collective-permute-done.3.refs_8_.refs_12_ = bf16[2,64,384]{2,1,0:T(8,128)(2,1)S(1)} collective-permute-done((bf16[2,64,384]{2,1,0:T(8,128)(2,1)S(1)}, bf16[2,64,384]{2,1,0:T(8,128)(2,1)S(1)}, u32[]{:S(2)}, u32[]{:S(2)}) %collective-permute-start.3) | collective-permute-done | bytes 98336 | tf_op jit(solution)/shard_map/ppermute | solution.py:30
  13.7 0.0 collective-permute-start.4
  13.7 0.0 collective-permute-done.1.refs_6_.refs_10_
  13.7 0.5 collective-permute-start.2
  14.2 7.1 %counts.1 = (bf16[512,128]{1,0:T(8,128)(2,1)S(1)}, f32[768,2304]{1,0:T(8,128)S(1)}, f32[768,2304]{1,0:T(8,128)S(1)}, f32[768,2304]{1,0:T(8,128)S(1)}) custom-call(s32[2,64,138]{2,1,0:T(8,128)S(1)} %get-tuple-element.40.near_ref, f32[4608,2304]{1,0:T(8,128)} %refs_9_.1), custom_call_target="tpu_custom_call" | custom-call | flops 3000000000 | bytes 21233664 | tf_op jit(solution)/shard_map/counts/pallas_call | solution.py:515
  21.3 0.0 collective-permute-done.refs_5_.refs_9_
  21.3 0.0 collective-permute-done.6.refs_11_.refs_15_
  21.3 0.4 adjoint.1.refs_0_
  21.7 2.6 %collective-permute-start.12 = (f32[144,128]{1,0:T(8,128)S(1)}, f32[144,128]{1,0:T(8,128)S(1)}, u32[]{:S(2)}, u32[]{:S(2)}) collective-permute-start(f32[144,128]{1,0:T(8,128)S(1)} %adjoint.1.refs_0_), channel_id=1, source_target_pairs={{0,6},{1,7},{2,4},{3,5},{4,2},{5,3},{6,0},{7,1},{8,14},{9,15},{10,... | collective-permute-start | bytes 221192 | tf_op jit(solution)/shard_map/ppermute | solution.py:30
  24.3 0.0 collective-permute-start.10
  24.3 1.9 %collective-permute-start.8 = (f32[144,128]{1,0:T(8,128)S(1)}, f32[144,128]{1,0:T(8,128)S(1)}, u32[]{:S(2)}, u32[]{:S(2)}) collective-permute-start(f32[144,128]{1,0:T(8,128)S(1)} %adjoint.1.refs_0_), channel_id=1, source_target_pairs={{0,2},{1,3},{2,0},{3,1},{4,6},{5,7},{6,4},{7,5},{8,10},{9,11},{10,... | collective-permute-start | bytes 221192 | tf_op jit(solution)/shard_map/ppermute | solution.py:30
  26.1 2.5 %collective-permute-done.12.refs_6_ = f32[144,128]{1,0:T(8,128)S(1)} collective-permute-done((f32[144,128]{1,0:T(8,128)S(1)}, f32[144,128]{1,0:T(8,128)S(1)}, u32[]{:S(2)}, u32[]{:S(2)}) %collective-permute-start.12) | collective-permute-done | bytes 73760 | tf_op jit(solution)/shard_map/ppermute | solution.py:30
  28.6 0.0 collective-permute-start.13
  28.6 2.3 %collective-permute-done.10.refs_4_ = f32[144,128]{1,0:T(8,128)S(1)} collective-permute-done((f32[144,128]{1,0:T(8,128)S(1)}, f32[144,128]{1,0:T(8,128)S(1)}, u32[]{:S(2)}, u32[]{:S(2)}) %collective-permute-start.10) | collective-permute-done | bytes 73760 | tf_op jit(solution)/shard_map/ppermute | solution.py:30
  30.9 0.0 collective-permute-start.11
  30.9 0.0 collective-permute-done.8.refs_2_
  30.9 0.5 collective-permute-start.9
  31.4 0.7 collective-permute-done.11.refs_5_
  32.2 0.2 collective-permute-done.9.refs_3_
  32.3 3.0 %jacobian_first.1 = (bf16[16,2304]{1,0:T(8,128)(2,1)S(1)}, bf16[16,2304]{1,0:T(8,128)(2,1)S(1)}, bf16[16,2304]{1,0:T(8,128)(2,1)S(1)}, bf16[16,2304]{1,0:T(8,128)(2,1)S(1)}, f32[768,2304]{1,0:T(8,128)S(1)}) custom-call(f32[144,128]{1,0:T(8,128)S(1)} %adjoint.1.refs_0_, f32[144,128]{1,0:T(8,128)S(1)} %collective-permute-done.7.refs_1_, ...), custom_call_target="tpu_custom_call" | custom-call | flops 3000000000 | bytes 7077888 | tf_op jit(solution)/shard_map/jacobian_first/pallas_call | solution.py:543
  35.3 0.6 collective-permute-start.17
  35.9 0.5 collective-permute-start.18
  36.4 2.4 %collective-permute-start.19 = (bf16[16,2304]{1,0:T(8,128)(2,1)S(1)}, bf16[16,2304]{1,0:T(8,128)(2,1)S(1)}, u32[]{:S(2)}, u32[]{:S(2)}) collective-permute-start(bf16[16,2304]{1,0:T(8,128)(2,1)S(1)} %get-tuple-element.53), channel_id=1, source_target_pairs={{0,24},{8,16},{16,8},{24,0},{1,25},{9,17},{17,9},{25,1},{2,26},{10... | collective-permute-start | bytes 221192 | tf_op jit(solution)/shard_map/ppermute | solution.py:30
  38.9 3.4 %jacobian_last.1 = (bf16[16,4608]{1,0:T(8,128)(2,1)S(1)}, bf16[16,4608]{1,0:T(8,128)(2,1)S(1)}, bf16[16,4608]{1,0:T(8,128)(2,1)S(1)}, bf16[16,4608]{1,0:T(8,128)(2,1)S(1)}, f32[768,2304]{1,0:T(8,128)S(1)}) custom-call(f32[144,128]{1,0:T(8,128)S(1)} %adjoint.1.refs_0_, f32[144,128]{1,0:T(8,128)S(1)} %collective-permute-done.7.refs_1_, ...), custom_call_target="tpu_custom_call" | custom-call | flops 3000000000 | bytes 7077888 | tf_op jit(solution)/shard_map/jacobian_last/pallas_call | solution.py:543
  42.3 0.6 collective-permute-start.14
  42.9 0.5 collective-permute-start.15
  43.4 2.4 %collective-permute-start.16 = (bf16[16,4608]{1,0:T(8,128)(2,1)S(1)}, bf16[16,4608]{1,0:T(8,128)(2,1)S(1)}, u32[]{:S(2)}, u32[]{:S(2)}) collective-permute-start(bf16[16,4608]{1,0:T(8,128)(2,1)S(1)} %get-tuple-element.49), channel_id=1, source_target_pairs={{0,24},{8,16},{16,8},{24,0},{1,25},{9,17},{17,9},{25,1},{2,26},{10... | collective-permute-start | bytes 442376 | tf_op jit(solution)/shard_map/ppermute | solution.py:30
  45.9 5.4 %product_first.1.refs_4_ = f32[64,2304]{1,0:T(8,128)S(1)} custom-call(bf16[16,2304]{1,0:T(8,128)(2,1)S(1)} %get-tuple-element.50.refs_0_, bf16[16,2304]{1,0:T(8,128)(2,1)S(1)} %collective-permute-done.17.refs_1_, bf16[16,2304]{1,0:T(8,128)(2,1)S(1)} %collective-permute-done.18.refs_2_, bf16[16,2304]{1,0:T(8,128)(2,1)S(1)} %collective-permute-done.19.refs_3_, ...), custom_call_target="tpu_custom_call" | custom-call | flops 2717908992 | bytes 21233664 | tf_op jit(solution)/shard_map/product_first/pallas_call | solution.py:563
  51.4 0.0 copy-start.1
  51.4 0.0 copy-start.2
  51.4 0.0 copy-start
  51.4 7.3 %product_last.1 = (f32[16,2560]{1,0:T(8,128)S(1)}, f32[16,2560]{1,0:T(8,128)S(1)}, f32[16,2560]{1,0:T(8,128)S(1)}, f32[16,2560]{1,0:T(8,128)S(1)}) custom-call(bf16[16,4608]{1,0:T(8,128)(2,1)S(1)} %get-tuple-element.46.refs_0_, bf16[16,4608]{1,0:T(8,128)(2,1)S(1)} %collective-permute-done.14.refs_1_, bf16[16,4608]{1,0:T(8,128)(2,1)S(1)} %collective-permute-done.15.refs_2_, ...), custom_call_target="tpu_custom_call" | custom-call | flops 2717908992 | bytes 21233664 | tf_op jit(solution)/shard_map/product_last/pallas_call | solution.py:574
  58.7 1.2 %collective-permute-start.20 = (f32[16,2560]{1,0:T(8,128)S(1)}, f32[16,2560]{1,0:T(8,128)S(1)}, u32[]{:S(2)}, u32[]{:S(2)}) collective-permute-start(f32[16,2560]{1,0:T(8,128)S(1)} %get-tuple-element.60), channel_id=1, source_target_pairs={{0,8},{8,0},{16,24},{24,16},{1,9},{9,1},{17,25},{25,17},{2,10},{10... | collective-permute-start | bytes 491528 | tf_op jit(solution)/shard_map/ppermute | solution.py:30
  59.9 0.7 collective-permute-start.21
  60.6 1.7 %collective-permute-start.22 = (f32[16,2560]{1,0:T(8,128)S(1)}, f32[16,2560]{1,0:T(8,128)S(1)}, u32[]{:S(2)}, u32[]{:S(2)}) collective-permute-start(f32[16,2560]{1,0:T(8,128)S(1)} %get-tuple-element.62), channel_id=1, source_target_pairs={{0,24},{8,16},{16,8},{24,0},{1,25},{9,17},{17,9},{25,1},{2,26},{10... | collective-permute-start | bytes 491528 | tf_op jit(solution)/shard_map/ppermute | solution.py:30
  62.2 3.0 %collective-permute-done.20.refs_1_ = f32[16,2560]{1,0:T(8,128)S(1)} collective-permute-done((f32[16,2560]{1,0:T(8,128)S(1)}, f32[16,2560]{1,0:T(8,128)S(1)}, u32[]{:S(2)}, u32[]{:S(2)}) %collective-permute-start.20) | collective-permute-done | bytes 163872 | tf_op jit(solution)/shard_map/ppermute | solution.py:30
  65.3 2.5 %collective-permute-done.21.refs_2_ = f32[16,2560]{1,0:T(8,128)S(1)} collective-permute-done((f32[16,2560]{1,0:T(8,128)S(1)}, f32[16,2560]{1,0:T(8,128)S(1)}, u32[]{:S(2)}, u32[]{:S(2)}) %collective-permute-start.21) | collective-permute-done | bytes 163872 | tf_op jit(solution)/shard_map/ppermute | solution.py:30
  67.8 0.1 sum.1
  67.9 2.6 %collective-permute-start.25 = (bf16[16,2816]{1,0:T(8,128)(2,1)S(1)}, bf16[16,2816]{1,0:T(8,128)(2,1)S(1)}, u32[]{:S(2)}, u32[]{:S(2)}) collective-permute-start(bf16[16,2816]{1,0:T(8,128)(2,1)S(1)} %get-tuple-element.63.refs_0_), channel_id=1, source_target_pairs={{0,6},{1,7},{2,4},{3,5},{4,2},{5,3},{6,0},{7,1},{8,14},{9,15},{10,... | collective-permute-start | bytes 270344 | tf_op jit(solution)/shard_map/ppermute | solution.py:30
  70.5 1.9 %collective-permute-start.23 = (bf16[16,2816]{1,0:T(8,128)(2,1)S(1)}, bf16[16,2816]{1,0:T(8,128)(2,1)S(1)}, u32[]{:S(2)}, u32[]{:S(2)}) collective-permute-start(bf16[16,2816]{1,0:T(8,128)(2,1)S(1)} %get-tuple-element.63.refs_0_), channel_id=1, source_target_pairs={{0,2},{1,3},{2,0},{3,1},{4,6},{5,7},{6,4},{7,5},{8,10},{9,11},{10,... | collective-permute-start | bytes 270344 | tf_op jit(solution)/shard_map/ppermute | solution.py:30
  72.3 1.1 %collective-permute-start.30 = (bf16[16,2880]{1,0:T(8,128)(2,1)S(1)}, bf16[16,2880]{1,0:T(8,128)(2,1)S(1)}, u32[]{:S(2)}, u32[]{:S(2)}) collective-permute-start(bf16[16,2880]{1,0:T(8,128)(2,1)S(1)} %get-tuple-element.71), channel_id=1, source_target_pairs={{0,8},{8,0},{16,24},{24,16},{1,9},{9,1},{17,25},{25,17},{2,10},{10... | collective-permute-start | bytes 276488 | tf_op jit(solution)/shard_map/ppermute | solution.py:30
  73.5 0.9 collective-permute-start.31
  74.4 1.5 %collective-permute-start.32 = (bf16[16,2880]{1,0:T(8,128)(2,1)S(1)}, bf16[16,2880]{1,0:T(8,128)(2,1)S(1)}, u32[]{:S(2)}, u32[]{:S(2)}) collective-permute-start(bf16[16,2880]{1,0:T(8,128)(2,1)S(1)} %get-tuple-element.73), channel_id=1, source_target_pairs={{0,24},{8,16},{16,8},{24,0},{1,25},{9,17},{17,9},{25,1},{2,26},{10... | collective-permute-start | bytes 276488 | tf_op jit(solution)/shard_map/ppermute | solution.py:30
  75.9 0.4 collective-permute-done.24.refs_2_
  76.2 0.1 route.1
  76.3 0.0 collective-permute-start.26
  76.4 1.4 %collective-permute-start.27 = (bf16[16,2304]{1,0:T(8,128)(2,1)S(1)}, bf16[16,2304]{1,0:T(8,128)(2,1)S(1)}, u32[]{:S(2)}, u32[]{:S(2)}) collective-permute-start(bf16[16,2304]{1,0:T(8,128)(2,1)S(1)} %get-tuple-element.67), channel_id=1, source_target_pairs={{0,8},{8,0},{16,24},{24,16},{1,9},{9,1},{17,25},{25,17},{2,10},{10... | collective-permute-start | bytes 221192 | tf_op jit(solution)/shard_map/ppermute | solution.py:30
  77.8 1.0 collective-permute-start.28
  78.8 1.2 %collective-permute-start.29 = (bf16[16,2304]{1,0:T(8,128)(2,1)S(1)}, bf16[16,2304]{1,0:T(8,128)(2,1)S(1)}, u32[]{:S(2)}, u32[]{:S(2)}) collective-permute-start(bf16[16,2304]{1,0:T(8,128)(2,1)S(1)} %get-tuple-element.69), channel_id=1, source_target_pairs={{0,24},{8,16},{16,8},{24,0},{1,25},{9,17},{17,9},{25,1},{2,26},{10... | collective-permute-start | bytes 221192 | tf_op jit(solution)/shard_map/ppermute | solution.py:30
  79.9 1.8 %inverse.1 = (f32[64,64]{1,0:T(8,128)S(1)}, f32[64,1]{1,0:T(8,128)S(1)}) custom-call(f32[64,64]{1,0:T(8,128)S(1)} %get-tuple-element.64.refs_0_, f32[64,64]{1,0:T(8,128)S(1)} %collective-permute-done.26.refs_1_, f32[1,64]{1,0:T(1,128)S(1)} %bitcast.2, f32[1,64]{1,0:T(1,128)S(1)} %bitcast.3), custom_call_target="tpu_custom_call" | custom-call | tf_op jit(solution)/shard_map/inverse/pallas_call | solution.py:615
  81.8 0.4 collective-permute-done.28.refs_2_
  82.1 1.9 %collective-permute-done.29.refs_3_ = bf16[16,2304]{1,0:T(8,128)(2,1)S(1)} collective-permute-done((bf16[16,2304]{1,0:T(8,128)(2,1)S(1)}, bf16[16,2304]{1,0:T(8,128)(2,1)S(1)}, u32[]{:S(2)}, u32[]{:S(2)}) %collective-permute-start.29) | collective-permute-done | bytes 73760 | tf_op jit(solution)/shard_map/ppermute | solution.py:30
  84.0 0.2 merge.1
  84.2 0.1 collective-permute-start.34
  84.3 4.1 %collective-permute-start.33 = (f32[1,576]{1,0:T(1,128)S(1)}, f32[1,576]{1,0:T(1,128)S(1)}, u32[]{:S(2)}, u32[]{:S(2)}) collective-permute-start(f32[1,576]{1,0:T(1,128)S(1)} %get-tuple-element.74), channel_id=1, source_target_pairs={{0,0},{1,4},{2,8},{3,12},{4,16},{5,20},{6,24},{7,28},{8,1},{9,5},{... | collective-permute-start | bytes 6920 | tf_op jit(solution)/shard_map/ppermute | solution.py:637
  88.4 4.9 %collective-permute-done.33.moved_ref = f32[1,576]{1,0:T(1,128)S(1)} collective-permute-done((f32[1,576]{1,0:T(1,128)S(1)}, f32[1,576]{1,0:T(1,128)S(1)}, u32[]{:S(2)}, u32[]{:S(2)}) %collective-permute-start.33) | collective-permute-done | bytes 2336 | tf_op jit(solution)/shard_map/ppermute | solution.py:637
  93.4 15.7 %update.1 = (f32[576]{0:T(1024)}, f32[4608,2304]{1,0:T(8,128)}) custom-call(f32[576]{0:T(1024)S(1)} %copy-done, f32[1,576]{1,0:T(1,128)S(1)} %collective-permute-done.33.moved_ref, bf16[64,2304]{1,0:T(8,128)(2,1)S(1)} %get-tuple-element.75.refs_0_, bf16[64,2304]{1,0:T(8,128)(2,1)S(1)} %collective-permute-done.34.refs_1_, ...), custom_call_target="tpu_custom_call" | custom-call | flops 1358954496 | bytes 42467328 | tf_op jit(solution)/shard_map/update/pallas_call | solution.py:640
  (24 shorter events, 0.1 us)
Async XLA Ops:
  1.8 7.4 %collective-permute-start.5 = (bf16[2,64,384]{2,1,0:T(8,128)(2,1)S(1)}, bf16[2,64,384]{2,1,0:T(8,128)(2,1)S(1)}, u32[]{:S(2)}, u32[]{:S(2)}) collective-permute-start(bf16[2,64,384]{2,1,0:T(8,128)(2,1)S(1)} %get-tuple-element.45.refs_4_.refs_8_), channel_id=1, source_target_pairs={{0,6},{1,7},{2,4},{3,5},{4,2},{5,3},{6,0},{7,1},{8,14},{9,15},{10,... | collective-permute-start | bytes 294920 | tf_op jit(solution)/shard_map/ppermute | solution.py:30
  5.4 8.3 %collective-permute-start.3 = (bf16[2,64,384]{2,1,0:T(8,128)(2,1)S(1)}, bf16[2,64,384]{2,1,0:T(8,128)(2,1)S(1)}, u32[]{:S(2)}, u32[]{:S(2)}) collective-permute-start(bf16[2,64,384]{2,1,0:T(8,128)(2,1)S(1)} %get-tuple-element.45.refs_4_.refs_8_), channel_id=1, source_target_pairs={{0,4},{1,5},{2,6},{3,7},{4,0},{5,1},{6,2},{7,3},{8,12},{9,13},{10,... | collective-permute-start | bytes 294920 | tf_op jit(solution)/shard_map/ppermute | solution.py:30
  5.4 8.3 %collective-permute-start.1 = (bf16[2,64,384]{2,1,0:T(8,128)(2,1)S(1)}, bf16[2,64,384]{2,1,0:T(8,128)(2,1)S(1)}, u32[]{:S(2)}, u32[]{:S(2)}) collective-permute-start(bf16[2,64,384]{2,1,0:T(8,128)(2,1)S(1)} %get-tuple-element.45.refs_4_.refs_8_), channel_id=1, source_target_pairs={{0,2},{1,3},{2,0},{3,1},{4,6},{5,7},{6,4},{7,5},{8,10},{9,11},{10,... | collective-permute-start | bytes 294920 | tf_op jit(solution)/shard_map/ppermute | solution.py:30
  6.2 15.1 %collective-permute-start = (bf16[2,64,384]{2,1,0:T(8,128)(2,1)S(1)}, bf16[2,64,384]{2,1,0:T(8,128)(2,1)S(1)}, u32[]{:S(2)}, u32[]{:S(2)}) collective-permute-start(bf16[2,64,384]{2,1,0:T(8,128)(2,1)S(1)} %get-tuple-element.45.refs_4_.refs_8_), channel_id=1, source_target_pairs={{0,1},{1,0},{2,3},{3,2},{4,5},{5,4},{6,7},{7,6},{8,9},{9,8},{10,11... | collective-permute-start | bytes 294920 | tf_op jit(solution)/shard_map/ppermute | solution.py:30
  9.1 12.2 %collective-permute-start.6 = (bf16[2,64,384]{2,1,0:T(8,128)(2,1)S(1)}, bf16[2,64,384]{2,1,0:T(8,128)(2,1)S(1)}, u32[]{:S(2)}, u32[]{:S(2)}) collective-permute-start(bf16[2,64,384]{2,1,0:T(8,128)(2,1)S(1)} %collective-permute-done.5.refs_10_.refs_14_), channel_id=1, source_target_pairs={{0,1},{1,0},{2,3},{3,2},{4,5},{5,4},{6,7},{7,6},{8,9},{9,8},{10,11... | collective-permute-start | bytes 294920 | tf_op jit(solution)/shard_map/ppermute | solution.py:30
  13.7 7.6 %collective-permute-start.4 = (bf16[2,64,384]{2,1,0:T(8,128)(2,1)S(1)}, bf16[2,64,384]{2,1,0:T(8,128)(2,1)S(1)}, u32[]{:S(2)}, u32[]{:S(2)}) collective-permute-start(bf16[2,64,384]{2,1,0:T(8,128)(2,1)S(1)} %collective-permute-done.3.refs_8_.refs_12_), channel_id=1, source_target_pairs={{0,1},{1,0},{2,3},{3,2},{4,5},{5,4},{6,7},{7,6},{8,9},{9,8},{10,11... | collective-permute-start | bytes 294920 | tf_op jit(solution)/shard_map/ppermute | solution.py:30
  13.7 7.6 %collective-permute-start.2 = (bf16[2,64,384]{2,1,0:T(8,128)(2,1)S(1)}, bf16[2,64,384]{2,1,0:T(8,128)(2,1)S(1)}, u32[]{:S(2)}, u32[]{:S(2)}) collective-permute-start(bf16[2,64,384]{2,1,0:T(8,128)(2,1)S(1)} %collective-permute-done.1.refs_6_.refs_10_), channel_id=1, source_target_pairs={{0,1},{1,0},{2,3},{3,2},{4,5},{5,4},{6,7},{7,6},{8,9},{9,8},{10,11... | collective-permute-start | bytes 294920 | tf_op jit(solution)/shard_map/ppermute | solution.py:30
  21.7 6.9 %collective-permute-start.12 = (f32[144,128]{1,0:T(8,128)S(1)}, f32[144,128]{1,0:T(8,128)S(1)}, u32[]{:S(2)}, u32[]{:S(2)}) collective-permute-start(f32[144,128]{1,0:T(8,128)S(1)} %adjoint.1.refs_0_), channel_id=1, source_target_pairs={{0,6},{1,7},{2,4},{3,5},{4,2},{5,3},{6,0},{7,1},{8,14},{9,15},{10,... | collective-permute-start | bytes 221192 | tf_op jit(solution)/shard_map/ppermute | solution.py:30
  24.3 6.6 %collective-permute-start.10 = (f32[144,128]{1,0:T(8,128)S(1)}, f32[144,128]{1,0:T(8,128)S(1)}, u32[]{:S(2)}, u32[]{:S(2)}) collective-permute-start(f32[144,128]{1,0:T(8,128)S(1)} %adjoint.1.refs_0_), channel_id=1, source_target_pairs={{0,4},{1,5},{2,6},{3,7},{4,0},{5,1},{6,2},{7,3},{8,12},{9,13},{10,... | collective-permute-start | bytes 221192 | tf_op jit(solution)/shard_map/ppermute | solution.py:30
  24.3 6.6 %collective-permute-start.8 = (f32[144,128]{1,0:T(8,128)S(1)}, f32[144,128]{1,0:T(8,128)S(1)}, u32[]{:S(2)}, u32[]{:S(2)}) collective-permute-start(f32[144,128]{1,0:T(8,128)S(1)} %adjoint.1.refs_0_), channel_id=1, source_target_pairs={{0,2},{1,3},{2,0},{3,1},{4,6},{5,7},{6,4},{7,5},{8,10},{9,11},{10,... | collective-permute-start | bytes 221192 | tf_op jit(solution)/shard_map/ppermute | solution.py:30
  26.1 5.3 %collective-permute-start.7 = (f32[144,128]{1,0:T(8,128)S(1)}, f32[144,128]{1,0:T(8,128)S(1)}, u32[]{:S(2)}, u32[]{:S(2)}) collective-permute-start(f32[144,128]{1,0:T(8,128)S(1)} %adjoint.1.refs_0_), channel_id=1, source_target_pairs={{0,1},{1,0},{2,3},{3,2},{4,5},{5,4},{6,7},{7,6},{8,9},{9,8},{10,11... | collective-permute-start | bytes 221192 | tf_op jit(solution)/shard_map/ppermute | solution.py:30
  28.6 2.8 %collective-permute-start.13 = (f32[144,128]{1,0:T(8,128)S(1)}, f32[144,128]{1,0:T(8,128)S(1)}, u32[]{:S(2)}, u32[]{:S(2)}) collective-permute-start(f32[144,128]{1,0:T(8,128)S(1)} %collective-permute-done.12.refs_6_), channel_id=1, source_target_pairs={{0,1},{1,0},{2,3},{3,2},{4,5},{5,4},{6,7},{7,6},{8,9},{9,8},{10,11... | collective-permute-start | bytes 221192 | tf_op jit(solution)/shard_map/ppermute | solution.py:30
  30.9 1.3 %collective-permute-start.11 = (f32[144,128]{1,0:T(8,128)S(1)}, f32[144,128]{1,0:T(8,128)S(1)}, u32[]{:S(2)}, u32[]{:S(2)}) collective-permute-start(f32[144,128]{1,0:T(8,128)S(1)} %collective-permute-done.10.refs_4_), channel_id=1, source_target_pairs={{0,1},{1,0},{2,3},{3,2},{4,5},{5,4},{6,7},{7,6},{8,9},{9,8},{10,11... | collective-permute-start | bytes 221192 | tf_op jit(solution)/shard_map/ppermute | solution.py:30
  30.9 1.4 %collective-permute-start.9 = (f32[144,128]{1,0:T(8,128)S(1)}, f32[144,128]{1,0:T(8,128)S(1)}, u32[]{:S(2)}, u32[]{:S(2)}) collective-permute-start(f32[144,128]{1,0:T(8,128)S(1)} %collective-permute-done.8.refs_2_), channel_id=1, source_target_pairs={{0,1},{1,0},{2,3},{3,2},{4,5},{5,4},{6,7},{7,6},{8,9},{9,8},{10,11... | collective-permute-start | bytes 221192 | tf_op jit(solution)/shard_map/ppermute | solution.py:30
  35.3 8.1 %collective-permute-start.17 = (bf16[16,2304]{1,0:T(8,128)(2,1)S(1)}, bf16[16,2304]{1,0:T(8,128)(2,1)S(1)}, u32[]{:S(2)}, u32[]{:S(2)}) collective-permute-start(bf16[16,2304]{1,0:T(8,128)(2,1)S(1)} %get-tuple-element.51), channel_id=1, source_target_pairs={{0,8},{8,0},{16,24},{24,16},{1,9},{9,1},{17,25},{25,17},{2,10},{10... | collective-permute-start | bytes 221192 | tf_op jit(solution)/shard_map/ppermute | solution.py:30
  35.9 9.9 %collective-permute-start.18 = (bf16[16,2304]{1,0:T(8,128)(2,1)S(1)}, bf16[16,2304]{1,0:T(8,128)(2,1)S(1)}, u32[]{:S(2)}, u32[]{:S(2)}) collective-permute-start(bf16[16,2304]{1,0:T(8,128)(2,1)S(1)} %get-tuple-element.52), channel_id=1, source_target_pairs={{0,16},{8,24},{16,0},{24,8},{1,17},{9,25},{17,1},{25,9},{2,18},{10... | collective-permute-start | bytes 221192 | tf_op jit(solution)/shard_map/ppermute | solution.py:30
  36.4 9.4 %collective-permute-start.19 = (bf16[16,2304]{1,0:T(8,128)(2,1)S(1)}, bf16[16,2304]{1,0:T(8,128)(2,1)S(1)}, u32[]{:S(2)}, u32[]{:S(2)}) collective-permute-start(bf16[16,2304]{1,0:T(8,128)(2,1)S(1)} %get-tuple-element.53), channel_id=1, source_target_pairs={{0,24},{8,16},{16,8},{24,0},{1,25},{9,17},{17,9},{25,1},{2,26},{10... | collective-permute-start | bytes 221192 | tf_op jit(solution)/shard_map/ppermute | solution.py:30
  42.3 9.0 %collective-permute-start.14 = (bf16[16,4608]{1,0:T(8,128)(2,1)S(1)}, bf16[16,4608]{1,0:T(8,128)(2,1)S(1)}, u32[]{:S(2)}, u32[]{:S(2)}) collective-permute-start(bf16[16,4608]{1,0:T(8,128)(2,1)S(1)} %get-tuple-element.47), channel_id=1, source_target_pairs={{0,8},{8,0},{16,24},{24,16},{1,9},{9,1},{17,25},{25,17},{2,10},{10... | collective-permute-start | bytes 442376 | tf_op jit(solution)/shard_map/ppermute | solution.py:30
  42.9 8.4 %collective-permute-start.15 = (bf16[16,4608]{1,0:T(8,128)(2,1)S(1)}, bf16[16,4608]{1,0:T(8,128)(2,1)S(1)}, u32[]{:S(2)}, u32[]{:S(2)}) collective-permute-start(bf16[16,4608]{1,0:T(8,128)(2,1)S(1)} %get-tuple-element.48), channel_id=1, source_target_pairs={{0,16},{8,24},{16,0},{24,8},{1,17},{9,25},{17,1},{25,9},{2,18},{10... | collective-permute-start | bytes 442376 | tf_op jit(solution)/shard_map/ppermute | solution.py:30
  43.4 7.9 %collective-permute-start.16 = (bf16[16,4608]{1,0:T(8,128)(2,1)S(1)}, bf16[16,4608]{1,0:T(8,128)(2,1)S(1)}, u32[]{:S(2)}, u32[]{:S(2)}) collective-permute-start(bf16[16,4608]{1,0:T(8,128)(2,1)S(1)} %get-tuple-element.49), channel_id=1, source_target_pairs={{0,24},{8,16},{16,8},{24,0},{1,25},{9,17},{17,9},{25,1},{2,26},{10... | collective-permute-start | bytes 442376 | tf_op jit(solution)/shard_map/ppermute | solution.py:30
  51.4 28.6 %copy-start.1 = (f32[64]{0:T(128)S(1)}, f32[64]{0:T(128)}, u32[]{:S(2)}) copy-start(f32[64]{0:T(128)} %param.20) | copy-start | bytes 772
  51.4 28.6 %copy-start.2 = (f32[64]{0:T(128)S(1)}, f32[64]{0:T(128)}, u32[]{:S(2)}) copy-start(f32[64]{0:T(128)} %param.21) | copy-start | bytes 772
  51.4 42.0 %copy-start = (f32[576]{0:T(1024)S(1)}, f32[576]{0:T(1024)}, u32[]{:S(2)}) copy-start(f32[576]{0:T(1024)} %weights_ref.1) | copy-start | bytes 6916
  58.7 6.6 %collective-permute-start.20 = (f32[16,2560]{1,0:T(8,128)S(1)}, f32[16,2560]{1,0:T(8,128)S(1)}, u32[]{:S(2)}, u32[]{:S(2)}) collective-permute-start(f32[16,2560]{1,0:T(8,128)S(1)} %get-tuple-element.60), channel_id=1, source_target_pairs={{0,8},{8,0},{16,24},{24,16},{1,9},{9,1},{17,25},{25,17},{2,10},{10... | collective-permute-start | bytes 491528 | tf_op jit(solution)/shard_map/ppermute | solution.py:30
  59.9 7.8 %collective-permute-start.21 = (f32[16,2560]{1,0:T(8,128)S(1)}, f32[16,2560]{1,0:T(8,128)S(1)}, u32[]{:S(2)}, u32[]{:S(2)}) collective-permute-start(f32[16,2560]{1,0:T(8,128)S(1)} %get-tuple-element.61), channel_id=1, source_target_pairs={{0,16},{8,24},{16,0},{24,8},{1,17},{9,25},{17,1},{25,9},{2,18},{10... | collective-permute-start | bytes 491528 | tf_op jit(solution)/shard_map/ppermute | solution.py:30
  60.6 7.2 %collective-permute-start.22 = (f32[16,2560]{1,0:T(8,128)S(1)}, f32[16,2560]{1,0:T(8,128)S(1)}, u32[]{:S(2)}, u32[]{:S(2)}) collective-permute-start(f32[16,2560]{1,0:T(8,128)S(1)} %get-tuple-element.62), channel_id=1, source_target_pairs={{0,24},{8,16},{16,8},{24,0},{1,25},{9,17},{17,9},{25,1},{2,26},{10... | collective-permute-start | bytes 491528 | tf_op jit(solution)/shard_map/ppermute | solution.py:30
  67.9 6.5 %collective-permute-start.25 = (bf16[16,2816]{1,0:T(8,128)(2,1)S(1)}, bf16[16,2816]{1,0:T(8,128)(2,1)S(1)}, u32[]{:S(2)}, u32[]{:S(2)}) collective-permute-start(bf16[16,2816]{1,0:T(8,128)(2,1)S(1)} %get-tuple-element.63.refs_0_), channel_id=1, source_target_pairs={{0,6},{1,7},{2,4},{3,5},{4,2},{5,3},{6,0},{7,1},{8,14},{9,15},{10,... | collective-permute-start | bytes 270344 | tf_op jit(solution)/shard_map/ppermute | solution.py:30
  70.5 5.7 %collective-permute-start.24 = (bf16[16,2816]{1,0:T(8,128)(2,1)S(1)}, bf16[16,2816]{1,0:T(8,128)(2,1)S(1)}, u32[]{:S(2)}, u32[]{:S(2)}) collective-permute-start(bf16[16,2816]{1,0:T(8,128)(2,1)S(1)} %get-tuple-element.63.refs_0_), channel_id=1, source_target_pairs={{0,4},{1,5},{2,6},{3,7},{4,0},{5,1},{6,2},{7,3},{8,12},{9,13},{10,... | collective-permute-start | bytes 270344 | tf_op jit(solution)/shard_map/ppermute | solution.py:30
  70.5 5.7 %collective-permute-start.23 = (bf16[16,2816]{1,0:T(8,128)(2,1)S(1)}, bf16[16,2816]{1,0:T(8,128)(2,1)S(1)}, u32[]{:S(2)}, u32[]{:S(2)}) collective-permute-start(bf16[16,2816]{1,0:T(8,128)(2,1)S(1)} %get-tuple-element.63.refs_0_), channel_id=1, source_target_pairs={{0,2},{1,3},{2,0},{3,1},{4,6},{5,7},{6,4},{7,5},{8,10},{9,11},{10,... | collective-permute-start | bytes 270344 | tf_op jit(solution)/shard_map/ppermute | solution.py:30
  72.3 5.4 %collective-permute-start.30 = (bf16[16,2880]{1,0:T(8,128)(2,1)S(1)}, bf16[16,2880]{1,0:T(8,128)(2,1)S(1)}, u32[]{:S(2)}, u32[]{:S(2)}) collective-permute-start(bf16[16,2880]{1,0:T(8,128)(2,1)S(1)} %get-tuple-element.71), channel_id=1, source_target_pairs={{0,8},{8,0},{16,24},{24,16},{1,9},{9,1},{17,25},{25,17},{2,10},{10... | collective-permute-start | bytes 276488 | tf_op jit(solution)/shard_map/ppermute | solution.py:30
  73.5 8.3 %collective-permute-start.31 = (bf16[16,2880]{1,0:T(8,128)(2,1)S(1)}, bf16[16,2880]{1,0:T(8,128)(2,1)S(1)}, u32[]{:S(2)}, u32[]{:S(2)}) collective-permute-start(bf16[16,2880]{1,0:T(8,128)(2,1)S(1)} %get-tuple-element.72), channel_id=1, source_target_pairs={{0,16},{8,24},{16,0},{24,8},{1,17},{9,25},{17,1},{25,9},{2,18},{10... | collective-permute-start | bytes 276488 | tf_op jit(solution)/shard_map/ppermute | solution.py:30
  74.4 7.4 %collective-permute-start.32 = (bf16[16,2880]{1,0:T(8,128)(2,1)S(1)}, bf16[16,2880]{1,0:T(8,128)(2,1)S(1)}, u32[]{:S(2)}, u32[]{:S(2)}) collective-permute-start(bf16[16,2880]{1,0:T(8,128)(2,1)S(1)} %get-tuple-element.73), channel_id=1, source_target_pairs={{0,24},{8,16},{16,8},{24,0},{1,25},{9,17},{17,9},{25,1},{2,26},{10... | collective-permute-start | bytes 276488 | tf_op jit(solution)/shard_map/ppermute | solution.py:30
  76.3 2.4 %collective-permute-start.26 = (f32[64,64]{1,0:T(8,128)S(1)}, f32[64,64]{1,0:T(8,128)S(1)}, u32[]{:S(2)}, u32[]{:S(2)}) collective-permute-start(f32[64,64]{1,0:T(8,128)S(1)} %get-tuple-element.64.refs_0_), channel_id=1, source_target_pairs={{0,1},{1,0},{2,3},{3,2},{4,5},{5,4},{6,7},{7,6},{8,9},{9,8},{10,11... | collective-permute-start | bytes 49160 | tf_op jit(solution)/shard_map/ppermute | solution.py:30
  76.4 5.4 %collective-permute-start.27 = (bf16[16,2304]{1,0:T(8,128)(2,1)S(1)}, bf16[16,2304]{1,0:T(8,128)(2,1)S(1)}, u32[]{:S(2)}, u32[]{:S(2)}) collective-permute-start(bf16[16,2304]{1,0:T(8,128)(2,1)S(1)} %get-tuple-element.67), channel_id=1, source_target_pairs={{0,8},{8,0},{16,24},{24,16},{1,9},{9,1},{17,25},{25,17},{2,10},{10... | collective-permute-start | bytes 221192 | tf_op jit(solution)/shard_map/ppermute | solution.py:30
  77.8 4.4 %collective-permute-start.28 = (bf16[16,2304]{1,0:T(8,128)(2,1)S(1)}, bf16[16,2304]{1,0:T(8,128)(2,1)S(1)}, u32[]{:S(2)}, u32[]{:S(2)}) collective-permute-start(bf16[16,2304]{1,0:T(8,128)(2,1)S(1)} %get-tuple-element.68), channel_id=1, source_target_pairs={{0,16},{8,24},{16,0},{24,8},{1,17},{9,25},{17,1},{25,9},{2,18},{10... | collective-permute-start | bytes 221192 | tf_op jit(solution)/shard_map/ppermute | solution.py:30
  78.8 5.3 %collective-permute-start.29 = (bf16[16,2304]{1,0:T(8,128)(2,1)S(1)}, bf16[16,2304]{1,0:T(8,128)(2,1)S(1)}, u32[]{:S(2)}, u32[]{:S(2)}) collective-permute-start(bf16[16,2304]{1,0:T(8,128)(2,1)S(1)} %get-tuple-element.69), channel_id=1, source_target_pairs={{0,24},{8,16},{16,8},{24,0},{1,25},{9,17},{17,9},{25,1},{2,26},{10... | collective-permute-start | bytes 221192 | tf_op jit(solution)/shard_map/ppermute | solution.py:30
  84.2 9.2 %collective-permute-start.34 = (bf16[64,2304]{1,0:T(8,128)(2,1)S(1)}, bf16[64,2304]{1,0:T(8,128)(2,1)S(1)}, u32[]{:S(2)}, u32[]{:S(2)}) collective-permute-start(bf16[64,2304]{1,0:T(8,128)(2,1)S(1)} %get-tuple-element.75.refs_0_), channel_id=1, source_target_pairs={{0,1},{1,0},{2,3},{3,2},{4,5},{5,4},{6,7},{7,6},{8,9},{9,8},{10,11... | collective-permute-start | bytes 884744 | tf_op jit(solution)/shard_map/ppermute | solution.py:30
  84.3 9.1 %collective-permute-start.33 = (f32[1,576]{1,0:T(1,128)S(1)}, f32[1,576]{1,0:T(1,128)S(1)}, u32[]{:S(2)}, u32[]{:S(2)}) collective-permute-start(f32[1,576]{1,0:T(1,128)S(1)} %get-tuple-element.74), channel_id=1, source_target_pairs={{0,0},{1,4},{2,8},{3,12},{4,16},{5,20},{6,24},{7,28},{8,1},{9,5},{... | collective-permute-start | bytes 6920 | tf_op jit(solution)/shard_map/ppermute | solution.py:637

commit v3 on v2

--- a/solution.py
+++ b/solution.py
@@ -296,9 +296,14 @@
         multiply(whole, jac, base + i * depth, depth, tiles.at[i % slots], 1)
         if i + slots < len(copies):
             copies[i + slots].start()
-    inner = lax.dot_general(
-        whole[...], side[...], (((1,), (1,)), ((), ())), precision=FULL, preferred_element_type=F32
-    )
+    inner = 0.0
+    left = whole[...]
+    for _ in range(3):
+        term = left.astype(BF16)
+        left = left - term.astype(F32)
+        inner = inner + lax.dot_general(
+            term, side[...], (((1,), (1,)), ((), ())), preferred_element_type=F32
+        )
     me = lax.axis_index("row")
     overall, width = whole.shape
     measures = overall // peers
@@ -578,7 +583,7 @@
         out_specs=[VMEM] * rows,
         scratch_shapes=[
             pltpu.VMEM((overall, part_b), BF16),
-            pltpu.VMEM((overall, width), F32),
+            pltpu.VMEM((overall, width), BF16),
             pltpu.VMEM((overall, width), F32),
             pltpu.VMEM((2, depth, width), F32),
             dma((2,)),

time: 109 us -> 109 us (level)
  no operation moved by 1% of the time
where the time goes in v3:
time: 109 us
  Pallas kernels  45.2 us (41%)
  starting transfers between devices  36.4 us (33%)
  waiting for transfers between devices  26.2 us (24%)
    ppermute x34, starting transfers between devices, swap(): return lax.ppermute(block, axis, [(i, i ^ step) for i in range(n)])  32.2 us
    ppermute x34, waiting for transfers between devices, swap(): return lax.ppermute(block, axis, [(i, i ^ step) for i in range(n)])  21.3 us
    pallas_call x1, Pallas kernels, on_device(): pl.pallas_call(functools.partial(update_kernel, THIN), out_shape=[shape((...  15.7 us
    pallas_call x1, Pallas kernels, on_device(): pl.pallas_call(functools.partial(counts_kernel, 0), out_shape=[shape((ato...  7.06 us
    pallas_call x1, Pallas kernels, on_device(): pl.pallas_call(functools.partial(product_last_kernel, rows, depth, rest),...  6.84 us
    pallas_call x2, Pallas kernels, on_device(): pl.pallas_call(functools.partial(jacobian_kernel, cols, rows, width_in, s...  6.44 us
    pallas_call x1, Pallas kernels, on_device(): pl.pallas_call(functools.partial(product_first_kernel, rows, depth), out_...  5.43 us
    ppermute x1, waiting for transfers between devices, on_device(): moved = lax.ppermute(change, ('row', 'col'), pairs)  4.93 us
  transfers between devices with their start and end apart: 35, of which 12 were waited for; matrix products, arithmetic and copies ran while one was open for 0% of the time, Pallas kernels for 16%

profile of v3, /device:TPU:6, one launch (start us, length us, event | category | flops | bytes accessed | tf_op | source)
XLA Modules:
  0.0 108.8 jit_solution(8199309483617084252)
XLA Ops:
  0.6 1.1 %pack.1 = (bf16[2,64,384]{2,1,0:T(8,128)(2,1)S(1)}, s32[2,64,138]{2,1,0:T(8,128)S(1)}, s32[2,64]{1,0:T(2,128)S(1)}, f32[2,128]{1,0:T(2,128)S(1)}, f32[16,128]{1,0:T(8,128)S(1)}) custom-call(bf16[2,64,128]{2,1,0:T(8,128)(2,1)} %up_ref.1, bf16[2,64,144]{2,1,0:T(8,128)(2,1)} %act_ref.1, s32[2,64,138]{2,1,0:T(8,128)} %neighbors_ref.1, s32[2,64]{1,0:T(2,128)} %types_ref.1, ...), custom_call_target="tpu_custom_call" | custom-call | tf_op jit(solution)/shard_map/pack/pallas_call | solution.py:498
  1.8 3.7 %collective-permute-start.5 = (bf16[2,64,384]{2,1,0:T(8,128)(2,1)S(1)}, bf16[2,64,384]{2,1,0:T(8,128)(2,1)S(1)}, u32[]{:S(2)}, u32[]{:S(2)}) collective-permute-start(bf16[2,64,384]{2,1,0:T(8,128)(2,1)S(1)} %get-tuple-element.45.refs_4_.refs_8_), channel_id=1, source_target_pairs={{0,6},{1,7},{2,4},{3,5},{4,2},{5,3},{6,0},{7,1},{8,14},{9,15},{10,... | collective-permute-start | bytes 294920 | tf_op jit(solution)/shard_map/ppermute | solution.py:30
  5.4 0.0 collective-permute-start.3
  5.4 0.8 collective-permute-start.1
  6.2 0.0 collective-permute-start
  6.2 2.9 %collective-permute-done.5.refs_10_.refs_14_ = bf16[2,64,384]{2,1,0:T(8,128)(2,1)S(1)} collective-permute-done((bf16[2,64,384]{2,1,0:T(8,128)(2,1)S(1)}, bf16[2,64,384]{2,1,0:T(8,128)(2,1)S(1)}, u32[]{:S(2)}, u32[]{:S(2)}) %collective-permute-start.5) | collective-permute-done | bytes 98336 | tf_op jit(solution)/shard_map/ppermute | solution.py:30
  9.1 0.0 collective-permute-start.6
  9.1 4.6 %collective-permute-done.3.refs_8_.refs_12_ = bf16[2,64,384]{2,1,0:T(8,128)(2,1)S(1)} collective-permute-done((bf16[2,64,384]{2,1,0:T(8,128)(2,1)S(1)}, bf16[2,64,384]{2,1,0:T(8,128)(2,1)S(1)}, u32[]{:S(2)}, u32[]{:S(2)}) %collective-permute-start.3) | collective-permute-done | bytes 98336 | tf_op jit(solution)/shard_map/ppermute | solution.py:30
  13.7 0.0 collective-permute-start.4
  13.7 0.0 collective-permute-done.1.refs_6_.refs_10_
  13.7 0.5 collective-permute-start.2
  14.2 7.1 %counts.1 = (bf16[512,128]{1,0:T(8,128)(2,1)S(1)}, f32[768,2304]{1,0:T(8,128)S(1)}, f32[768,2304]{1,0:T(8,128)S(1)}, f32[768,2304]{1,0:T(8,128)S(1)}) custom-call(s32[2,64,138]{2,1,0:T(8,128)S(1)} %get-tuple-element.40.near_ref, f32[4608,2304]{1,0:T(8,128)} %refs_9_.1), custom_call_target="tpu_custom_call" | custom-call | flops 3000000000 | bytes 21233664 | tf_op jit(solution)/shard_map/counts/pallas_call | solution.py:520
  21.3 0.0 collective-permute-done.refs_5_.refs_9_
  21.3 0.0 collective-permute-done.6.refs_11_.refs_15_
  21.3 0.4 adjoint.1.refs_0_
  21.7 2.6 %collective-permute-start.12 = (f32[144,128]{1,0:T(8,128)S(1)}, f32[144,128]{1,0:T(8,128)S(1)}, u32[]{:S(2)}, u32[]{:S(2)}) collective-permute-start(f32[144,128]{1,0:T(8,128)S(1)} %adjoint.1.refs_0_), channel_id=1, source_target_pairs={{0,6},{1,7},{2,4},{3,5},{4,2},{5,3},{6,0},{7,1},{8,14},{9,15},{10,... | collective-permute-start | bytes 221192 | tf_op jit(solution)/shard_map/ppermute | solution.py:30
  24.3 0.0 collective-permute-start.10
  24.3 1.9 %collective-permute-start.8 = (f32[144,128]{1,0:T(8,128)S(1)}, f32[144,128]{1,0:T(8,128)S(1)}, u32[]{:S(2)}, u32[]{:S(2)}) collective-permute-start(f32[144,128]{1,0:T(8,128)S(1)} %adjoint.1.refs_0_), channel_id=1, source_target_pairs={{0,2},{1,3},{2,0},{3,1},{4,6},{5,7},{6,4},{7,5},{8,10},{9,11},{10,... | collective-permute-start | bytes 221192 | tf_op jit(solution)/shard_map/ppermute | solution.py:30
  26.1 2.5 %collective-permute-done.12.refs_6_ = f32[144,128]{1,0:T(8,128)S(1)} collective-permute-done((f32[144,128]{1,0:T(8,128)S(1)}, f32[144,128]{1,0:T(8,128)S(1)}, u32[]{:S(2)}, u32[]{:S(2)}) %collective-permute-start.12) | collective-permute-done | bytes 73760 | tf_op jit(solution)/shard_map/ppermute | solution.py:30
  28.6 0.0 collective-permute-start.13
  28.6 2.3 %collective-permute-done.10.refs_4_ = f32[144,128]{1,0:T(8,128)S(1)} collective-permute-done((f32[144,128]{1,0:T(8,128)S(1)}, f32[144,128]{1,0:T(8,128)S(1)}, u32[]{:S(2)}, u32[]{:S(2)}) %collective-permute-start.10) | collective-permute-done | bytes 73760 | tf_op jit(solution)/shard_map/ppermute | solution.py:30
  30.9 0.0 collective-permute-start.11
  30.9 0.0 collective-permute-done.8.refs_2_
  30.9 0.5 collective-permute-start.9
  31.4 0.7 collective-permute-done.11.refs_5_
  32.2 0.2 collective-permute-done.9.refs_3_
  32.3 3.0 %jacobian_first.1 = (bf16[16,2304]{1,0:T(8,128)(2,1)S(1)}, bf16[16,2304]{1,0:T(8,128)(2,1)S(1)}, bf16[16,2304]{1,0:T(8,128)(2,1)S(1)}, bf16[16,2304]{1,0:T(8,128)(2,1)S(1)}, f32[768,2304]{1,0:T(8,128)S(1)}) custom-call(f32[144,128]{1,0:T(8,128)S(1)} %adjoint.1.refs_0_, f32[144,128]{1,0:T(8,128)S(1)} %collective-permute-done.7.refs_1_, ...), custom_call_target="tpu_custom_call" | custom-call | flops 3000000000 | bytes 7077888 | tf_op jit(solution)/shard_map/jacobian_first/pallas_call | solution.py:548
  35.3 0.6 collective-permute-start.17
  35.9 0.5 collective-permute-start.18
  36.4 2.4 %collective-permute-start.19 = (bf16[16,2304]{1,0:T(8,128)(2,1)S(1)}, bf16[16,2304]{1,0:T(8,128)(2,1)S(1)}, u32[]{:S(2)}, u32[]{:S(2)}) collective-permute-start(bf16[16,2304]{1,0:T(8,128)(2,1)S(1)} %get-tuple-element.53), channel_id=1, source_target_pairs={{0,24},{8,16},{16,8},{24,0},{1,25},{9,17},{17,9},{25,1},{2,26},{10... | collective-permute-start | bytes 221192 | tf_op jit(solution)/shard_map/ppermute | solution.py:30
  38.9 3.4 %jacobian_last.1 = (bf16[16,4608]{1,0:T(8,128)(2,1)S(1)}, bf16[16,4608]{1,0:T(8,128)(2,1)S(1)}, bf16[16,4608]{1,0:T(8,128)(2,1)S(1)}, bf16[16,4608]{1,0:T(8,128)(2,1)S(1)}, f32[768,2304]{1,0:T(8,128)S(1)}) custom-call(f32[144,128]{1,0:T(8,128)S(1)} %adjoint.1.refs_0_, f32[144,128]{1,0:T(8,128)S(1)} %collective-permute-done.7.refs_1_, ...), custom_call_target="tpu_custom_call" | custom-call | flops 3000000000 | bytes 7077888 | tf_op jit(solution)/shard_map/jacobian_last/pallas_call | solution.py:548
  42.3 0.6 collective-permute-start.14
  42.9 0.5 collective-permute-start.15
  43.4 2.4 %collective-permute-start.16 = (bf16[16,4608]{1,0:T(8,128)(2,1)S(1)}, bf16[16,4608]{1,0:T(8,128)(2,1)S(1)}, u32[]{:S(2)}, u32[]{:S(2)}) collective-permute-start(bf16[16,4608]{1,0:T(8,128)(2,1)S(1)} %get-tuple-element.49), channel_id=1, source_target_pairs={{0,24},{8,16},{16,8},{24,0},{1,25},{9,17},{17,9},{25,1},{2,26},{10... | collective-permute-start | bytes 442376 | tf_op jit(solution)/shard_map/ppermute | solution.py:30
  45.9 5.4 %product_first.1.refs_4_ = f32[64,2304]{1,0:T(8,128)S(1)} custom-call(bf16[16,2304]{1,0:T(8,128)(2,1)S(1)} %get-tuple-element.50.refs_0_, bf16[16,2304]{1,0:T(8,128)(2,1)S(1)} %collective-permute-done.17.refs_1_, bf16[16,2304]{1,0:T(8,128)(2,1)S(1)} %collective-permute-done.18.refs_2_, bf16[16,2304]{1,0:T(8,128)(2,1)S(1)} %collective-permute-done.19.refs_3_, ...), custom_call_target="tpu_custom_call" | custom-call | flops 2717908992 | bytes 21233664 | tf_op jit(solution)/shard_map/product_first/pallas_call | solution.py:568
  51.4 0.0 copy-start.1
  51.4 0.0 copy-start.2
  51.4 0.0 copy-start
  51.4 6.8 %product_last.1 = (f32[16,2560]{1,0:T(8,128)S(1)}, f32[16,2560]{1,0:T(8,128)S(1)}, f32[16,2560]{1,0:T(8,128)S(1)}, f32[16,2560]{1,0:T(8,128)S(1)}) custom-call(bf16[16,4608]{1,0:T(8,128)(2,1)S(1)} %get-tuple-element.46.refs_0_, bf16[16,4608]{1,0:T(8,128)(2,1)S(1)} %collective-permute-done.14.refs_1_, bf16[16,4608]{1,0:T(8,128)(2,1)S(1)} %collective-permute-done.15.refs_2_, ...), custom_call_target="tpu_custom_call" | custom-call | flops 2717908992 | bytes 21233664 | tf_op jit(solution)/shard_map/product_last/pallas_call | solution.py:579
  58.2 1.2 %collective-permute-start.20 = (f32[16,2560]{1,0:T(8,128)S(1)}, f32[16,2560]{1,0:T(8,128)S(1)}, u32[]{:S(2)}, u32[]{:S(2)}) collective-permute-start(f32[16,2560]{1,0:T(8,128)S(1)} %get-tuple-element.60), channel_id=1, source_target_pairs={{0,8},{8,0},{16,24},{24,16},{1,9},{9,1},{17,25},{25,17},{2,10},{10... | collective-permute-start | bytes 491528 | tf_op jit(solution)/shard_map/ppermute | solution.py:30
  59.5 0.7 collective-permute-start.21
  60.1 1.7 %collective-permute-start.22 = (f32[16,2560]{1,0:T(8,128)S(1)}, f32[16,2560]{1,0:T(8,128)S(1)}, u32[]{:S(2)}, u32[]{:S(2)}) collective-permute-start(f32[16,2560]{1,0:T(8,128)S(1)} %get-tuple-element.62), channel_id=1, source_target_pairs={{0,24},{8,16},{16,8},{24,0},{1,25},{9,17},{17,9},{25,1},{2,26},{10... | collective-permute-start | bytes 491528 | tf_op jit(solution)/shard_map/ppermute | solution.py:30
  61.8 3.0 %collective-permute-done.20.refs_1_ = f32[16,2560]{1,0:T(8,128)S(1)} collective-permute-done((f32[16,2560]{1,0:T(8,128)S(1)}, f32[16,2560]{1,0:T(8,128)S(1)}, u32[]{:S(2)}, u32[]{:S(2)}) %collective-permute-start.20) | collective-permute-done | bytes 163872 | tf_op jit(solution)/shard_map/ppermute | solution.py:30
  64.8 2.5 %collective-permute-done.21.refs_2_ = f32[16,2560]{1,0:T(8,128)S(1)} collective-permute-done((f32[16,2560]{1,0:T(8,128)S(1)}, f32[16,2560]{1,0:T(8,128)S(1)}, u32[]{:S(2)}, u32[]{:S(2)}) %collective-permute-start.21) | collective-permute-done | bytes 163872 | tf_op jit(solution)/shard_map/ppermute | solution.py:30
  67.3 0.1 sum.1
  67.5 2.6 %collective-permute-start.25 = (bf16[16,2816]{1,0:T(8,128)(2,1)S(1)}, bf16[16,2816]{1,0:T(8,128)(2,1)S(1)}, u32[]{:S(2)}, u32[]{:S(2)}) collective-permute-start(bf16[16,2816]{1,0:T(8,128)(2,1)S(1)} %get-tuple-element.63.refs_0_), channel_id=1, source_target_pairs={{0,6},{1,7},{2,4},{3,5},{4,2},{5,3},{6,0},{7,1},{8,14},{9,15},{10,... | collective-permute-start | bytes 270344 | tf_op jit(solution)/shard_map/ppermute | solution.py:30
  70.0 1.9 %collective-permute-start.23 = (bf16[16,2816]{1,0:T(8,128)(2,1)S(1)}, bf16[16,2816]{1,0:T(8,128)(2,1)S(1)}, u32[]{:S(2)}, u32[]{:S(2)}) collective-permute-start(bf16[16,2816]{1,0:T(8,128)(2,1)S(1)} %get-tuple-element.63.refs_0_), channel_id=1, source_target_pairs={{0,2},{1,3},{2,0},{3,1},{4,6},{5,7},{6,4},{7,5},{8,10},{9,11},{10,... | collective-permute-start | bytes 270344 | tf_op jit(solution)/shard_map/ppermute | solution.py:30
  71.9 1.1 %collective-permute-start.30 = (bf16[16,2880]{1,0:T(8,128)(2,1)S(1)}, bf16[16,2880]{1,0:T(8,128)(2,1)S(1)}, u32[]{:S(2)}, u32[]{:S(2)}) collective-permute-start(bf16[16,2880]{1,0:T(8,128)(2,1)S(1)} %get-tuple-element.71), channel_id=1, source_target_pairs={{0,8},{8,0},{16,24},{24,16},{1,9},{9,1},{17,25},{25,17},{2,10},{10... | collective-permute-start | bytes 276488 | tf_op jit(solution)/shard_map/ppermute | solution.py:30
  73.0 0.9 collective-permute-start.31
  73.9 1.5 %collective-permute-start.32 = (bf16[16,2880]{1,0:T(8,128)(2,1)S(1)}, bf16[16,2880]{1,0:T(8,128)(2,1)S(1)}, u32[]{:S(2)}, u32[]{:S(2)}) collective-permute-start(bf16[16,2880]{1,0:T(8,128)(2,1)S(1)} %get-tuple-element.73), channel_id=1, source_target_pairs={{0,24},{8,16},{16,8},{24,0},{1,25},{9,17},{17,9},{25,1},{2,26},{10... | collective-permute-start | bytes 276488 | tf_op jit(solution)/shard_map/ppermute | solution.py:30
  75.4 0.4 collective-permute-done.24.refs_2_
  75.8 0.1 route.1
  75.9 0.0 collective-permute-start.26
  75.9 1.4 %collective-permute-start.27 = (bf16[16,2304]{1,0:T(8,128)(2,1)S(1)}, bf16[16,2304]{1,0:T(8,128)(2,1)S(1)}, u32[]{:S(2)}, u32[]{:S(2)}) collective-permute-start(bf16[16,2304]{1,0:T(8,128)(2,1)S(1)} %get-tuple-element.67), channel_id=1, source_target_pairs={{0,8},{8,0},{16,24},{24,16},{1,9},{9,1},{17,25},{25,17},{2,10},{10... | collective-permute-start | bytes 221192 | tf_op jit(solution)/shard_map/ppermute | solution.py:30
  77.3 1.0 collective-permute-start.28
  78.3 1.2 %collective-permute-start.29 = (bf16[16,2304]{1,0:T(8,128)(2,1)S(1)}, bf16[16,2304]{1,0:T(8,128)(2,1)S(1)}, u32[]{:S(2)}, u32[]{:S(2)}) collective-permute-start(bf16[16,2304]{1,0:T(8,128)(2,1)S(1)} %get-tuple-element.69), channel_id=1, source_target_pairs={{0,24},{8,16},{16,8},{24,0},{1,25},{9,17},{17,9},{25,1},{2,26},{10... | collective-permute-start | bytes 221192 | tf_op jit(solution)/shard_map/ppermute | solution.py:30
  79.5 1.8 %inverse.1 = (f32[64,64]{1,0:T(8,128)S(1)}, f32[64,1]{1,0:T(8,128)S(1)}) custom-call(f32[64,64]{1,0:T(8,128)S(1)} %get-tuple-element.64.refs_0_, f32[64,64]{1,0:T(8,128)S(1)} %collective-permute-done.26.refs_1_, f32[1,64]{1,0:T(1,128)S(1)} %bitcast.2, f32[1,64]{1,0:T(1,128)S(1)} %bitcast.3), custom_call_target="tpu_custom_call" | custom-call | tf_op jit(solution)/shard_map/inverse/pallas_call | solution.py:620
  81.3 0.4 collective-permute-done.28.refs_2_
  81.7 1.9 %collective-permute-done.29.refs_3_ = bf16[16,2304]{1,0:T(8,128)(2,1)S(1)} collective-permute-done((bf16[16,2304]{1,0:T(8,128)(2,1)S(1)}, bf16[16,2304]{1,0:T(8,128)(2,1)S(1)}, u32[]{:S(2)}, u32[]{:S(2)}) %collective-permute-start.29) | collective-permute-done | bytes 73760 | tf_op jit(solution)/shard_map/ppermute | solution.py:30
  83.6 0.2 merge.1
  83.8 0.1 collective-permute-start.34
  83.8 4.1 %collective-permute-start.33 = (f32[1,576]{1,0:T(1,128)S(1)}, f32[1,576]{1,0:T(1,128)S(1)}, u32[]{:S(2)}, u32[]{:S(2)}) collective-permute-start(f32[1,576]{1,0:T(1,128)S(1)} %get-tuple-element.74), channel_id=1, source_target_pairs={{0,0},{1,4},{2,8},{3,12},{4,16},{5,20},{6,24},{7,28},{8,1},{9,5},{... | collective-permute-start | bytes 6920 | tf_op jit(solution)/shard_map/ppermute | solution.py:642
  88.0 4.9 %collective-permute-done.33.moved_ref = f32[1,576]{1,0:T(1,128)S(1)} collective-permute-done((f32[1,576]{1,0:T(1,128)S(1)}, f32[1,576]{1,0:T(1,128)S(1)}, u32[]{:S(2)}, u32[]{:S(2)}) %collective-permute-start.33) | collective-permute-done | bytes 2336 | tf_op jit(solution)/shard_map/ppermute | solution.py:642
  92.9 15.7 %update.1 = (f32[576]{0:T(1024)}, f32[4608,2304]{1,0:T(8,128)}) custom-call(f32[576]{0:T(1024)S(1)} %copy-done, f32[1,576]{1,0:T(1,128)S(1)} %collective-permute-done.33.moved_ref, bf16[64,2304]{1,0:T(8,128)(2,1)S(1)} %get-tuple-element.75.refs_0_, bf16[64,2304]{1,0:T(8,128)(2,1)S(1)} %collective-permute-done.34.refs_1_, ...), custom_call_target="tpu_custom_call" | custom-call | flops 1358954496 | bytes 42467328 | tf_op jit(solution)/shard_map/update/pallas_call | solution.py:645
  (24 shorter events, 0.1 us)
Async XLA Ops:
  1.8 7.4 %collective-permute-start.5 = (bf16[2,64,384]{2,1,0:T(8,128)(2,1)S(1)}, bf16[2,64,384]{2,1,0:T(8,128)(2,1)S(1)}, u32[]{:S(2)}, u32[]{:S(2)}) collective-permute-start(bf16[2,64,384]{2,1,0:T(8,128)(2,1)S(1)} %get-tuple-element.45.refs_4_.refs_8_), channel_id=1, source_target_pairs={{0,6},{1,7},{2,4},{3,5},{4,2},{5,3},{6,0},{7,1},{8,14},{9,15},{10,... | collective-permute-start | bytes 294920 | tf_op jit(solution)/shard_map/ppermute | solution.py:30
  5.4 8.3 %collective-permute-start.3 = (bf16[2,64,384]{2,1,0:T(8,128)(2,1)S(1)}, bf16[2,64,384]{2,1,0:T(8,128)(2,1)S(1)}, u32[]{:S(2)}, u32[]{:S(2)}) collective-permute-start(bf16[2,64,384]{2,1,0:T(8,128)(2,1)S(1)} %get-tuple-element.45.refs_4_.refs_8_), channel_id=1, source_target_pairs={{0,4},{1,5},{2,6},{3,7},{4,0},{5,1},{6,2},{7,3},{8,12},{9,13},{10,... | collective-permute-start | bytes 294920 | tf_op jit(solution)/shard_map/ppermute | solution.py:30
  5.4 8.3 %collective-permute-start.1 = (bf16[2,64,384]{2,1,0:T(8,128)(2,1)S(1)}, bf16[2,64,384]{2,1,0:T(8,128)(2,1)S(1)}, u32[]{:S(2)}, u32[]{:S(2)}) collective-permute-start(bf16[2,64,384]{2,1,0:T(8,128)(2,1)S(1)} %get-tuple-element.45.refs_4_.refs_8_), channel_id=1, source_target_pairs={{0,2},{1,3},{2,0},{3,1},{4,6},{5,7},{6,4},{7,5},{8,10},{9,11},{10,... | collective-permute-start | bytes 294920 | tf_op jit(solution)/shard_map/ppermute | solution.py:30
  6.2 15.1 %collective-permute-start = (bf16[2,64,384]{2,1,0:T(8,128)(2,1)S(1)}, bf16[2,64,384]{2,1,0:T(8,128)(2,1)S(1)}, u32[]{:S(2)}, u32[]{:S(2)}) collective-permute-start(bf16[2,64,384]{2,1,0:T(8,128)(2,1)S(1)} %get-tuple-element.45.refs_4_.refs_8_), channel_id=1, source_target_pairs={{0,1},{1,0},{2,3},{3,2},{4,5},{5,4},{6,7},{7,6},{8,9},{9,8},{10,11... | collective-permute-start | bytes 294920 | tf_op jit(solution)/shard_map/ppermute | solution.py:30
  9.1 12.2 %collective-permute-start.6 = (bf16[2,64,384]{2,1,0:T(8,128)(2,1)S(1)}, bf16[2,64,384]{2,1,0:T(8,128)(2,1)S(1)}, u32[]{:S(2)}, u32[]{:S(2)}) collective-permute-start(bf16[2,64,384]{2,1,0:T(8,128)(2,1)S(1)} %collective-permute-done.5.refs_10_.refs_14_), channel_id=1, source_target_pairs={{0,1},{1,0},{2,3},{3,2},{4,5},{5,4},{6,7},{7,6},{8,9},{9,8},{10,11... | collective-permute-start | bytes 294920 | tf_op jit(solution)/shard_map/ppermute | solution.py:30
  13.7 7.6 %collective-permute-start.4 = (bf16[2,64,384]{2,1,0:T(8,128)(2,1)S(1)}, bf16[2,64,384]{2,1,0:T(8,128)(2,1)S(1)}, u32[]{:S(2)}, u32[]{:S(2)}) collective-permute-start(bf16[2,64,384]{2,1,0:T(8,128)(2,1)S(1)} %collective-permute-done.3.refs_8_.refs_12_), channel_id=1, source_target_pairs={{0,1},{1,0},{2,3},{3,2},{4,5},{5,4},{6,7},{7,6},{8,9},{9,8},{10,11... | collective-permute-start | bytes 294920 | tf_op jit(solution)/shard_map/ppermute | solution.py:30
  13.7 7.6 %collective-permute-start.2 = (bf16[2,64,384]{2,1,0:T(8,128)(2,1)S(1)}, bf16[2,64,384]{2,1,0:T(8,128)(2,1)S(1)}, u32[]{:S(2)}, u32[]{:S(2)}) collective-permute-start(bf16[2,64,384]{2,1,0:T(8,128)(2,1)S(1)} %collective-permute-done.1.refs_6_.refs_10_), channel_id=1, source_target_pairs={{0,1},{1,0},{2,3},{3,2},{4,5},{5,4},{6,7},{7,6},{8,9},{9,8},{10,11... | collective-permute-start | bytes 294920 | tf_op jit(solution)/shard_map/ppermute | solution.py:30
  21.7 6.9 %collective-permute-start.12 = (f32[144,128]{1,0:T(8,128)S(1)}, f32[144,128]{1,0:T(8,128)S(1)}, u32[]{:S(2)}, u32[]{:S(2)}) collective-permute-start(f32[144,128]{1,0:T(8,128)S(1)} %adjoint.1.refs_0_), channel_id=1, source_target_pairs={{0,6},{1,7},{2,4},{3,5},{4,2},{5,3},{6,0},{7,1},{8,14},{9,15},{10,... | collective-permute-start | bytes 221192 | tf_op jit(solution)/shard_map/ppermute | solution.py:30
  24.3 6.6 %collective-permute-start.10 = (f32[144,128]{1,0:T(8,128)S(1)}, f32[144,128]{1,0:T(8,128)S(1)}, u32[]{:S(2)}, u32[]{:S(2)}) collective-permute-start(f32[144,128]{1,0:T(8,128)S(1)} %adjoint.1.refs_0_), channel_id=1, source_target_pairs={{0,4},{1,5},{2,6},{3,7},{4,0},{5,1},{6,2},{7,3},{8,12},{9,13},{10,... | collective-permute-start | bytes 221192 | tf_op jit(solution)/shard_map/ppermute | solution.py:30
  24.3 6.6 %collective-permute-start.8 = (f32[144,128]{1,0:T(8,128)S(1)}, f32[144,128]{1,0:T(8,128)S(1)}, u32[]{:S(2)}, u32[]{:S(2)}) collective-permute-start(f32[144,128]{1,0:T(8,128)S(1)} %adjoint.1.refs_0_), channel_id=1, source_target_pairs={{0,2},{1,3},{2,0},{3,1},{4,6},{5,7},{6,4},{7,5},{8,10},{9,11},{10,... | collective-permute-start | bytes 221192 | tf_op jit(solution)/shard_map/ppermute | solution.py:30
  26.1 5.3 %collective-permute-start.7 = (f32[144,128]{1,0:T(8,128)S(1)}, f32[144,128]{1,0:T(8,128)S(1)}, u32[]{:S(2)}, u32[]{:S(2)}) collective-permute-start(f32[144,128]{1,0:T(8,128)S(1)} %adjoint.1.refs_0_), channel_id=1, source_target_pairs={{0,1},{1,0},{2,3},{3,2},{4,5},{5,4},{6,7},{7,6},{8,9},{9,8},{10,11... | collective-permute-start | bytes 221192 | tf_op jit(solution)/shard_map/ppermute | solution.py:30
  28.6 2.8 %collective-permute-start.13 = (f32[144,128]{1,0:T(8,128)S(1)}, f32[144,128]{1,0:T(8,128)S(1)}, u32[]{:S(2)}, u32[]{:S(2)}) collective-permute-start(f32[144,128]{1,0:T(8,128)S(1)} %collective-permute-done.12.refs_6_), channel_id=1, source_target_pairs={{0,1},{1,0},{2,3},{3,2},{4,5},{5,4},{6,7},{7,6},{8,9},{9,8},{10,11... | collective-permute-start | bytes 221192 | tf_op jit(solution)/shard_map/ppermute | solution.py:30
  30.9 1.3 %collective-permute-start.11 = (f32[144,128]{1,0:T(8,128)S(1)}, f32[144,128]{1,0:T(8,128)S(1)}, u32[]{:S(2)}, u32[]{:S(2)}) collective-permute-start(f32[144,128]{1,0:T(8,128)S(1)} %collective-permute-done.10.refs_4_), channel_id=1, source_target_pairs={{0,1},{1,0},{2,3},{3,2},{4,5},{5,4},{6,7},{7,6},{8,9},{9,8},{10,11... | collective-permute-start | bytes 221192 | tf_op jit(solution)/shard_map/ppermute | solution.py:30
  30.9 1.4 %collective-permute-start.9 = (f32[144,128]{1,0:T(8,128)S(1)}, f32[144,128]{1,0:T(8,128)S(1)}, u32[]{:S(2)}, u32[]{:S(2)}) collective-permute-start(f32[144,128]{1,0:T(8,128)S(1)} %collective-permute-done.8.refs_2_), channel_id=1, source_target_pairs={{0,1},{1,0},{2,3},{3,2},{4,5},{5,4},{6,7},{7,6},{8,9},{9,8},{10,11... | collective-permute-start | bytes 221192 | tf_op jit(solution)/shard_map/ppermute | solution.py:30
  35.3 8.1 %collective-permute-start.17 = (bf16[16,2304]{1,0:T(8,128)(2,1)S(1)}, bf16[16,2304]{1,0:T(8,128)(2,1)S(1)}, u32[]{:S(2)}, u32[]{:S(2)}) collective-permute-start(bf16[16,2304]{1,0:T(8,128)(2,1)S(1)} %get-tuple-element.51), channel_id=1, source_target_pairs={{0,8},{8,0},{16,24},{24,16},{1,9},{9,1},{17,25},{25,17},{2,10},{10... | collective-permute-start | bytes 221192 | tf_op jit(solution)/shard_map/ppermute | solution.py:30
  35.9 9.9 %collective-permute-start.18 = (bf16[16,2304]{1,0:T(8,128)(2,1)S(1)}, bf16[16,2304]{1,0:T(8,128)(2,1)S(1)}, u32[]{:S(2)}, u32[]{:S(2)}) collective-permute-start(bf16[16,2304]{1,0:T(8,128)(2,1)S(1)} %get-tuple-element.52), channel_id=1, source_target_pairs={{0,16},{8,24},{16,0},{24,8},{1,17},{9,25},{17,1},{25,9},{2,18},{10... | collective-permute-start | bytes 221192 | tf_op jit(solution)/shard_map/ppermute | solution.py:30
  36.4 9.4 %collective-permute-start.19 = (bf16[16,2304]{1,0:T(8,128)(2,1)S(1)}, bf16[16,2304]{1,0:T(8,128)(2,1)S(1)}, u32[]{:S(2)}, u32[]{:S(2)}) collective-permute-start(bf16[16,2304]{1,0:T(8,128)(2,1)S(1)} %get-tuple-element.53), channel_id=1, source_target_pairs={{0,24},{8,16},{16,8},{24,0},{1,25},{9,17},{17,9},{25,1},{2,26},{10... | collective-permute-start | bytes 221192 | tf_op jit(solution)/shard_map/ppermute | solution.py:30
  42.3 9.0 %collective-permute-start.14 = (bf16[16,4608]{1,0:T(8,128)(2,1)S(1)}, bf16[16,4608]{1,0:T(8,128)(2,1)S(1)}, u32[]{:S(2)}, u32[]{:S(2)}) collective-permute-start(bf16[16,4608]{1,0:T(8,128)(2,1)S(1)} %get-tuple-element.47), channel_id=1, source_target_pairs={{0,8},{8,0},{16,24},{24,16},{1,9},{9,1},{17,25},{25,17},{2,10},{10... | collective-permute-start | bytes 442376 | tf_op jit(solution)/shard_map/ppermute | solution.py:30
  42.9 8.4 %collective-permute-start.15 = (bf16[16,4608]{1,0:T(8,128)(2,1)S(1)}, bf16[16,4608]{1,0:T(8,128)(2,1)S(1)}, u32[]{:S(2)}, u32[]{:S(2)}) collective-permute-start(bf16[16,4608]{1,0:T(8,128)(2,1)S(1)} %get-tuple-element.48), channel_id=1, source_target_pairs={{0,16},{8,24},{16,0},{24,8},{1,17},{9,25},{17,1},{25,9},{2,18},{10... | collective-permute-start | bytes 442376 | tf_op jit(solution)/shard_map/ppermute | solution.py:30
  43.4 7.9 %collective-permute-start.16 = (bf16[16,4608]{1,0:T(8,128)(2,1)S(1)}, bf16[16,4608]{1,0:T(8,128)(2,1)S(1)}, u32[]{:S(2)}, u32[]{:S(2)}) collective-permute-start(bf16[16,4608]{1,0:T(8,128)(2,1)S(1)} %get-tuple-element.49), channel_id=1, source_target_pairs={{0,24},{8,16},{16,8},{24,0},{1,25},{9,17},{17,9},{25,1},{2,26},{10... | collective-permute-start | bytes 442376 | tf_op jit(solution)/shard_map/ppermute | solution.py:30
  51.4 28.1 %copy-start.1 = (f32[64]{0:T(128)S(1)}, f32[64]{0:T(128)}, u32[]{:S(2)}) copy-start(f32[64]{0:T(128)} %param.20) | copy-start | bytes 772
  51.4 28.1 %copy-start.2 = (f32[64]{0:T(128)S(1)}, f32[64]{0:T(128)}, u32[]{:S(2)}) copy-start(f32[64]{0:T(128)} %param.21) | copy-start | bytes 772
  51.4 41.5 %copy-start = (f32[576]{0:T(1024)S(1)}, f32[576]{0:T(1024)}, u32[]{:S(2)}) copy-start(f32[576]{0:T(1024)} %weights_ref.1) | copy-start | bytes 6916
  58.2 6.6 %collective-permute-start.20 = (f32[16,2560]{1,0:T(8,128)S(1)}, f32[16,2560]{1,0:T(8,128)S(1)}, u32[]{:S(2)}, u32[]{:S(2)}) collective-permute-start(f32[16,2560]{1,0:T(8,128)S(1)} %get-tuple-element.60), channel_id=1, source_target_pairs={{0,8},{8,0},{16,24},{24,16},{1,9},{9,1},{17,25},{25,17},{2,10},{10... | collective-permute-start | bytes 491528 | tf_op jit(solution)/shard_map/ppermute | solution.py:30
  59.5 7.8 %collective-permute-start.21 = (f32[16,2560]{1,0:T(8,128)S(1)}, f32[16,2560]{1,0:T(8,128)S(1)}, u32[]{:S(2)}, u32[]{:S(2)}) collective-permute-start(f32[16,2560]{1,0:T(8,128)S(1)} %get-tuple-element.61), channel_id=1, source_target_pairs={{0,16},{8,24},{16,0},{24,8},{1,17},{9,25},{17,1},{25,9},{2,18},{10... | collective-permute-start | bytes 491528 | tf_op jit(solution)/shard_map/ppermute | solution.py:30
  60.1 7.2 %collective-permute-start.22 = (f32[16,2560]{1,0:T(8,128)S(1)}, f32[16,2560]{1,0:T(8,128)S(1)}, u32[]{:S(2)}, u32[]{:S(2)}) collective-permute-start(f32[16,2560]{1,0:T(8,128)S(1)} %get-tuple-element.62), channel_id=1, source_target_pairs={{0,24},{8,16},{16,8},{24,0},{1,25},{9,17},{17,9},{25,1},{2,26},{10... | collective-permute-start | bytes 491528 | tf_op jit(solution)/shard_map/ppermute | solution.py:30
  67.5 6.5 %collective-permute-start.25 = (bf16[16,2816]{1,0:T(8,128)(2,1)S(1)}, bf16[16,2816]{1,0:T(8,128)(2,1)S(1)}, u32[]{:S(2)}, u32[]{:S(2)}) collective-permute-start(bf16[16,2816]{1,0:T(8,128)(2,1)S(1)} %get-tuple-element.63.refs_0_), channel_id=1, source_target_pairs={{0,6},{1,7},{2,4},{3,5},{4,2},{5,3},{6,0},{7,1},{8,14},{9,15},{10,... | collective-permute-start | bytes 270344 | tf_op jit(solution)/shard_map/ppermute | solution.py:30
  70.0 5.7 %collective-permute-start.24 = (bf16[16,2816]{1,0:T(8,128)(2,1)S(1)}, bf16[16,2816]{1,0:T(8,128)(2,1)S(1)}, u32[]{:S(2)}, u32[]{:S(2)}) collective-permute-start(bf16[16,2816]{1,0:T(8,128)(2,1)S(1)} %get-tuple-element.63.refs_0_), channel_id=1, source_target_pairs={{0,4},{1,5},{2,6},{3,7},{4,0},{5,1},{6,2},{7,3},{8,12},{9,13},{10,... | collective-permute-start | bytes 270344 | tf_op jit(solution)/shard_map/ppermute | solution.py:30
  70.0 5.7 %collective-permute-start.23 = (bf16[16,2816]{1,0:T(8,128)(2,1)S(1)}, bf16[16,2816]{1,0:T(8,128)(2,1)S(1)}, u32[]{:S(2)}, u32[]{:S(2)}) collective-permute-start(bf16[16,2816]{1,0:T(8,128)(2,1)S(1)} %get-tuple-element.63.refs_0_), channel_id=1, source_target_pairs={{0,2},{1,3},{2,0},{3,1},{4,6},{5,7},{6,4},{7,5},{8,10},{9,11},{10,... | collective-permute-start | bytes 270344 | tf_op jit(solution)/shard_map/ppermute | solution.py:30
  71.9 5.4 %collective-permute-start.30 = (bf16[16,2880]{1,0:T(8,128)(2,1)S(1)}, bf16[16,2880]{1,0:T(8,128)(2,1)S(1)}, u32[]{:S(2)}, u32[]{:S(2)}) collective-permute-start(bf16[16,2880]{1,0:T(8,128)(2,1)S(1)} %get-tuple-element.71), channel_id=1, source_target_pairs={{0,8},{8,0},{16,24},{24,16},{1,9},{9,1},{17,25},{25,17},{2,10},{10... | collective-permute-start | bytes 276488 | tf_op jit(solution)/shard_map/ppermute | solution.py:30
  73.0 8.3 %collective-permute-start.31 = (bf16[16,2880]{1,0:T(8,128)(2,1)S(1)}, bf16[16,2880]{1,0:T(8,128)(2,1)S(1)}, u32[]{:S(2)}, u32[]{:S(2)}) collective-permute-start(bf16[16,2880]{1,0:T(8,128)(2,1)S(1)} %get-tuple-element.72), channel_id=1, source_target_pairs={{0,16},{8,24},{16,0},{24,8},{1,17},{9,25},{17,1},{25,9},{2,18},{10... | collective-permute-start | bytes 276488 | tf_op jit(solution)/shard_map/ppermute | solution.py:30
  73.9 7.4 %collective-permute-start.32 = (bf16[16,2880]{1,0:T(8,128)(2,1)S(1)}, bf16[16,2880]{1,0:T(8,128)(2,1)S(1)}, u32[]{:S(2)}, u32[]{:S(2)}) collective-permute-start(bf16[16,2880]{1,0:T(8,128)(2,1)S(1)} %get-tuple-element.73), channel_id=1, source_target_pairs={{0,24},{8,16},{16,8},{24,0},{1,25},{9,17},{17,9},{25,1},{2,26},{10... | collective-permute-start | bytes 276488 | tf_op jit(solution)/shard_map/ppermute | solution.py:30
  75.9 2.4 %collective-permute-start.26 = (f32[64,64]{1,0:T(8,128)S(1)}, f32[64,64]{1,0:T(8,128)S(1)}, u32[]{:S(2)}, u32[]{:S(2)}) collective-permute-start(f32[64,64]{1,0:T(8,128)S(1)} %get-tuple-element.64.refs_0_), channel_id=1, source_target_pairs={{0,1},{1,0},{2,3},{3,2},{4,5},{5,4},{6,7},{7,6},{8,9},{9,8},{10,11... | collective-permute-start | bytes 49160 | tf_op jit(solution)/shard_map/ppermute | solution.py:30
  75.9 5.4 %collective-permute-start.27 = (bf16[16,2304]{1,0:T(8,128)(2,1)S(1)}, bf16[16,2304]{1,0:T(8,128)(2,1)S(1)}, u32[]{:S(2)}, u32[]{:S(2)}) collective-permute-start(bf16[16,2304]{1,0:T(8,128)(2,1)S(1)} %get-tuple-element.67), channel_id=1, source_target_pairs={{0,8},{8,0},{16,24},{24,16},{1,9},{9,1},{17,25},{25,17},{2,10},{10... | collective-permute-start | bytes 221192 | tf_op jit(solution)/shard_map/ppermute | solution.py:30
  77.3 4.4 %collective-permute-start.28 = (bf16[16,2304]{1,0:T(8,128)(2,1)S(1)}, bf16[16,2304]{1,0:T(8,128)(2,1)S(1)}, u32[]{:S(2)}, u32[]{:S(2)}) collective-permute-start(bf16[16,2304]{1,0:T(8,128)(2,1)S(1)} %get-tuple-element.68), channel_id=1, source_target_pairs={{0,16},{8,24},{16,0},{24,8},{1,17},{9,25},{17,1},{25,9},{2,18},{10... | collective-permute-start | bytes 221192 | tf_op jit(solution)/shard_map/ppermute | solution.py:30
  78.3 5.3 %collective-permute-start.29 = (bf16[16,2304]{1,0:T(8,128)(2,1)S(1)}, bf16[16,2304]{1,0:T(8,128)(2,1)S(1)}, u32[]{:S(2)}, u32[]{:S(2)}) collective-permute-start(bf16[16,2304]{1,0:T(8,128)(2,1)S(1)} %get-tuple-element.69), channel_id=1, source_target_pairs={{0,24},{8,16},{16,8},{24,0},{1,25},{9,17},{17,9},{25,1},{2,26},{10... | collective-permute-start | bytes 221192 | tf_op jit(solution)/shard_map/ppermute | solution.py:30
  83.8 9.2 %collective-permute-start.34 = (bf16[64,2304]{1,0:T(8,128)(2,1)S(1)}, bf16[64,2304]{1,0:T(8,128)(2,1)S(1)}, u32[]{:S(2)}, u32[]{:S(2)}) collective-permute-start(bf16[64,2304]{1,0:T(8,128)(2,1)S(1)} %get-tuple-element.75.refs_0_), channel_id=1, source_target_pairs={{0,1},{1,0},{2,3},{3,2},{4,5},{5,4},{6,7},{7,6},{8,9},{9,8},{10,11... | collective-permute-start | bytes 884744 | tf_op jit(solution)/shard_map/ppermute | solution.py:30
  83.8 9.1 %collective-permute-start.33 = (f32[1,576]{1,0:T(1,128)S(1)}, f32[1,576]{1,0:T(1,128)S(1)}, u32[]{:S(2)}, u32[]{:S(2)}) collective-permute-start(f32[1,576]{1,0:T(1,128)S(1)} %get-tuple-element.74), channel_id=1, source_target_pairs={{0,0},{1,4},{2,8},{3,12},{4,16},{5,20},{6,24},{7,28},{8,1},{9,5},{... | collective-permute-start | bytes 6920 | tf_op jit(solution)/shard_map/ppermute | solution.py:642
